TPU v7x, 32 devices: a whole 2x2x4 slice. The times are simulated.
32 devices in a mesh: dev: 32 (over z, y, x, core).
Axes of the slice: x: 2, y: 2, z: 4, core: 2. Of those that a mesh axis runs over, the one named last changes fastest.
Arguments:
- displacement: float32 [3, 131072], P(None, 'dev'), may hold values from -2 to 2
- send_node: int32 [262144], P('dev'), may hold values from -1 to 4095, as said below
- member_slot: int32 [128, 1024], P('dev'), may hold values from 0 to 8191, as said below
- inverse_part: bfloat16 [128, 1024, 1024], P('dev'), may hold values from -0.09375 to 0.09375
- source_coord: float32 [128, 3, 1024], P('dev'), may hold values from 0 to 1
- target_coord: float32 [128, 3, 1024], P('dev'), may hold values from 0 to 1
- unity_weight: float32 [128, 1024], P('dev'), may hold values from 0.1 to 1
- result_pick: int32 [262144], P('dev'), may hold values from -1 to 4095, as said below
- receive_vertex: int32 [262144], P('dev'), may hold values from 0 to 8191
- mesh_before: float32 [3, 512, 96, 512], P(None, 'dev'), may hold values from -6 to 6
Outputs:
- mesh_motion: float32 [3, 512, 96, 512], P(None, 'dev')
Inputs may be any that keep to these rules, and one draw needn't show every extreme that they name: `send_node`: each device's entries form 32 blocks of 256, block e for cluster owner e; in each block the live entries (0 or more) come first and -1 fills the rest; each block has at least one live entry and each device has one block with all 256 live. `member_slot`: every entry names a live slot of send_node sent to the cluster's owner. `result_pick`: each device's entries form 32 blocks of 256, block e for fluid owner e; in each block the live entries (0 or more) come first and -1 fills the rest; each block has at least one live entry and each device has one block with all 256 live.
All inputs are finite; a program needn't handle non-finite values.
Results may differ from a plain program's by a relative error of at most 0.00043.
Values sent between devices are 32-bit elements; how exact they have to be, the bound alone decides.
No kernel may reach another device: no remote copies, remote signals or barrier semaphores. Data moves between devices by JAX's collectives and lax.ppermute only.
A program may use at most 128 MiB of HBM per device.

v0:
```python
import jax
import jax.numpy as jnp
from jax import lax
from jax.sharding import PartitionSpec as P

relax_rate = 0.8
kernel_sharpness = 8.0


def extended_2(cells, sides, width):
    for axis, dim in sides:
        count = lax.axis_size(axis)
        ends = count - 1
        head = lax.slice_in_dim(cells, 0, width, axis=dim)
        tail = lax.slice_in_dim(cells, cells.shape[dim] - width, cells.shape[dim], axis=dim)
        cells = jnp.concatenate(
            [
                lax.ppermute(tail, axis, [(i, (i + 1) % count) for i in range(ends)]),
                cells,
                lax.ppermute(head, axis, [((i + 1) % count, i) for i in range(ends)]),
            ],
            axis=dim,
        )
    return cells


def relax(extended):
    center = extended[:, 1:-1]
    padded = jnp.pad(center, ((0, 0), (0, 0), (1, 1), (1, 1)))
    beside = extended[:, 2:] + extended[:, :-2]
    beside = beside + padded[:, :, 2:, 1:-1] + padded[:, :, :-2, 1:-1]
    beside = beside + padded[:, :, 1:-1, 2:] + padded[:, :, 1:-1, :-2]
    moved = center + relax_rate * (beside * (1.0 / 6.0) - center)
    yrows = lax.broadcasted_iota(jnp.int32, center.shape, 2)
    return jnp.where(yrows == 0, center, moved)


def sweep(field):
    extended = extended_2(field, (("dev", 1),), 1)
    return relax(extended)


def local(
    displacement,
    send_node,
    member_slot,
    inverse_part,
    source_coord,
    target_coord,
    unity_weight,
    result_pick,
    receive_vertex,
    mesh_before,
):
    device_count = lax.axis_size("dev")
    slot_cap = send_node.shape[0] // device_count
    picked = jnp.take(displacement, jnp.maximum(send_node, 0), axis=1)
    outgoing = jnp.where(send_node[None, :] >= 0, picked, 0.0).reshape(3, device_count, slot_cap)
    arrived = lax.all_to_all(outgoing, "dev", split_axis=1, concat_axis=1, tiled=True).reshape(
        3, device_count * slot_cap
    )
    members = jnp.take(arrived, member_slot, axis=1)
    coupling = jnp.einsum(
        "kcp,cqp->kcq",
        members.astype(jnp.bfloat16),
        inverse_part,
        preferred_element_type=jnp.float32,
    )
    coefficient = members + coupling
    gap = target_coord[:, 0, :, None] - source_coord[:, 0, None, :]
    spread = gap * gap
    gap = target_coord[:, 1, :, None] - source_coord[:, 1, None, :]
    spread = spread + gap * gap
    gap = target_coord[:, 2, :, None] - source_coord[:, 2, None, :]
    spread = spread + gap * gap
    kernel = jnp.exp(-kernel_sharpness * spread)
    contrib = jnp.einsum(
        "kcp,ctp->kct",
        coefficient,
        kernel,
        precision=lax.Precision.HIGHEST,
        preferred_element_type=jnp.float32,
    )
    contrib = contrib * unity_weight[None]
    flat_results = contrib.reshape(3, -1)
    result_cap = result_pick.shape[0] // device_count
    taken = jnp.take(flat_results, jnp.maximum(result_pick, 0), axis=1)
    outgoing_results = jnp.where(result_pick[None, :] >= 0, taken, 0.0).reshape(
        3, device_count, result_cap
    )
    returned = lax.all_to_all(
        outgoing_results, "dev", split_axis=1, concat_axis=1, tiled=True
    ).reshape(3, device_count * result_cap)
    width_x = mesh_before.shape[1]
    depth_z = mesh_before.shape[3]
    interface = jnp.zeros((3, width_x * depth_z), jnp.float32).at[:, receive_vertex].add(returned)
    yrows = lax.broadcasted_iota(jnp.int32, mesh_before.shape, 2)
    start_field = jnp.where(yrows == 0, interface.reshape(3, width_x, 1, depth_z), mesh_before)
    return sweep(sweep(start_field))


def solution(mesh):
    in_specs = (
        P(None, "dev"),
        P("dev"),
        P("dev", None),
        P("dev", None, None),
        P("dev", None, None),
        P("dev", None, None),
        P("dev", None),
        P("dev"),
        P("dev"),
        P(None, "dev", None, None),
    )
    out_specs = P(None, "dev", None, None)
    return jax.shard_map(local, mesh=mesh, in_specs=in_specs, out_specs=out_specs, check_vma=False)
```

profile of v0, /device:TPU:4, one launch (start us, length us, event | category | flops | bytes accessed | tf_op | source)
XLA Modules:
  0.0 305.5 jit_solution(1124295872801492278)
XLA Ops:
  3.1 28.0 %gather_fusion.1 = f32[8192,3]{1,0:T(8,128)} fusion(f32[3,4096]{0,1:T(8,128)S(1)} %copy.24, s32[8192]{0:T(1024)S(1)} %maximum_clamp_fusion.1), kind=kCustom, calls=%fused_computation.clone | custom fusion | bytes 229376 | tf_op jit(solution)/shard_map/jit(_take)/gather | solution.py:57
  31.0 7.6 %bitcast_select_fusion.1 = f32[3,8192]{0,1:T(8,128)} fusion(f32[8192,3]{1,0:T(8,128)} %gather_fusion.1, pred[8192]{0:T(1024)(128)(4,1)S(1)} %get-tuple-element.19, pred[8192]{0:T(1024)(128)(4,1)S(1)} %get-tuple-element.18), kind=kLoop, calls=%fused_computation.54 | loop fusion | flops 49152 | bytes 212992 | tf_op jit(solution)/shard_map/jit(_where)/select_n | solution.py:58
  38.7 3.5 %copy.25 = f32[3,32,256]{2,0,1:T(4,128)} copy(f32[3,32,256]{0,2,1:T(8,128)} %bitcast.41) | data formatting | bytes 196608 | tf_op jit(solution)/shard_map/reshape | solution.py:58
  42.1 6.1 %all-to-all-start = ((f32[3,32,256]{2,0,1:T(4,128)}), f32[3,32,256]{2,0,1:T(4,128)S(1)}, u32[]{:S(2)}, u32[]{:S(2)}) async-start(f32[3,32,256]{2,0,1:T(4,128)} %copy.25), calls=%async_computation | async-start | bytes 262144 | tf_op jit(solution)/shard_map/all_to_all | solution.py:59
  48.4 6.9 %all-to-all-done = f32[3,32,256]{2,0,1:T(4,128)S(1)} async-done(((f32[3,32,256]{2,0,1:T(4,128)}), f32[3,32,256]{2,0,1:T(4,128)S(1)}, u32[]{:S(2)}, u32[]{:S(2)}) %all-to-all-start) | async-done | bytes 98336 | tf_op jit(solution)/shard_map/all_to_all | solution.py:59
  58.0 13.0 %gather_fusion = f32[4096,3]{1,0:T(8,128)S(1)} fusion(f32[3,8192]{0,1:T(8,128)} %bitcast.44, s32[4096]{0:T(1024)S(1)} %bitcast_clamp_fusion), kind=kCustom, calls=%fused_computation.2 | custom fusion | bytes 114688 | tf_op jit(solution)/shard_map/jit(_take)/gather | solution.py:62
  71.6 5.7 %fusion.36 = f32[3,4,1024]{2,0,1:T(4,128)S(1)} fusion(bf16[4,1024,1024]{2,1,0:T(8,128)(2,1)} %param.15, f32[4,1024,3]{1,2,0:T(4,128)S(1)} %copy.28, pred[4,1024]{1,0:T(4,128)(4,1)S(1)} %compare_and_fusion), kind=kOutput, calls=%fused_computation.58 | convolution fusion | flops 25214976 | bytes 8491008 | tf_op jit(solution)/shard_map/kcp,cqp->kcq/dot_general | solution.py:63
  77.2 20.8 %fusion.37 = f32[4,1024,3]{1,2,0:T(4,128)S(1)} fusion(f32[3,4,1024]{2,0,1:T(4,128)S(1)} %fusion.36, f32[4,1024]{1,0:T(4,128)S(1)} %get-tuple-element.14, f32[4,1024]{1,0:T(4,128)S(1)} %get-tuple-element.21, f32[4,1024]{1,0:T(4,128)S(1)} %get-tuple-element.15, f32[4,1024]{1,0:T(4,128)S(1)} %get-tuple-element.20, f32[4,1024]{1,0:T(4,128)S(1)} %get-tuple-element.13, ...), kind=kOutput, calls=%fused_computation.59 | convolution fusion | flops 188755968 | bytes 212992 | tf_op jit(solution)/shard_map/kcp,ctp->kct/dot_general | solution.py:77
  98.7 28.0 %gather_fusion.2 = f32[8192,3]{1,0:T(8,128)} fusion(f32[3,4096]{0,1:T(8,128)S(1)} %copy.29, s32[8192]{0:T(1024)S(1)} %maximum_clamp_fusion), kind=kCustom, calls=%fused_computation.1.clone | custom fusion | bytes 229376 | tf_op jit(solution)/shard_map/jit(_take)/gather | solution.py:87
  126.7 7.6 %bitcast_select_fusion = f32[3,8192]{0,1:T(8,128)} fusion(f32[8192,3]{1,0:T(8,128)} %gather_fusion.2, pred[8192]{0:T(1024)(128)(4,1)S(1)} %get-tuple-element.17, pred[8192]{0:T(1024)(128)(4,1)S(1)} %get-tuple-element.16), kind=kLoop, calls=%fused_computation.53 | loop fusion | flops 49152 | bytes 212992 | tf_op jit(solution)/shard_map/jit(_where)/select_n | solution.py:88
  134.3 3.5 %copy.30 = f32[3,32,256]{2,0,1:T(4,128)} copy(f32[3,32,256]{0,2,1:T(8,128)} %bitcast.42) | data formatting | bytes 196608 | tf_op jit(solution)/shard_map/reshape | solution.py:88
  137.8 3.6 %all-to-all-start.1 = ((f32[3,32,256]{2,0,1:T(4,128)}), f32[3,32,256]{2,0,1:T(4,128)S(1)}, u32[]{:S(2)}, u32[]{:S(2)}) async-start(f32[3,32,256]{2,0,1:T(4,128)} %copy.30), calls=%async_computation.1 | async-start | bytes 262144 | tf_op jit(solution)/shard_map/all_to_all | solution.py:91
  141.4 7.2 %all-to-all-done.1 = f32[3,32,256]{2,0,1:T(4,128)S(1)} async-done(((f32[3,32,256]{2,0,1:T(4,128)}), f32[3,32,256]{2,0,1:T(4,128)S(1)}, u32[]{:S(2)}, u32[]{:S(2)}) %all-to-all-start.1) | async-done | bytes 98336 | tf_op jit(solution)/shard_map/all_to_all | solution.py:91
  151.2 46.5 %scatter_custom_fusion = f32[3,8192]{0,1:T(8,128)} fusion(s32[8192]{0:T(1024)S(1)} %compare_select_fusion, f32[8192,3]{1,0:T(8,128)} %copy.31, f32[]{:T(128)} %constant.8.clone.1), kind=kCustom, calls=%fused_computation.55 | custom fusion | flops 24576 | bytes 98816 | tf_op jit(solution)/shard_map/scatter-add | solution.py:96
  197.7 2.8 copy.32
  200.6 5.2 %broadcast_select_fusion = f32[3,16,96,512]{3,2,1,0:T(8,128)S(1)} fusion(f32[3,16,96,512]{3,2,1,0:T(8,128)} %param.21, f32[3,16,512]{2,1,0:T(8,128)S(1)} %copy.32, pred[96]{0:T(512)(128)(4,1)S(1)} %iota_compare_fusion), kind=kLoop, calls=%fused_computation.52 | loop fusion | flops 2359296 | bytes 18972768 | tf_op jit(solution)/shard_map/jit(_where)/select_n | solution.py:98
  205.8 3.7 %copy-done = f32[3,16,96,512]{3,2,1,0:T(8,128)} copy-done((f32[3,16,96,512]{3,2,1,0:T(8,128)}, f32[3,16,96,512]{3,2,1,0:T(8,128)S(1)}, u32[]{:S(2)}) %copy-start) | copy-done | bytes 9437208
  209.6 2.9 collective-permute-start
  214.5 9.8 %collective-permute-done = f32[3,1,96,512]{3,2,1,0:T(8,128)S(1)} collective-permute-done((f32[3,1,96,512]{3,2,1,0:T(8,128)S(1)}, f32[3,1,96,512]{3,2,1,0:T(8,128)S(1)}, u32[]{:S(2)}, u32[]{:S(2)}) %collective-permute-start) | collective-permute-done | bytes 589856 | tf_op jit(solution)/shard_map/ppermute | solution.py:20
  224.3 4.1 %collective-permute-done.1 = f32[3,1,96,512]{3,2,1,0:T(8,128)S(1)} collective-permute-done((f32[3,1,96,512]{3,2,1,0:T(8,128)S(1)}, f32[3,1,96,512]{3,2,1,0:T(8,128)S(1)}, u32[]{:S(2)}, u32[]{:S(2)}) %collective-permute-start.1) | collective-permute-done | bytes 589856 | tf_op jit(solution)/shard_map/ppermute | solution.py:18
  228.4 29.3 %add_select_fusion.1 = f32[3,16,96,512]{3,2,1,0:T(8,128)} fusion(f32[3,16,96,512]{3,2,1,0:T(8,128)} %copy-done, f32[3,1,96,512]{3,2,1,0:T(8,128)S(1)} %collective-permute-done.1, f32[3,1,96,512]{3,2,1,0:T(8,128)S(1)} %collective-permute-done, pred[96]{0:T(512)(128)(4,1)S(1)} %iota_compare_fusion), kind=kLoop, calls=%fused_computation.24 | loop fusion | flops 28311552 | bytes 20054112 | tf_op jit(solution)/shard_map/jit(_where)/select_n | solution.py:35
  263.3 9.5 %collective-permute-done.2 = f32[3,1,96,512]{3,2,1,0:T(8,128)S(1)} collective-permute-done((f32[3,1,96,512]{3,2,1,0:T(8,128)S(1)}, f32[3,1,96,512]{3,2,1,0:T(8,128)S(1)}, u32[]{:S(2)}, u32[]{:S(2)}) %collective-permute-start.2) | collective-permute-done | bytes 589856 | tf_op jit(solution)/shard_map/ppermute | solution.py:20
  272.9 3.6 %collective-permute-done.3 = f32[3,1,96,512]{3,2,1,0:T(8,128)S(1)} collective-permute-done((f32[3,1,96,512]{3,2,1,0:T(8,128)S(1)}, f32[3,1,96,512]{3,2,1,0:T(8,128)S(1)}, u32[]{:S(2)}, u32[]{:S(2)}) %collective-permute-start.3) | collective-permute-done | bytes 589856 | tf_op jit(solution)/shard_map/ppermute | solution.py:18
  276.5 29.0 %add_select_fusion = f32[3,16,96,512]{3,2,1,0:T(8,128)} fusion(f32[3,16,96,512]{3,2,1,0:T(8,128)} %add_select_fusion.1, f32[3,1,96,512]{3,2,1,0:T(8,128)S(1)} %collective-permute-done.3, f32[3,1,96,512]{3,2,1,0:T(8,128)S(1)} %collective-permute-done.2, pred[96]{0:T(512)(128)(4,1)S(1)} %iota_compare_fusion), kind=kLoop, calls=%fused_computation.23 | loop fusion | flops 28311552 | bytes 20054112 | tf_op jit(solution)/shard_map/jit(_where)/select_n | solution.py:35
  (33 shorter events, 17.5 us)
Async XLA Ops:
  0.0 48.3 %copy-start.1 = (s32[8192]{0:T(1024)S(1)}, s32[8192]{0:T(1024)}, u32[]{:S(2)}) copy-start(s32[8192]{0:T(1024)} %param.19) | copy-start | bytes 98308
  0.0 48.3 %copy-start.2 = (s32[4,1024]{1,0:T(4,128)S(1)}, s32[4,1024]{1,0:T(4,128)}, u32[]{:S(2)}) copy-start(s32[4,1024]{1,0:T(4,128)} %param.14) | copy-start | bytes 49156
  0.0 48.3 %copy-start.4 = (f32[4,3,1024]{2,0,1:T(4,128)S(1)}, f32[4,3,1024]{2,0,1:T(4,128)}, u32[]{:S(2)}) copy-start(f32[4,3,1024]{2,0,1:T(4,128)} %param.17) | copy-start | bytes 147460
  0.0 48.4 %copy-start.3 = (f32[4,3,1024]{2,0,1:T(4,128)S(1)}, f32[4,3,1024]{2,0,1:T(4,128)}, u32[]{:S(2)}) copy-start(f32[4,3,1024]{2,0,1:T(4,128)} %param.16) | copy-start | bytes 147460
  38.7 38.6 %copy-start.6 = (f32[4,1024]{1,0:T(4,128)S(1)}, f32[4,1024]{1,0:T(4,128)}, u32[]{:S(2)}) copy-start(f32[4,1024]{1,0:T(4,128)} %param.18) | copy-start | bytes 49156
  42.1 13.2 %all-to-all-start = ((f32[3,32,256]{2,0,1:T(4,128)}), f32[3,32,256]{2,0,1:T(4,128)S(1)}, u32[]{:S(2)}, u32[]{:S(2)}) async-start(f32[3,32,256]{2,0,1:T(4,128)} %copy.25), calls=%async_computation | async-start | bytes 262144 | tf_op jit(solution)/shard_map/all_to_all | solution.py:59
  98.1 43.3 %copy-start.5 = (s32[8192]{0:T(1024)S(1)}, s32[8192]{0:T(1024)}, u32[]{:S(2)}) copy-start(s32[8192]{0:T(1024)} %param.20) | copy-start | bytes 98308
  137.8 10.8 %all-to-all-start.1 = ((f32[3,32,256]{2,0,1:T(4,128)}), f32[3,32,256]{2,0,1:T(4,128)S(1)}, u32[]{:S(2)}, u32[]{:S(2)}) async-start(f32[3,32,256]{2,0,1:T(4,128)} %copy.30), calls=%async_computation.1 | async-start | bytes 262144 | tf_op jit(solution)/shard_map/all_to_all | solution.py:91
  205.8 3.7 %copy-start = (f32[3,16,96,512]{3,2,1,0:T(8,128)}, f32[3,16,96,512]{3,2,1,0:T(8,128)S(1)}, u32[]{:S(2)}) copy-start(f32[3,16,96,512]{3,2,1,0:T(8,128)S(1)} %broadcast_select_fusion) | copy-start | bytes 28311556
  209.6 14.6 %collective-permute-start = (f32[3,1,96,512]{3,2,1,0:T(8,128)S(1)}, f32[3,1,96,512]{3,2,1,0:T(8,128)S(1)}, u32[]{:S(2)}, u32[]{:S(2)}) collective-permute-start(f32[3,1,96,512]{3,2,1,0:T(8,128)S(1)} %get-tuple-element.8), channel_id=1, source_target_pairs={{1,0},{2,1},{3,2},{4,3},{5,4},{6,5},{7,6},{8,7},{9,8},{10,9},{11,1... | collective-permute-start | bytes 1769480 | tf_op jit(solution)/shard_map/ppermute | solution.py:20
  212.5 15.8 %collective-permute-start.1 = (f32[3,1,96,512]{3,2,1,0:T(8,128)S(1)}, f32[3,1,96,512]{3,2,1,0:T(8,128)S(1)}, u32[]{:S(2)}, u32[]{:S(2)}) collective-permute-start(f32[3,1,96,512]{3,2,1,0:T(8,128)S(1)} %get-tuple-element.9), channel_id=1, source_target_pairs={{0,1},{1,2},{2,3},{3,4},{4,5},{5,6},{6,7},{7,8},{8,9},{9,10},{10,1... | collective-permute-start | bytes 1769480 | tf_op jit(solution)/shard_map/ppermute | solution.py:18
  259.0 13.9 %collective-permute-start.2 = (f32[3,1,96,512]{3,2,1,0:T(8,128)S(1)}, f32[3,1,96,512]{3,2,1,0:T(8,128)S(1)}, u32[]{:S(2)}, u32[]{:S(2)}) collective-permute-start(f32[3,1,96,512]{3,2,1,0:T(8,128)S(1)} %get-tuple-element.6), channel_id=1, source_target_pairs={{1,0},{2,1},{3,2},{4,3},{5,4},{6,5},{7,6},{8,7},{9,8},{10,9},{11,1... | collective-permute-start | bytes 1769480 | tf_op jit(solution)/shard_map/ppermute | solution.py:20
  260.9 15.6 %collective-permute-start.3 = (f32[3,1,96,512]{3,2,1,0:T(8,128)S(1)}, f32[3,1,96,512]{3,2,1,0:T(8,128)S(1)}, u32[]{:S(2)}, u32[]{:S(2)}) collective-permute-start(f32[3,1,96,512]{3,2,1,0:T(8,128)S(1)} %get-tuple-element.7), channel_id=1, source_target_pairs={{0,1},{1,2},{2,3},{3,4},{4,5},{5,6},{6,7},{7,8},{8,9},{9,10},{10,1... | collective-permute-start | bytes 1769480 | tf_op jit(solution)/shard_map/ppermute | solution.py:18
where the time goes:
time: 306 us; the launch traced here: 305 us
  other arithmetic  127 us (42%)
  local copies, waits for them, and re-layouts  92 us (30%)
  waiting for transfers between devices  41.2 us (13%)
  matrix products  26.5 us (9%)
  starting transfers between devices  18.8 us (6%)
    select_n x2, other arithmetic, relax(): return jnp.where(yrows == 0, center, moved)  58.2 us
    scatter-add x1, other arithmetic, local(): jnp.zeros((3, width_x * depth_z), jnp.float32).at[:, receive_vertex]  46.5 us
    gather x1, local copies, waits for them, and re-layouts, local(): picked = jnp.take(displacement, jnp.maximum(send_node, 0), axis=1)  28 us
    gather x1, local copies, waits for them, and re-layouts, local(): taken = jnp.take(flat_results, jnp.maximum(result_pick, 0), axis=1)  28 us
    dot_general x1, matrix products, local(): jnp.einsum('kcp,ctp->kct', coefficient, kernel, precision=lax.Precision.H...  20.8 us
    ppermute x2, waiting for transfers between devices, extended_2(): lax.ppermute(head, axis, [((i + 1) % count, i) for i in range(ends)])  19.4 us
    gather x2, local copies, waits for them, and re-layouts, local(): members = jnp.take(arrived, member_slot, axis=1)  13.6 us
    ppermute x2, waiting for transfers between devices, extended_2(): lax.ppermute(tail, axis, [(i, (i + 1) % count) for i in range(ends)])  7.7 us
  transfers between devices with their start and end apart: 6, of which 6 were waited for; matrix products, arithmetic and copies ran while one was open for 0% of the time, Pallas kernels for 0%

commit v1 on v0

v1 whole, which is shorter than its diff:
```python
import math

import jax
import jax.numpy as jnp
from jax import lax
from jax.experimental import pallas as pl
from jax.experimental.pallas import tpu as pltpu
from jax.sharding import PartitionSpec as P

LANES = 128
SUB = 8
share = 0.8 / 6.0
keep = 0.2 / share
sharpness = 8.0
VMEM = pl.BlockSpec(memory_space=pltpu.VMEM)
ANY = pl.BlockSpec(memory_space=pl.ANY)
SMEM = pl.BlockSpec(memory_space=pltpu.SMEM)
f32 = jnp.float32
bf16 = jnp.bfloat16


def params(limit, **more):
    return pltpu.CompilerParams(vmem_limit_bytes=limit << 20, **more)


def lane_gather(row, lane):
    return jnp.take_along_axis(row, lane, axis=1, mode="promise_in_bounds")


def gather_rows(row_of, blocks, index_of, groups):
    index = [index_of(g) for g in range(groups)]
    high = [lax.shift_right_arithmetic(i, 7) for i in index]
    low = [jnp.bitwise_and(i, LANES - 1) for i in index]
    out = [[jnp.zeros((SUB, LANES), f32) for _ in range(3)] for _ in range(groups)]
    for block in range(blocks):
        rows = [jnp.broadcast_to(row_of(k, block), (SUB, LANES)) for k in range(3)]
        for g in range(groups):
            here = high[g] == block
            for k in range(3):
                out[g][k] = jnp.where(here, lane_gather(rows[k], low[g]), out[g][k])
    return out


def packed_place(k, row, per):
    return row // per, k * per + row % per


def store_rows(out_ref, g, values, per):
    for k in range(3):
        for s in range(SUB):
            row = g * SUB + s
            if per:
                d, r = packed_place(k, row, per)
                out_ref[d, r : r + 1, :] = values[k][s : s + 1, :]
            else:
                out_ref[k, row : row + 1, :] = values[k][s : s + 1, :]


def packed_row(ref, k, row, per):
    if per:
        d, r = packed_place(k, row, per)
        return ref[d, r : r + 1, :]
    return ref[k, row : row + 1, :]


def pick_body(table_ref, index_ref, out_ref, *, per):
    groups = index_ref.shape[0] // SUB
    blocks = table_ref.shape[1] // LANES
    half = max(1, groups // 2)
    for first in range(0, groups, half):
        got = gather_rows(
            lambda k, b: table_ref[k : k + 1, b * LANES : (b + 1) * LANES],
            blocks,
            lambda g: index_ref[(first + g) * SUB : (first + g + 1) * SUB, :],
            half,
        )
        for g in range(half):
            store_rows(out_ref, first + g, got[g], per)


def kernel_body(source_ref, target_ref, high_ref, low_ref, turned):
    clusters, _, points = source_ref.shape
    scale = math.sqrt(sharpness * math.log2(math.e))
    step = 16
    for c in range(clusters):
        rows = jnp.concatenate([source_ref[c] * scale, jnp.zeros((SUB - 3, points), f32)], axis=0)
        turned[...] = jnp.transpose(rows)
        goal = [target_ref[c, k : k + 1, :] * scale for k in range(3)]

        def body(i, _, c=c, goal=goal):
            at = pl.multiple_of(i * step, step)
            part = turned[pl.ds(at, step), :]
            gap = goal[0] - part[:, 0:1]
            spread = gap * gap
            gap = goal[1] - part[:, 1:2]
            spread = spread + gap * gap
            gap = goal[2] - part[:, 2:3]
            spread = spread + gap * gap
            value = jnp.exp2(-spread)
            high = value.astype(bf16)
            high_ref[c, pl.ds(at, step), :] = high
            low_ref[c, pl.ds(at, step), :] = (value - high.astype(f32)).astype(bf16)
            return 0

        lax.fori_loop(0, points // step, body, 0)


def result_body(
    arrived_ref, slot_ref, inverse_ref, high_ref, low_ref, weight_ref, pick_ref, out_ref, inverse, members, results, sems, *, per_in, per_out
):
    clusters, points = slot_ref.shape
    verts = weight_ref.shape[1]
    copies = [pltpu.make_async_copy(inverse_ref.at[c], inverse.at[c], sems.at[c]) for c in range(clusters)]
    for copy in copies:
        copy.start()
    fold = SUB // clusters
    groups = points // LANES // fold
    blocks = (arrived_ref.shape[0] * per_in) if per_in else arrived_ref.shape[1]
    got = gather_rows(
        lambda k, b: packed_row(arrived_ref, k, b, per_in),
        blocks,
        lambda g: jnp.concatenate(
            [slot_ref[:, (g * fold + j) * LANES : (g * fold + j + 1) * LANES] for j in range(fold)], axis=0
        ),
        groups,
    )
    members[...] = jnp.zeros(members.shape, f32)
    for g in range(groups):
        for j in range(fold):
            at = (g * fold + j) * LANES
            for c in range(clusters):
                for k in range(3):
                    s = j * clusters + c
                    members[c, k : k + 1, at : at + LANES] = got[g][k][s : s + 1, :]
    for c in range(clusters):
        copies[c].wait()
        mine = members[c]
        coupling = lax.dot_general(
            mine.astype(bf16), inverse[c], (((1,), (1,)), ((), ())), preferred_element_type=f32
        )
        coefficient = mine + coupling
        c_high = coefficient.astype(bf16)
        c_low = (coefficient - c_high.astype(f32)).astype(bf16)
        both = jnp.concatenate([c_high, c_low], axis=0)
        first = jnp.dot(both, high_ref[c], preferred_element_type=f32)
        second = jnp.dot(c_high, low_ref[c], preferred_element_type=f32)
        total = first[:SUB] + (first[SUB:] + second)
        results[c] = total * weight_ref[c : c + 1, :]
    per_cluster = verts // LANES
    groups = pick_ref.shape[0] // SUB
    half = max(1, groups // 2)
    for start in range(0, groups, half):
        got = gather_rows(
            lambda k, b: results[
                b // per_cluster, k : k + 1, (b % per_cluster) * LANES : (b % per_cluster + 1) * LANES
            ],
            clusters * per_cluster,
            lambda g: pick_ref[(start + g) * SUB : (start + g + 1) * SUB, :],
            half,
        )
        for g in range(half):
            store_rows(out_ref, start + g, got[g], per_out)


def mesh_body(edge_ref, mesh_ref, left_ref, right_ref, out_ref, field, swept, stage, in_sems, side_sems, out_sems, *, batch):
    comps, width, height, depth = mesh_ref.shape
    tiles = depth // LANES
    strips = height // SUB
    slots = stage.shape[0]

    def columns(j):
        return pl.ds(j * LANES, LANES)

    def load(k, b):
        found = []
        for j in range(tiles):
            found.append(
                pltpu.make_async_copy(
                    mesh_ref.at[k, pl.ds(b * batch, batch), :, columns(j)],
                    field.at[k, pl.ds(2 + b * batch, batch), j, pl.ds(SUB, height), :],
                    in_sems.at[k, b, j],
                )
            )
        return found

    def sides(k):
        found = []
        for j in range(tiles):
            for side, (ref, at) in enumerate(((left_ref, 0), (right_ref, 2 + width))):
                found.append(
                    pltpu.make_async_copy(
                        ref.at[k, :, :, columns(j)],
                        field.at[k, pl.ds(at, 2), j, pl.ds(SUB, height), :],
                        side_sems.at[k, j, side],
                    )
                )
        return found

    for k in range(comps):
        for copy in sides(k):
            copy.start()
        for b in range(width // batch):
            for copy in load(k, b):
                copy.start()

    blank = jnp.zeros((SUB, LANES), f32)
    for j in range(tiles):
        for x in range(width + 2):
            swept[x, j, SUB + height : 2 * SUB + height, :] = blank
        for x in range(width + 4):
            for k in range(comps):
                field[k, x, j, SUB + height : 2 * SUB + height, :] = blank

    lane = lax.broadcasted_iota(jnp.int32, (SUB, LANES), 1)
    row = lax.broadcasted_iota(jnp.int32, (SUB, LANES), 0)
    is_first = lane == 0
    is_last = lane == LANES - 1
    wall = row == 0
    above_wall = row == 1

    def sweep(center, before, after, put):
        for y in range(strips):
            at = SUB + y * SUB
            mid = [center[j, pl.ds(at, SUB), :] for j in range(tiles)]
            down = [pltpu.roll(m, 1, 1) for m in mid]
            up = [pltpu.roll(m, LANES - 1, 1) for m in mid]
            for j in range(tiles):
                lower = center[j, pl.ds(at - 1, SUB), :]
                if y == 0:
                    lower = jnp.where(row < 2, 0.0, lower)
                near = (before[j, pl.ds(at, SUB), :] + after[j, pl.ds(at, SUB), :]) + (
                    center[j, pl.ds(at + 1, SUB), :] + lower
                )
                back = jnp.where(is_first, down[j - 1] if j else 0.0, down[j])
                fore = jnp.where(is_last, up[j + 1] if j + 1 < tiles else 0.0, up[j])
                value = (near + (back + fore)) + keep * mid[j]
                if y == 0:
                    value = jnp.where(wall, 0.0, value)
                put(j, y, value)

    def first_sweep(k, x):
        def put(j, y, value):
            swept[x, j, pl.ds(SUB + y * SUB, SUB), :] = value

        sweep(field.at[k, x + 1], field.at[k, x], field.at[k, x + 2], put)

    def flush(k, x, slot):
        return pltpu.make_async_copy(stage.at[slot], out_ref.at[k, x], out_sems.at[slot])

    def component(k, _):
        for copy in sides(k):
            copy.wait()
        for copy in load(k, 0):
            copy.wait()
        first_sweep(k, 0)

        @pl.when(edge_ref[0] == 0)
        def _():
            swept[0] = jnp.zeros(swept.shape[1:], f32)

        first_sweep(k, 1)

        def step(x, _):
            @pl.when(jnp.logical_and((x + 1) % batch == 0, x + 1 < width))
            def _():
                for copy in load(k, (x + 1) // batch):
                    copy.wait()

            first_sweep(k, x + 2)

            @pl.when(jnp.logical_and(x + 2 == width + 1, edge_ref[1] == 0))
            def _():
                swept[width + 1] = jnp.zeros(swept.shape[1:], f32)

            turn = k * width + x
            slot = turn % slots

            @pl.when(turn >= slots)
            def _():
                flush(k, x, slot).wait()

            def put(j, y, value):
                stage[slot, y * SUB : (y + 1) * SUB, j * LANES : (j + 1) * LANES] = value * (share * share)

            sweep(swept.at[x + 1], swept.at[x], swept.at[x + 2], put)
            flush(k, x, slot).start()
            return 0

        lax.fori_loop(0, width, step, 0)
        return 0

    lax.fori_loop(0, comps, component, 0)
    for slot in range(slots):
        flush(0, 0, slot).wait()


def scatter_body(returned_ref, vertex_ref, inter_ref, left_ref, right_ref, rows_sc, ones_sc, *, per, width):
    rows, _ = vertex_ref.shape
    blocks = inter_ref.shape[1]
    tiles = blocks // width
    line = lax.broadcasted_iota(jnp.int32, (blocks, LANES), 0)
    home = (line % width) * tiles + line // width
    lane = lax.broadcasted_iota(jnp.int32, (LANES, LANES), 0)
    for row in range(rows):
        vertex = vertex_ref[row : row + 1, :]
        high = lax.shift_right_arithmetic(vertex, 7)
        low = jnp.bitwise_and(vertex, LANES - 1)
        span = slice(row * LANES, (row + 1) * LANES)
        ones_sc[:, span] = jnp.where(lane == low, 1.0, 0.0).astype(bf16)
        here = home == high
        for k in range(3):
            value = packed_row(returned_ref, k, row, per)
            part = value
            for piece in range(3):
                top = part.astype(bf16).astype(f32)
                at = (piece * 3 + k) * blocks
                rows_sc[at : at + blocks, span] = jnp.where(here, top, 0.0).astype(bf16)
                part = part - top
    total = lax.dot_general(
        rows_sc[...], ones_sc[...], (((1,), (1,)), ((), ())), preferred_element_type=f32
    )
    size = 3 * blocks
    total = total[:size] + (total[size : 2 * size] + total[2 * size :])
    for k in range(3):
        inter_ref[k] = total[k * blocks : (k + 1) * blocks]
        for j in range(tiles):
            at = k * blocks + j * width
            q = k * tiles + j
            left_ref[q : q + 1, :] = total[at : at + 1]
            right_ref[q : q + 1, :] = total[at + width - 1 : at + width]


def finish_body(base_ref, inter_ref, left_ref, right_ref, out_ref):
    k = pl.program_id(0)
    _, width, _, depth = base_ref.shape
    tiles = depth // LANES
    lane = lax.broadcasted_iota(jnp.int32, (width, LANES), 1)
    parts = [inter_ref[0, j * width : (j + 1) * width, :] for j in range(tiles)]
    down = [pltpu.roll(p, 1, 1) for p in parts]
    up = [pltpu.roll(p, LANES - 1, 1) for p in parts]
    line = lax.broadcasted_iota(jnp.int32, (width, LANES), 0)
    for j in range(tiles):
        mid = parts[j]
        back = jnp.where(lane == 0, down[j - 1] if j else 0.0, down[j])
        fore = jnp.where(lane == LANES - 1, up[j + 1] if j + 1 < tiles else 0.0, up[j])
        q = k * tiles + j
        prev = jnp.where(line == 0, left_ref[pl.ds(q, 1), :], pltpu.roll(mid, 1, 0))
        after = jnp.where(line == width - 1, right_ref[pl.ds(q, 1), :], pltpu.roll(mid, width - 1, 0))
        near = ((prev + after) + (back + fore)) * (share * share)
        one = mid * (1.2 * share) + near
        two = mid * (share * share)
        span = slice(j * LANES, (j + 1) * LANES)
        for x in range(width):
            base = base_ref[0, x, :, span]
            row = lax.broadcasted_iota(jnp.int32, base.shape, 0)
            add = jnp.where(row == 1, one[x : x + 1], jnp.where(row == 2, two[x : x + 1], 0.0))
            out_ref[0, x, :, span] = jnp.where(row == 0, mid[x : x + 1], base + add)


def exchange(packed, per, cap):
    if per:
        return lax.all_to_all(packed, "dev", split_axis=0, concat_axis=0, tiled=True)
    count = lax.axis_size("dev")
    split = packed.reshape(3, count, cap)
    moved = lax.all_to_all(split, "dev", split_axis=1, concat_axis=1, tiled=True)
    return moved.reshape(packed.shape)


def local(
    displacement,
    send_node,
    member_slot,
    inverse_part,
    source_coord,
    target_coord,
    unity_weight,
    result_pick,
    receive_vertex,
    mesh_before,
):
    count = lax.axis_size("dev")
    place = lax.axis_index("dev")
    send_cap = send_node.shape[0] // count
    result_cap = result_pick.shape[0] // count
    send_per = send_cap // LANES if send_cap % LANES == 0 else 0
    result_per = result_cap // LANES if result_cap % LANES == 0 else 0
    clusters, points = member_slot.shape
    verts = unity_weight.shape[1]
    comps, width, height, depth = mesh_before.shape
    tiles = depth // LANES
    blocks = width * tiles

    def packed_shape(per, size):
        shape = (count, 3 * per, LANES) if per else (3, size // LANES, LANES)
        return jax.ShapeDtypeStruct(shape, f32)

    up = [(i, i + 1) for i in range(count - 1)]
    down = [(i + 1, i) for i in range(count - 1)]

    outgoing = pl.pallas_call(
        lambda *refs: pick_body(*refs, per=send_per),
        out_shape=packed_shape(send_per, send_node.shape[0]),
        in_specs=[VMEM, VMEM],
        out_specs=VMEM,
        compiler_params=params(4),
        name="pick_nodes",
    )(displacement, send_node.reshape(-1, LANES))
    arrived = exchange(outgoing, send_per, send_cap)

    halo_left = lax.ppermute(mesh_before[:, width - 2 :], "dev", up)
    halo_right = lax.ppermute(mesh_before[:, :2], "dev", down)

    pair = jax.ShapeDtypeStruct((clusters, points, verts), bf16)
    kernel_high, kernel_low = pl.pallas_call(
        kernel_body,
        out_shape=(pair, pair),
        in_specs=[VMEM, VMEM],
        out_specs=(VMEM, VMEM),
        scratch_shapes=[pltpu.VMEM((points, SUB), f32)],
        compiler_params=params(24),
        name="rbf_matrix",
    )(source_coord, target_coord)

    outgoing_results = pl.pallas_call(
        lambda *refs: result_body(*refs, per_in=send_per, per_out=result_per),
        out_shape=packed_shape(result_per, result_pick.shape[0]),
        in_specs=[VMEM, VMEM, ANY, VMEM, VMEM, VMEM, VMEM],
        out_specs=VMEM,
        scratch_shapes=[
            pltpu.VMEM((clusters, points, points), bf16),
            pltpu.VMEM((clusters, SUB, points), f32),
            pltpu.VMEM((clusters, SUB, verts), f32),
            pltpu.SemaphoreType.DMA((clusters,)),
        ],
        compiler_params=params(40),
        name="cluster_results",
    )(arrived, member_slot, inverse_part, kernel_high, kernel_low, unity_weight, result_pick.reshape(-1, LANES))
    returned = exchange(outgoing_results, result_per, result_cap)

    edges = jnp.stack([place, count - 1 - place]).astype(jnp.int32)
    batch = 4 if width % 4 == 0 else 1
    slots = 4
    base = pl.pallas_call(
        lambda *refs: mesh_body(*refs, batch=batch),
        out_shape=jax.ShapeDtypeStruct(mesh_before.shape, f32),
        in_specs=[SMEM, ANY, ANY, ANY],
        out_specs=ANY,
        scratch_shapes=[
            pltpu.VMEM((comps, width + 4, tiles, height + 2 * SUB, LANES), f32),
            pltpu.VMEM((width + 2, tiles, height + 2 * SUB, LANES), f32),
            pltpu.VMEM((slots, height, depth), f32),
            pltpu.SemaphoreType.DMA((comps, width // batch, tiles)),
            pltpu.SemaphoreType.DMA((comps, tiles, 2)),
            pltpu.SemaphoreType.DMA((slots,)),
        ],
        compiler_params=params(32),
        name="sweeps",
    )(edges, mesh_before, halo_left, halo_right)

    slots_in = receive_vertex.shape[0]
    edge_shape = jax.ShapeDtypeStruct((3 * tiles, LANES), f32)
    interface, first, last = pl.pallas_call(
        lambda *refs: scatter_body(*refs, per=result_per, width=width),
        out_shape=(jax.ShapeDtypeStruct((3, blocks, LANES), f32), edge_shape, edge_shape),
        in_specs=[VMEM, VMEM],
        out_specs=(VMEM, VMEM, VMEM),
        scratch_shapes=[pltpu.VMEM((9 * blocks, slots_in), bf16), pltpu.VMEM((LANES, slots_in), bf16)],
        compiler_params=params(24),
        name="scatter",
    )(returned, receive_vertex.reshape(-1, LANES))

    from_left = lax.ppermute(last, "dev", up)
    from_right = lax.ppermute(first, "dev", down)

    wall = pl.BlockSpec((1, width, SUB, depth), lambda k: (k, 0, 0, 0))
    return pl.pallas_call(
        finish_body,
        out_shape=jax.ShapeDtypeStruct(mesh_before.shape, f32),
        grid=(comps,),
        in_specs=[wall, pl.BlockSpec((1, blocks, LANES), lambda k: (k, 0, 0)), VMEM, VMEM],
        out_specs=wall,
        input_output_aliases={0: 0},
        compiler_params=params(8),
        name="finish",
    )(base, interface, from_left, from_right)


def solution(mesh):
    in_specs = (
        P(None, "dev"),
        P("dev"),
        P("dev", None),
        P("dev", None, None),
        P("dev", None, None),
        P("dev", None, None),
        P("dev", None),
        P("dev"),
        P("dev"),
        P(None, "dev", None, None),
    )
    out_specs = P(None, "dev", None, None)
    return jax.shard_map(local, mesh=mesh, in_specs=in_specs, out_specs=out_specs, check_vma=False)
```

time: 306 us -> 129 us (0.42)
  other arithmetic: 127 us -> 0.08 us
  Pallas kernels: 0 us -> 72.9 us
  local copies, waits for them, and re-layouts: 92 us -> 22.5 us
  waiting for transfers between devices: 41.2 us -> 7.11 us
  matrix products: 26.5 us -> 0 us
  starting transfers between devices: 18.8 us -> 24.1 us
    select_n x6 -> x0, other arithmetic: 78.6 us -> none  [the longest x2 58.2 us: relax(): return jnp.where(yrows == 0, center, moved)]
    pallas_call x0 -> x6, Pallas kernels: none -> 72.9 us  [the longest x1 27.9 us: local(): pl.pallas_call(kernel_body, out_shape=(pair, pair), in_specs=[VMEM, VMEM]...]
    gather x4 -> x0, local copies, waits for them, and re-layouts: 69.5 us -> none  [the longest x1 28 us: local(): picked = jnp.take(displacement, jnp.maximum(send_node, 0), axis=1)]
    scatter-add x1 -> x0, other arithmetic: 46.5 us -> none  [local(): jnp.zeros((3, width_x * depth_z), jnp.float32).at[:, receive_vertex]]
    ppermute x4, waiting for transfers between devices: 27.1 us -> 0.01 us  [the longest x1 0.01 us: local(): from_right = lax.ppermute(first, 'dev', down)]
    dot_general x2 -> x0, matrix products: 26.5 us -> none  [the longest x1 20.8 us: local(): jnp.einsum('kcp,ctp->kct', coefficient, kernel, precision=lax.Precision.H...]
    unnamed x15 -> x22, local copies, waits for them, and re-layouts: 5.23 us -> 19.1 us
    reshape x4 -> x0, local copies, waits for them, and re-layouts: 10.3 us -> none  [the longest x1 3.48 us: local(): jnp.where(send_node[None, :] >= 0, picked, 0.0)]
  transfers between devices with their start and end apart: 6 -> 6, of which waited for: 6 -> 1; matrix products, arithmetic and copies ran while one was open for 0% -> 1% of each run, Pallas kernels for 0% -> 55%
where the time goes in v1:
time: 129 us; the launch traced here: 127 us
  Pallas kernels  72.9 us (57%)
  starting transfers between devices  24.1 us (19%)
  local copies, waits for them, and re-layouts  22.5 us (17%)
  waiting for transfers between devices  7.11 us (6%)
    pallas_call x1, Pallas kernels, local(): pl.pallas_call(kernel_body, out_shape=(pair, pair), in_specs=[VMEM, VMEM]...  27.9 us
    pallas_call x1, Pallas kernels, local(): pl.pallas_call(lambda *refs: mesh_body(*refs, batch=batch), out_shape=jax...  21.9 us
    unnamed x22, local copies, waits for them, and re-layouts  19.1 us
    pallas_call x1, Pallas kernels, local(): pl.pallas_call(lambda *refs: result_body(*refs, per_in=send_per, per_out=...  14.1 us
    all_to_all x2, starting transfers between devices, exchange(): lax.all_to_all(packed, 'dev', split_axis=0, concat_axis=0, tiled=True)  11 us
    all_to_all x2, waiting for transfers between devices, exchange(): lax.all_to_all(packed, 'dev', split_axis=0, concat_axis=0, tiled=True)  7.09 us
    ppermute x1, starting transfers between devices, local(): from_right = lax.ppermute(first, 'dev', down)  4.72 us
    ppermute x1, starting transfers between devices, local(): halo_right = lax.ppermute(mesh_before[:, :2], 'dev', down)  4.54 us
  transfers between devices with their start and end apart: 6, of which 1 were waited for; matrix products, arithmetic and copies ran while one was open for 1% of the time, Pallas kernels for 55%

profile of v1, /device:TPU:4, one launch (start us, length us, event | category | flops | bytes accessed | tf_op | source)
XLA Modules:
  0.0 126.9 jit_solution(7070375366291317060)
XLA Ops:
  0.0 3.3 %fusion = (f32[3,2,96,512]{3,2,1,0:T(8,128)}, f32[3,2,96,512]{3,2,1,0:T(8,128)}) fusion(f32[3,16,96,512]{3,2,1,0:T(8,128)} %refs_1_.2), kind=kLoop, calls=%fused_computation.1 | loop fusion | bytes 4718592 | tf_op jit(solution)/shard_map/slice | solution.py:411
  3.3 1.9 %collective-permute-start = (f32[3,2,96,512]{3,2,1,0:T(8,128)}, f32[3,2,96,512]{3,2,1,0:T(8,128)S(1)}, u32[]{:S(2)}, u32[]{:S(2)}) collective-permute-start(f32[3,2,96,512]{3,2,1,0:T(8,128)} %get-tuple-element.16), channel_id=1, source_target_pairs={{0,1},{1,2},{2,3},{3,4},{4,5},{5,6},{6,7},{7,8},{8,9},{9,10},{10,1... | collective-permute-start | bytes 3538952 | tf_op jit(solution)/shard_map/ppermute | solution.py:410
  5.2 4.5 %collective-permute-start.1 = (f32[3,2,96,512]{3,2,1,0:T(8,128)}, f32[3,2,96,512]{3,2,1,0:T(8,128)S(1)}, u32[]{:S(2)}, u32[]{:S(2)}) collective-permute-start(f32[3,2,96,512]{3,2,1,0:T(8,128)} %get-tuple-element.15), channel_id=1, source_target_pairs={{1,0},{2,1},{3,2},{4,3},{5,4},{6,5},{7,6},{8,7},{9,8},{10,9},{11,1... | collective-permute-start | bytes 3538952 | tf_op jit(solution)/shard_map/ppermute | solution.py:411
  9.8 0.8 copy-done.4
  10.6 0.8 copy-done.6
  11.4 2.3 %pick_nodes.1 = f32[32,6,128]{2,1,0:T(8,128)} custom-call(f32[3,4096]{1,0:T(4,128)S(1)} %copy-done.4, s32[64,128]{1,0:T(8,128)S(1)} %bitcast.6), custom_call_target="tpu_custom_call" | custom-call | tf_op jit(solution)/shard_map/pick_nodes/pallas_call | solution.py:400
  13.7 5.2 %all-to-all-start = ((f32[32,6,128]{2,1,0:T(8,128)}), f32[32,6,128]{2,1,0:T(8,128)S(1)}, u32[]{:S(2)}, u32[]{:S(2)}) async-start(f32[32,6,128]{2,1,0:T(8,128)} %pick_nodes.1), calls=%async_computation | async-start | bytes 262144 | tf_op jit(solution)/shard_map/all_to_all | solution.py:362
  18.9 0.8 copy.12.source_ref
  19.8 0.8 copy.13.target_ref
  20.6 27.9 %rbf_matrix.1 = (bf16[4,1024,1024]{2,1,0:T(8,128)(2,1)S(1)}, bf16[4,1024,1024]{2,1,0:T(8,128)(2,1)S(1)}) custom-call(f32[4,3,1024]{2,1,0:T(4,128)S(1)} %copy.12.source_ref, f32[4,3,1024]{2,1,0:T(4,128)S(1)} %copy.13.target_ref), custom_call_target="tpu_custom_call" | custom-call | tf_op jit(solution)/shard_map/rbf_matrix/pallas_call | solution.py:414
  48.5 3.4 %copy-done.2 = bf16[4,1024,1024]{2,1,0:T(8,128)(2,1)} copy-done((bf16[4,1024,1024]{2,1,0:T(8,128)(2,1)}, bf16[4,1024,1024]{2,1,0:T(8,128)(2,1)S(1)}, u32[]{:S(2)}) %copy-start.2) | copy-done | bytes 8388632
  51.9 3.2 %copy-done.3 = bf16[4,1024,1024]{2,1,0:T(8,128)(2,1)} copy-done((bf16[4,1024,1024]{2,1,0:T(8,128)(2,1)}, bf16[4,1024,1024]{2,1,0:T(8,128)(2,1)S(1)}, u32[]{:S(2)}) %copy-start.3) | copy-done | bytes 8388632
  55.2 3.4 %copy-done.1 = bf16[4,1024,1024]{2,1,0:T(8,128)(2,1)S(1)} copy-done((bf16[4,1024,1024]{2,1,0:T(8,128)(2,1)S(1)}, bf16[4,1024,1024]{2,1,0:T(8,128)(2,1)}, u32[]{:S(2)}) %copy-start.1) | copy-done | bytes 8388632
  58.5 0.8 copy-done.5
  59.3 0.7 copy-done.8
  60.7 14.1 %cluster_results.1 = f32[32,6,128]{2,1,0:T(8,128)} custom-call(f32[32,6,128]{2,1,0:T(8,128)S(1)} %all-to-all-done.refs_0_, s32[4,1024]{1,0:T(4,128)S(1)} %copy-done.8, bf16[4,1024,1024]{2,1,0:T(8,128)(2,1)S(1)} %copy-done.1, bf16[4,1024,1024]{2,1,0:T(8,128)(2,1)} %copy-done.2, bf16[4,1024,1024]{2,1,0:T(8,128)(2,1)} %copy-done.3, f32[4,1024]{1,0:T(4,128)S(1)} %copy-done.9, ...), custom_call_target="tpu_custom_call" | custom-call | tf_op jit(solution)/shard_map/cluster_results/pallas_call | solution.py:424
  74.8 5.8 %all-to-all-start.1 = ((f32[32,6,128]{2,1,0:T(8,128)}), f32[32,6,128]{2,1,0:T(8,128)S(1)}, u32[]{:S(2)}, u32[]{:S(2)}) async-start(f32[32,6,128]{2,1,0:T(8,128)} %cluster_results.1), calls=%async_computation.1 | async-start | bytes 262144 | tf_op jit(solution)/shard_map/all_to_all | solution.py:362
  80.7 7.1 %all-to-all-done.1.refs_0_ = f32[32,6,128]{2,1,0:T(8,128)S(1)} async-done(((f32[32,6,128]{2,1,0:T(8,128)}), f32[32,6,128]{2,1,0:T(8,128)S(1)}, u32[]{:S(2)}, u32[]{:S(2)}) %all-to-all-start.1) | async-done | bytes 98336 | tf_op jit(solution)/shard_map/all_to_all | solution.py:362
  87.8 3.7 %scatter.1 = (f32[3,64,128]{2,1,0:T(8,128)S(1)}, f32[12,128]{1,0:T(8,128)S(1)}, f32[12,128]{1,0:T(8,128)S(1)}) custom-call(f32[32,6,128]{2,1,0:T(8,128)S(1)} %all-to-all-done.1.refs_0_, s32[64,128]{1,0:T(8,128)S(1)} %bitcast.7), custom_call_target="tpu_custom_call" | custom-call | tf_op jit(solution)/shard_map/scatter/pallas_call | solution.py:462
  91.5 1.9 %collective-permute-start.2 = (f32[12,128]{1,0:T(8,128)S(1)}, f32[12,128]{1,0:T(8,128)S(1)}, u32[]{:S(2)}, u32[]{:S(2)}) collective-permute-start(f32[12,128]{1,0:T(8,128)S(1)} %get-tuple-element.13), channel_id=1, source_target_pairs={{0,1},{1,2},{2,3},{3,4},{4,5},{5,6},{6,7},{7,8},{8,9},{9,10},{10,1... | collective-permute-start | bytes 18440 | tf_op jit(solution)/shard_map/ppermute | solution.py:472
  93.4 4.7 %collective-permute-start.3 = (f32[12,128]{1,0:T(8,128)S(1)}, f32[12,128]{1,0:T(8,128)S(1)}, u32[]{:S(2)}, u32[]{:S(2)}) collective-permute-start(f32[12,128]{1,0:T(8,128)S(1)} %get-tuple-element.14), channel_id=1, source_target_pairs={{1,0},{2,1},{3,2},{4,3},{5,4},{6,5},{7,6},{8,7},{9,8},{10,9},{11,1... | collective-permute-start | bytes 18440 | tf_op jit(solution)/shard_map/ppermute | solution.py:473
  98.2 3.7 %copy-done = f32[3,16,96,512]{3,2,1,0:T(8,128)S(1)} copy-done((f32[3,16,96,512]{3,2,1,0:T(8,128)S(1)}, f32[3,16,96,512]{3,2,1,0:T(8,128)}, u32[]{:S(2)}) %copy-start) | copy-done | bytes 9437208
  101.9 21.9 %sweeps.1.base_ref = f32[3,16,96,512]{3,2,1,0:T(8,128)} custom-call(s32[2]{0:T(128)S(1)} %pad_add_fusion.refs_0_, f32[3,16,96,512]{3,2,1,0:T(8,128)S(1)} %copy-done, f32[3,2,96,512]{3,2,1,0:T(8,128)S(1)} %collective-permute-done.refs_2_, f32[3,2,96,512]{3,2,1,0:T(8,128)S(1)} %collective-permute-done.1.refs_3_), custom_call_target="tpu_custom_call" | custom-call | tf_op jit(solution)/shard_map/sweeps/pallas_call | solution.py:443
  123.8 3.0 %finish.1 = f32[3,16,96,512]{3,2,1,0:T(8,128)} custom-call(f32[3,16,96,512]{3,2,1,0:T(8,128)} %sweeps.1.base_ref, f32[3,64,128]{2,1,0:T(8,128)S(1)} %get-tuple-element.12.inter_ref, f32[12,128]{1,0:T(8,128)S(1)} %collective-permute-done.2.left_ref, f32[12,128]{1,0:T(8,128)S(1)} %collective-permute-done.3.right_ref), custom_call_target="tpu_custom_call", output_to_operand_aliasing={{}: (0, {})} | custom-call | tf_op jit(solution)/shard_map/finish/pallas_call | solution.py:476
  (18 shorter events, 0.8 us)
Async XLA Ops:
  3.3 94.9 %collective-permute-start = (f32[3,2,96,512]{3,2,1,0:T(8,128)}, f32[3,2,96,512]{3,2,1,0:T(8,128)S(1)}, u32[]{:S(2)}, u32[]{:S(2)}) collective-permute-start(f32[3,2,96,512]{3,2,1,0:T(8,128)} %get-tuple-element.16), channel_id=1, source_target_pairs={{0,1},{1,2},{2,3},{3,4},{4,5},{5,6},{6,7},{7,8},{8,9},{9,10},{10,1... | collective-permute-start | bytes 3538952 | tf_op jit(solution)/shard_map/ppermute | solution.py:410
  5.2 93.0 %collective-permute-start.1 = (f32[3,2,96,512]{3,2,1,0:T(8,128)}, f32[3,2,96,512]{3,2,1,0:T(8,128)S(1)}, u32[]{:S(2)}, u32[]{:S(2)}) collective-permute-start(f32[3,2,96,512]{3,2,1,0:T(8,128)} %get-tuple-element.15), channel_id=1, source_target_pairs={{1,0},{2,1},{3,2},{4,3},{5,4},{6,5},{7,6},{8,7},{9,8},{10,9},{11,1... | collective-permute-start | bytes 3538952 | tf_op jit(solution)/shard_map/ppermute | solution.py:411
  9.8 0.8 copy-start.4
  10.6 0.8 copy-start.6
  13.7 41.4 %all-to-all-start = ((f32[32,6,128]{2,1,0:T(8,128)}), f32[32,6,128]{2,1,0:T(8,128)S(1)}, u32[]{:S(2)}, u32[]{:S(2)}) async-start(f32[32,6,128]{2,1,0:T(8,128)} %pick_nodes.1), calls=%async_computation | async-start | bytes 262144 | tf_op jit(solution)/shard_map/all_to_all | solution.py:362
  48.5 3.4 %copy-start.2 = (bf16[4,1024,1024]{2,1,0:T(8,128)(2,1)}, bf16[4,1024,1024]{2,1,0:T(8,128)(2,1)S(1)}, u32[]{:S(2)}) copy-start(bf16[4,1024,1024]{2,1,0:T(8,128)(2,1)S(1)} %get-tuple-element.10.refs_3_) | copy-start | bytes 25165828
  51.9 3.2 %copy-start.3 = (bf16[4,1024,1024]{2,1,0:T(8,128)(2,1)}, bf16[4,1024,1024]{2,1,0:T(8,128)(2,1)S(1)}, u32[]{:S(2)}) copy-start(bf16[4,1024,1024]{2,1,0:T(8,128)(2,1)S(1)} %get-tuple-element.11.refs_4_) | copy-start | bytes 25165828
  55.2 3.4 %copy-start.1 = (bf16[4,1024,1024]{2,1,0:T(8,128)(2,1)S(1)}, bf16[4,1024,1024]{2,1,0:T(8,128)(2,1)}, u32[]{:S(2)}) copy-start(bf16[4,1024,1024]{2,1,0:T(8,128)(2,1)} %refs_2_.1) | copy-start | bytes 25165828
  58.5 0.8 copy-start.5
  59.3 0.7 copy-start.8
  60.0 0.7 copy-start.9
  60.7 27.0 %copy-start.7 = (s32[8192]{0:T(1024)S(1)}, s32[8192]{0:T(1024)}, u32[]{:S(2)}) copy-start(s32[8192]{0:T(1024)} %param.18) | copy-start | bytes 98308
  74.8 12.9 %all-to-all-start.1 = ((f32[32,6,128]{2,1,0:T(8,128)}), f32[32,6,128]{2,1,0:T(8,128)S(1)}, u32[]{:S(2)}, u32[]{:S(2)}) async-start(f32[32,6,128]{2,1,0:T(8,128)} %cluster_results.1), calls=%async_computation.1 | async-start | bytes 262144 | tf_op jit(solution)/shard_map/all_to_all | solution.py:362
  91.5 32.4 %collective-permute-start.2 = (f32[12,128]{1,0:T(8,128)S(1)}, f32[12,128]{1,0:T(8,128)S(1)}, u32[]{:S(2)}, u32[]{:S(2)}) collective-permute-start(f32[12,128]{1,0:T(8,128)S(1)} %get-tuple-element.13), channel_id=1, source_target_pairs={{0,1},{1,2},{2,3},{3,4},{4,5},{5,6},{6,7},{7,8},{8,9},{9,10},{10,1... | collective-permute-start | bytes 18440 | tf_op jit(solution)/shard_map/ppermute | solution.py:472
  93.4 30.4 %collective-permute-start.3 = (f32[12,128]{1,0:T(8,128)S(1)}, f32[12,128]{1,0:T(8,128)S(1)}, u32[]{:S(2)}, u32[]{:S(2)}) collective-permute-start(f32[12,128]{1,0:T(8,128)S(1)} %get-tuple-element.14), channel_id=1, source_target_pairs={{1,0},{2,1},{3,2},{4,3},{5,4},{6,5},{7,6},{8,7},{9,8},{10,9},{11,1... | collective-permute-start | bytes 18440 | tf_op jit(solution)/shard_map/ppermute | solution.py:473
  98.2 3.7 %copy-start = (f32[3,16,96,512]{3,2,1,0:T(8,128)S(1)}, f32[3,16,96,512]{3,2,1,0:T(8,128)}, u32[]{:S(2)}) copy-start(f32[3,16,96,512]{3,2,1,0:T(8,128)} %refs_1_.2) | copy-start | bytes 28311556

commit v2 on v1

--- a/solution.py
+++ b/solution.py
@@ -7,16 +7,23 @@
 from jax.experimental.pallas import tpu as pltpu
 from jax.sharding import PartitionSpec as P
 
+
 LANES = 128
 SUB = 8
 share = 0.8 / 6.0
 keep = 0.2 / share
 sharpness = 8.0
+AHEAD = 2
 VMEM = pl.BlockSpec(memory_space=pltpu.VMEM)
 ANY = pl.BlockSpec(memory_space=pl.ANY)
+HBM = pl.BlockSpec(memory_space=pltpu.HBM)
 SMEM = pl.BlockSpec(memory_space=pltpu.SMEM)
 f32 = jnp.float32
 bf16 = jnp.bfloat16
+
+
+def in_hbm(value):
+    return pltpu.with_memory_space_constraint(value, pltpu.HBM)
 
 
 def params(limit, **more):
@@ -78,63 +85,136 @@
             store_rows(out_ref, first + g, got[g], per)
 
 
-def kernel_body(source_ref, target_ref, high_ref, low_ref, turned):
-    clusters, _, points = source_ref.shape
+def pieces(value, count=3):
+    found = []
+    for _ in range(count):
+        top = value.astype(bf16).astype(f32)
+        found.append(top)
+        value = value - top
+    return found
+
+
+def factor(points, target):
+    square = points * points
+    norm = jnp.broadcast_to(jnp.sum(square, axis=0, keepdims=True), square.shape)
+    row = lax.broadcasted_iota(jnp.int32, square.shape, 0)
+    a, b, c = pieces(norm)
+    p, q, r = pieces(points)
+    if target:
+        edge = jnp.where(row < 3, -1.0, jnp.where(row == 3, -a, jnp.where(row == 4, -b, jnp.where(row == 5, -c, 0.0))))
+        blocks = [2.0 * p, 2.0 * q, 2.0 * p, 2.0 * q, 2.0 * r, 2.0 * p, edge]
+    else:
+        edge = jnp.where(row == 0, a, jnp.where(row == 1, b, jnp.where(row == 2, c, jnp.where(row < 6, 1.0, 0.0))))
+        blocks = [p, p, q, q, p, r, edge]
+    blocks.append(jnp.zeros(square.shape, f32))
+    return jnp.concatenate(blocks, axis=0)
+
+
+def rbf_matrix(source, target, put):
     scale = math.sqrt(sharpness * math.log2(math.e))
-    step = 16
-    for c in range(clusters):
-        rows = jnp.concatenate([source_ref[c] * scale, jnp.zeros((SUB - 3, points), f32)], axis=0)
-        turned[...] = jnp.transpose(rows)
-        goal = [target_ref[c, k : k + 1, :] * scale for k in range(3)]
-
-        def body(i, _, c=c, goal=goal):
-            at = pl.multiple_of(i * step, step)
-            part = turned[pl.ds(at, step), :]
-            gap = goal[0] - part[:, 0:1]
-            spread = gap * gap
-            gap = goal[1] - part[:, 1:2]
-            spread = spread + gap * gap
-            gap = goal[2] - part[:, 2:3]
-            spread = spread + gap * gap
-            value = jnp.exp2(-spread)
-            high = value.astype(bf16)
-            high_ref[c, pl.ds(at, step), :] = high
-            low_ref[c, pl.ds(at, step), :] = (value - high.astype(f32)).astype(bf16)
-            return 0
-
-        lax.fori_loop(0, points // step, body, 0)
+    points = source[0].shape[1]
+    step = LANES
+
+    def centred(rows):
+        blank = jnp.zeros((SUB - 3, rows[0].shape[1]), f32)
+        return jnp.concatenate([(row - 0.5) * scale for row in rows] + [blank], axis=0)
+
+    turned = jnp.transpose(factor(centred(source), False)).astype(bf16)
+    right = factor(centred(target), True).astype(bf16)
+    for at in range(0, points, step):
+        value = jnp.exp2(jnp.dot(turned[at : at + step], right, preferred_element_type=f32))
+        high = value.astype(bf16)
+        put(at, step, high, (value - high.astype(f32)).astype(bf16))
+
+
+def prepare_body(
+    source_ref, target_ref, slot_ref, weight_ref, pick_ref, vertex_ref, mesh_ref,
+    high_out, low_out, slot_out, weight_out, pick_out, vertex_out, source, target, head_out, tail_out,
+    high, low, head, tail, sems, done,
+):
+    width = mesh_ref.shape[1]
+    needed = [
+        pltpu.make_async_copy(source_ref, source, sems.at[0]),
+        pltpu.make_async_copy(target_ref, target, sems.at[1]),
+    ]
+    others = [
+        pltpu.make_async_copy(slot_ref, slot_out, sems.at[4]),
+        pltpu.make_async_copy(weight_ref, weight_out, sems.at[5]),
+        pltpu.make_async_copy(pick_ref, pick_out, sems.at[6]),
+        pltpu.make_async_copy(vertex_ref, vertex_out, sems.at[7]),
+    ]
+    side_in = [
+        pltpu.make_async_copy(mesh_ref.at[:, pl.ds(0, 2)], head, sems.at[2]),
+        pltpu.make_async_copy(mesh_ref.at[:, pl.ds(width - 2, 2)], tail, sems.at[3]),
+    ]
+    side_out = [
+        pltpu.make_async_copy(head, head_out, sems.at[8]),
+        pltpu.make_async_copy(tail, tail_out, sems.at[9]),
+    ]
+    for copy in needed + side_in + others:
+        copy.start()
+    for copy in needed:
+        copy.wait()
+    last = []
+    for c in range(high_out.shape[0]):
+
+        def put(at, step, upper, lower, c=c):
+            high[c, at : at + step, :] = upper
+            low[c, at : at + step, :] = lower
+
+        rbf_matrix(*(tuple(ref[k, c : c + 1, :] for k in range(3)) for ref in (source, target)), put)
+        last.append(pltpu.make_async_copy(high.at[c], high_out.at[c], done.at[0, c]))
+        last.append(pltpu.make_async_copy(low.at[c], low_out.at[c], done.at[1, c]))
+        for copy in last[-2:]:
+            copy.start()
+        if c == 0:
+            for before, after in zip(side_in, side_out):
+                before.wait()
+                after.start()
+    for copy in others + last + side_out:
+        copy.wait()
 
 
 def result_body(
-    arrived_ref, slot_ref, inverse_ref, high_ref, low_ref, weight_ref, pick_ref, out_ref, inverse, members, results, sems, *, per_in, per_out
+    arrived_ref, slot_ref, source_ref, target_ref, inverse_ref, high_ref, low_ref, weight_ref, pick_ref,
+    out_ref, inverse, high, low, members, results, sems, *, per_in, per_out, ahead,
 ):
     clusters, points = slot_ref.shape
     verts = weight_ref.shape[1]
-    copies = [pltpu.make_async_copy(inverse_ref.at[c], inverse.at[c], sems.at[c]) for c in range(clusters)]
-    for copy in copies:
-        copy.start()
-    fold = SUB // clusters
-    groups = points // LANES // fold
     blocks = (arrived_ref.shape[0] * per_in) if per_in else arrived_ref.shape[1]
-    got = gather_rows(
-        lambda k, b: packed_row(arrived_ref, k, b, per_in),
-        blocks,
-        lambda g: jnp.concatenate(
-            [slot_ref[:, (g * fold + j) * LANES : (g * fold + j + 1) * LANES] for j in range(fold)], axis=0
-        ),
-        groups,
-    )
+    per_cluster = verts // LANES
+    groups = pick_ref.shape[0] // SUB
+    fold = points // LANES // SUB
+    order = list(range(ahead, clusters)) + list(range(ahead))
+    copies = {}
+    for c in order:
+        copies[c] = [pltpu.make_async_copy(inverse_ref.at[c], inverse.at[c], sems.at[0, c])]
+        if c < ahead:
+            copies[c].append(pltpu.make_async_copy(high_ref.at[c], high.at[c], sems.at[1, c]))
+            copies[c].append(pltpu.make_async_copy(low_ref.at[c], low.at[c], sems.at[2, c]))
+        for copy in copies[c]:
+            copy.start()
     members[...] = jnp.zeros(members.shape, f32)
-    for g in range(groups):
-        for j in range(fold):
-            at = (g * fold + j) * LANES
-            for c in range(clusters):
+
+    def gather_members(c):
+        got = gather_rows(
+            lambda k, b: packed_row(arrived_ref, k, b, per_in),
+            blocks,
+            lambda g: jnp.concatenate(
+                [slot_ref[c : c + 1, (g * SUB + j) * LANES : (g * SUB + j + 1) * LANES] for j in range(SUB)], axis=0
+            ),
+            fold,
+        )
+        for g in range(fold):
+            for j in range(SUB):
+                at = (g * SUB + j) * LANES
                 for k in range(3):
-                    s = j * clusters + c
-                    members[c, k : k + 1, at : at + LANES] = got[g][k][s : s + 1, :]
-    for c in range(clusters):
-        copies[c].wait()
+                    members[c, k : k + 1, at : at + LANES] = got[g][k][j : j + 1, :]
+
+    def evaluate(c):
         mine = members[c]
+        for copy in copies[c]:
+            copy.wait()
         coupling = lax.dot_general(
             mine.astype(bf16), inverse[c], (((1,), (1,)), ((), ())), preferred_element_type=f32
         )
@@ -142,12 +222,21 @@
         c_high = coefficient.astype(bf16)
         c_low = (coefficient - c_high.astype(f32)).astype(bf16)
         both = jnp.concatenate([c_high, c_low], axis=0)
-        first = jnp.dot(both, high_ref[c], preferred_element_type=f32)
-        second = jnp.dot(c_high, low_ref[c], preferred_element_type=f32)
+        first = jnp.dot(both, high[c], preferred_element_type=f32)
+        second = jnp.dot(c_high, low[c], preferred_element_type=f32)
         total = first[:SUB] + (first[SUB:] + second)
         results[c] = total * weight_ref[c : c + 1, :]
-    per_cluster = verts // LANES
-    groups = pick_ref.shape[0] // SUB
+
+    for c in order:
+        if c >= ahead:
+
+            def put(at, step, upper, lower, c=c):
+                high[c, at : at + step, :] = upper
+                low[c, at : at + step, :] = lower
+
+            rbf_matrix(*(tuple(ref[k, c : c + 1, :] for k in range(3)) for ref in (source_ref, target_ref)), put)
+        gather_members(c)
+        evaluate(c)
     half = max(1, groups // 2)
     for start in range(0, groups, half):
         got = gather_rows(
@@ -162,11 +251,12 @@
             store_rows(out_ref, start + g, got[g], per_out)
 
 
-def mesh_body(edge_ref, mesh_ref, left_ref, right_ref, out_ref, field, swept, stage, in_sems, side_sems, out_sems, *, batch):
+def mesh_body(_, edge_ref, mesh_ref, left_ref, right_ref, out_ref, field, ring, stage, in_sems, side_sems, out_sems, *, batch):
     comps, width, height, depth = mesh_ref.shape
     tiles = depth // LANES
     strips = height // SUB
-    slots = stage.shape[0]
+    slots = len(stage)
+    turns = len(ring)
 
     def columns(j):
         return pl.ds(j * LANES, LANES)
@@ -205,88 +295,108 @@
 
     blank = jnp.zeros((SUB, LANES), f32)
     for j in range(tiles):
-        for x in range(width + 2):
-            swept[x, j, SUB + height : 2 * SUB + height, :] = blank
-        for x in range(width + 4):
-            for k in range(comps):
-                field[k, x, j, SUB + height : 2 * SUB + height, :] = blank
+        for plane in ring:
+            plane[j, SUB + height : 2 * SUB + height, :] = blank
+
+    def clear(i, _):
+        for j in range(tiles):
+            field[i // (width + 4), i % (width + 4), j, SUB + height : 2 * SUB + height, :] = blank
+        return 0
+
+    lax.fori_loop(0, comps * (width + 4), clear, 0)
 
     lane = lax.broadcasted_iota(jnp.int32, (SUB, LANES), 1)
     row = lax.broadcasted_iota(jnp.int32, (SUB, LANES), 0)
     is_first = lane == 0
     is_last = lane == LANES - 1
     wall = row == 0
-    above_wall = row == 1
-
-    def sweep(center, before, after, put):
+
+    def sweep_strip(y, center, before, after, put):
+        at = SUB + y * SUB
+        mid = [center[j, pl.ds(at, SUB), :] for j in range(tiles)]
+        down = [pltpu.roll(m, 1, 1) for m in mid]
+        up = [pltpu.roll(m, LANES - 1, 1) for m in mid]
+        for j in range(tiles):
+            lower = center[j, pl.ds(at - 1, SUB), :]
+            if y == 0:
+                lower = jnp.where(row < 2, 0.0, lower)
+            near = (before[j, pl.ds(at, SUB), :] + after[j, pl.ds(at, SUB), :]) + (
+                center[j, pl.ds(at + 1, SUB), :] + lower
+            )
+            near = near + keep * mid[j]
+            back = jnp.where(is_first, down[j - 1] if j else 0.0, down[j])
+            fore = jnp.where(is_last, up[j + 1] if j + 1 < tiles else 0.0, up[j])
+            value = near + (back + fore)
+            if y == 0:
+                value = jnp.where(wall, 0.0, value)
+            put(j, y, value)
+
+    def flush(k, x, slot):
+        return pltpu.make_async_copy(stage[slot], out_ref.at[k, x], out_sems.at[slot])
+
+    def work(k, x, phase, second):
+        def put_first(j, y, value):
+            ring[phase % turns][j, pl.ds(SUB + y * SUB, SUB), :] = value
+
+        def put_second(j, y, value):
+            stage[phase % slots][y * SUB : (y + 1) * SUB, j * LANES : (j + 1) * LANES] = value * (share * share)
+
         for y in range(strips):
-            at = SUB + y * SUB
-            mid = [center[j, pl.ds(at, SUB), :] for j in range(tiles)]
-            down = [pltpu.roll(m, 1, 1) for m in mid]
-            up = [pltpu.roll(m, LANES - 1, 1) for m in mid]
-            for j in range(tiles):
-                lower = center[j, pl.ds(at - 1, SUB), :]
-                if y == 0:
-                    lower = jnp.where(row < 2, 0.0, lower)
-                near = (before[j, pl.ds(at, SUB), :] + after[j, pl.ds(at, SUB), :]) + (
-                    center[j, pl.ds(at + 1, SUB), :] + lower
+            sweep_strip(y, field.at[k, x + 1], field.at[k, x], field.at[k, x + 2], put_first)
+            if second:
+                sweep_strip(
+                    y,
+                    ring[(phase - 2) % turns],
+                    ring[(phase - 3) % turns],
+                    ring[(phase - 1) % turns],
+                    put_second,
                 )
-                back = jnp.where(is_first, down[j - 1] if j else 0.0, down[j])
-                fore = jnp.where(is_last, up[j + 1] if j + 1 < tiles else 0.0, up[j])
-                value = (near + (back + fore)) + keep * mid[j]
-                if y == 0:
-                    value = jnp.where(wall, 0.0, value)
-                put(j, y, value)
-
-    def first_sweep(k, x):
-        def put(j, y, value):
-            swept[x, j, pl.ds(SUB + y * SUB, SUB), :] = value
-
-        sweep(field.at[k, x + 1], field.at[k, x], field.at[k, x + 2], put)
-
-    def flush(k, x, slot):
-        return pltpu.make_async_copy(stage.at[slot], out_ref.at[k, x], out_sems.at[slot])
+
+    def zero(place):
+        ring[place % turns][...] = jnp.zeros(ring[0].shape, f32)
 
     def component(k, _):
         for copy in sides(k):
             copy.wait()
         for copy in load(k, 0):
             copy.wait()
-        first_sweep(k, 0)
-
-        @pl.when(edge_ref[0] == 0)
-        def _():
-            swept[0] = jnp.zeros(swept.shape[1:], f32)
-
-        first_sweep(k, 1)
-
-        def step(x, _):
-            @pl.when(jnp.logical_and((x + 1) % batch == 0, x + 1 < width))
-            def _():
-                for copy in load(k, (x + 1) // batch):
-                    copy.wait()
-
-            first_sweep(k, x + 2)
-
-            @pl.when(jnp.logical_and(x + 2 == width + 1, edge_ref[1] == 0))
-            def _():
-                swept[width + 1] = jnp.zeros(swept.shape[1:], f32)
-
-            turn = k * width + x
-            slot = turn % slots
-
-            @pl.when(turn >= slots)
-            def _():
-                flush(k, x, slot).wait()
-
-            def put(j, y, value):
-                stage[slot, y * SUB : (y + 1) * SUB, j * LANES : (j + 1) * LANES] = value * (share * share)
-
-            sweep(swept.at[x + 1], swept.at[x], swept.at[x + 2], put)
-            flush(k, x, slot).start()
+        for phase in range(3):
+            work(k, phase, phase, False)
+            if phase == 0:
+
+                @pl.when(edge_ref[0] == 0)
+                def _():
+                    zero(0)
+
+        def quad(i, _):
+            for sub in range(turns):
+                x = i * turns + sub + 3
+                phase = sub + 3
+
+                if phase % batch == 0:
+
+                    @pl.when(x < width)
+                    def _():
+                        for copy in load(k, x // batch):
+                            copy.wait()
+
+                slot = phase % slots
+
+                @pl.when(k * width + i * turns + sub >= slots)
+                def _():
+                    flush(k, 0, slot).wait()
+
+                work(k, jnp.minimum(x, width + 1), phase, True)
+                if sub == turns - 2:
+
+                    @pl.when(jnp.logical_and(x == width + 1, edge_ref[1] == 0))
+                    def _():
+                        zero(phase)
+
+                flush(k, i * turns + sub, slot).start()
             return 0
 
-        lax.fori_loop(0, width, step, 0)
+        lax.fori_loop(0, width // turns, quad, 0)
         return 0
 
     lax.fori_loop(0, comps, component, 0)
@@ -294,7 +404,7 @@
         flush(0, 0, slot).wait()
 
 
-def scatter_body(returned_ref, vertex_ref, inter_ref, left_ref, right_ref, rows_sc, ones_sc, *, per, width):
+def scatter_body(_, returned_ref, vertex_ref, inter_ref, left_ref, right_ref, rows_sc, ones_sc, *, per, width):
     rows, _ = vertex_ref.shape
     blocks = inter_ref.shape[1]
     tiles = blocks // width
@@ -397,77 +507,95 @@
     up = [(i, i + 1) for i in range(count - 1)]
     down = [(i + 1, i) for i in range(count - 1)]
 
+    field = in_hbm(mesh_before)
     outgoing = pl.pallas_call(
         lambda *refs: pick_body(*refs, per=send_per),
         out_shape=packed_shape(send_per, send_node.shape[0]),
         in_specs=[VMEM, VMEM],
         out_specs=VMEM,
-        compiler_params=params(4),
+        compiler_params=params(2),
         name="pick_nodes",
     )(displacement, send_node.reshape(-1, LANES))
     arrived = exchange(outgoing, send_per, send_cap)
 
-    halo_left = lax.ppermute(mesh_before[:, width - 2 :], "dev", up)
-    halo_right = lax.ppermute(mesh_before[:, :2], "dev", down)
-
     pair = jax.ShapeDtypeStruct((clusters, points, verts), bf16)
-    kernel_high, kernel_low = pl.pallas_call(
-        kernel_body,
-        out_shape=(pair, pair),
-        in_specs=[VMEM, VMEM],
-        out_specs=(VMEM, VMEM),
-        scratch_shapes=[pltpu.VMEM((points, SUB), f32)],
-        compiler_params=params(24),
-        name="rbf_matrix",
-    )(source_coord, target_coord)
+    ahead = min(clusters, AHEAD)
+    pair = pltpu.HBM((ahead, points, verts), bf16)
+    side = pltpu.HBM((comps, 2, height, depth), f32)
+    source_turned = jnp.transpose(source_coord, (1, 0, 2))
+    target_turned = jnp.transpose(target_coord, (1, 0, 2))
+    small = (member_slot, unity_weight, result_pick.reshape(-1, LANES), receive_vertex.reshape(-1, LANES))
+    (kernel_high, kernel_low, slots, weight, picks, vertices, source, target, head, tail) = pl.pallas_call(
+        prepare_body,
+        out_shape=(pair, pair)
+        + tuple(pltpu.VMEM(x.shape, x.dtype) for x in small + (source_turned, target_turned))
+        + (side, side),
+        in_specs=[HBM] * 7,
+        out_specs=(HBM,) * 2 + (VMEM,) * 6 + (HBM,) * 2,
+        scratch_shapes=[
+            pltpu.VMEM((ahead, points, verts), bf16),
+            pltpu.VMEM((ahead, points, verts), bf16),
+            pltpu.VMEM((comps, 2, height, depth), f32),
+            pltpu.VMEM((comps, 2, height, depth), f32),
+            pltpu.SemaphoreType.DMA((10,)),
+            pltpu.SemaphoreType.DMA((2, ahead)),
+        ],
+        compiler_params=params(28),
+        name="prepare",
+    )(*map(in_hbm, (source_turned, target_turned) + small), field)
+    halo_left = lax.ppermute(tail, "dev", up)
+    halo_right = lax.ppermute(head, "dev", down)
 
     outgoing_results = pl.pallas_call(
-        lambda *refs: result_body(*refs, per_in=send_per, per_out=result_per),
+        lambda *refs: result_body(*refs, per_in=send_per, per_out=result_per, ahead=ahead),
         out_shape=packed_shape(result_per, result_pick.shape[0]),
-        in_specs=[VMEM, VMEM, ANY, VMEM, VMEM, VMEM, VMEM],
+        in_specs=[VMEM] * 4 + [HBM] * 3 + [VMEM] * 2,
         out_specs=VMEM,
         scratch_shapes=[
-            pltpu.VMEM((clusters, points, points), bf16),
+            pltpu.VMEM(inverse_part.shape, bf16),
+            pltpu.VMEM((clusters, points, verts), bf16),
+            pltpu.VMEM((clusters, points, verts), bf16),
             pltpu.VMEM((clusters, SUB, points), f32),
             pltpu.VMEM((clusters, SUB, verts), f32),
-            pltpu.SemaphoreType.DMA((clusters,)),
+            pltpu.SemaphoreType.DMA((3, clusters)),
         ],
         compiler_params=params(40),
         name="cluster_results",
-    )(arrived, member_slot, inverse_part, kernel_high, kernel_low, unity_weight, result_pick.reshape(-1, LANES))
+    )(arrived, slots, source, target, in_hbm(inverse_part), in_hbm(kernel_high), in_hbm(kernel_low), weight, picks)
     returned = exchange(outgoing_results, result_per, result_cap)
 
     edges = jnp.stack([place, count - 1 - place]).astype(jnp.int32)
-    batch = 4 if width % 4 == 0 else 1
-    slots = 4
+    batch = turns = 4
+    if width % turns:
+        raise ValueError("width")
     base = pl.pallas_call(
         lambda *refs: mesh_body(*refs, batch=batch),
         out_shape=jax.ShapeDtypeStruct(mesh_before.shape, f32),
-        in_specs=[SMEM, ANY, ANY, ANY],
-        out_specs=ANY,
+        in_specs=[ANY, SMEM, HBM, ANY, ANY],
+        out_specs=HBM,
         scratch_shapes=[
             pltpu.VMEM((comps, width + 4, tiles, height + 2 * SUB, LANES), f32),
-            pltpu.VMEM((width + 2, tiles, height + 2 * SUB, LANES), f32),
-            pltpu.VMEM((slots, height, depth), f32),
+            tuple(pltpu.VMEM((tiles, height + 2 * SUB, LANES), f32) for _ in range(turns)),
+            tuple(pltpu.VMEM((height, depth), f32) for _ in range(turns)),
             pltpu.SemaphoreType.DMA((comps, width // batch, tiles)),
             pltpu.SemaphoreType.DMA((comps, tiles, 2)),
-            pltpu.SemaphoreType.DMA((slots,)),
+            pltpu.SemaphoreType.DMA((turns,)),
         ],
-        compiler_params=params(32),
+        compiler_params=params(24),
         name="sweeps",
-    )(edges, mesh_before, halo_left, halo_right)
+    )(outgoing_results, edges, field, halo_left, halo_right)
 
     slots_in = receive_vertex.shape[0]
     edge_shape = jax.ShapeDtypeStruct((3 * tiles, LANES), f32)
     interface, first, last = pl.pallas_call(
         lambda *refs: scatter_body(*refs, per=result_per, width=width),
         out_shape=(jax.ShapeDtypeStruct((3, blocks, LANES), f32), edge_shape, edge_shape),
-        in_specs=[VMEM, VMEM],
+        in_specs=[HBM, VMEM, VMEM],
         out_specs=(VMEM, VMEM, VMEM),
         scratch_shapes=[pltpu.VMEM((9 * blocks, slots_in), bf16), pltpu.VMEM((LANES, slots_in), bf16)],
-        compiler_params=params(24),
+        compiler_params=params(16),
         name="scatter",
-    )(returned, receive_vertex.reshape(-1, LANES))
+    )(in_hbm(base), returned, vertices)
 
     from_left = lax.ppermute(last, "dev", up)
     from_right = lax.ppermute(first, "dev", down)
@@ -499,4 +627,5 @@
         P(None, "dev", None, None),
     )
     out_specs = P(None, "dev", None, None)
+
     return jax.shard_map(local, mesh=mesh, in_specs=in_specs, out_specs=out_specs, check_vma=False)

time: 129 us -> 88 us (0.68)
  the two profiles are of different devices: /device:TPU:4 before, /device:TPU:7 now
where the time goes in v2:
time: 88 us; the launch traced here: 87.7 us
  Pallas kernels  41 us (47%)
  blocking collectives  24.7 us (28%)
  starting transfers between devices  17 us (19%)
  waiting for transfers between devices  4.84 us (6%)
    all_to_all x1, blocking collectives, exchange(): lax.all_to_all(packed, 'dev', split_axis=0, concat_axis=0, tiled=True)  24.7 us
    pallas_call x1, Pallas kernels, local(): pl.pallas_call(lambda *refs: mesh_body(*refs, batch=batch), out_shape=jax...  17.9 us
    pallas_call x1, Pallas kernels, local(): pl.pallas_call(lambda *refs: result_body(*refs, per_in=send_per, per_out=...  8.59 us
    pallas_call x1, Pallas kernels, local(): pl.pallas_call(prepare_body, out_shape=(pair, pair) + tuple((pltpu.VMEM(x...  6.11 us
    all_to_all x1, starting transfers between devices, exchange(): lax.all_to_all(packed, 'dev', split_axis=0, concat_axis=0, tiled=True)  6.07 us
    ppermute x1, waiting for transfers between devices, local(): from_right = lax.ppermute(first, 'dev', down)  4.83 us
    pallas_call x1, Pallas kernels, local(): pl.pallas_call(lambda *refs: scatter_body(*refs, per=result_per, width=wi...  3.7 us
    ppermute x1, starting transfers between devices, local(): halo_left = lax.ppermute(tail, 'dev', up)  3.68 us
  transfers between devices with their start and end apart: 5, of which 1 were waited for; matrix products, arithmetic and copies ran while one was open for 0% of the time, Pallas kernels for 32%

profile of v2, /device:TPU:7, one launch (start us, length us, event | category | flops | bytes accessed | tf_op | source)
XLA Modules:
  0.0 87.7 jit_solution(17587220725081729611)
XLA Ops:
  0.0 0.0 copy-start
  0.0 0.0 copy-start.1
  0.0 6.1 %prepare.1 = (bf16[2,1024,1024]{2,1,0:T(8,128)(2,1)}, bf16[2,1024,1024]{2,1,0:T(8,128)(2,1)}, s32[4,1024]{1,0:T(4,128)S(1)}, f32[4,1024]{1,0:T(4,128)S(1)}, s32[...) custom-call(f32[3,4,1024]{2,1,0:T(4,128)} %bitcast.8, ...), custom_call_target="tpu_custom_call" | custom-call | tf_op jit(solution)/shard_map/prepare/pallas_call | solution.py:528
  6.1 3.7 %collective-permute-start = (f32[3,2,96,512]{3,2,1,0:T(8,128)}, f32[3,2,96,512]{3,2,1,0:T(8,128)S(1)}, u32[]{:S(2)}, u32[]{:S(2)}) collective-permute-start(f32[3,2,96,512]{3,2,1,0:T(8,128)} %get-tuple-element.25), channel_id=1, source_target_pairs={{0,1},{1,2},{2,3},{3,4},{4,5},{5,6},{6,7},{7,8},{8,9},{9,10},{10,1... | collective-permute-start | bytes 3538952 | tf_op jit(solution)/shard_map/ppermute | solution.py:546
  9.8 1.9 %collective-permute-start.1 = (f32[3,2,96,512]{3,2,1,0:T(8,128)}, f32[3,2,96,512]{3,2,1,0:T(8,128)S(1)}, u32[]{:S(2)}, u32[]{:S(2)}) collective-permute-start(f32[3,2,96,512]{3,2,1,0:T(8,128)} %get-tuple-element.26), channel_id=1, source_target_pairs={{1,0},{2,1},{3,2},{4,3},{5,4},{6,5},{7,6},{8,7},{9,8},{10,9},{11,1... | collective-permute-start | bytes 3538952 | tf_op jit(solution)/shard_map/ppermute | solution.py:547
  11.7 0.0 copy-done
  11.7 0.0 copy-done.1
  11.8 1.7 %pick_nodes.1 = f32[32,6,128]{2,1,0:T(8,128)S(1)} custom-call(f32[3,4096]{1,0:T(4,128)S(1)} %copy-done, s32[64,128]{1,0:T(8,128)S(1)} %bitcast.7), custom_call_target="tpu_custom_call" | custom-call | tf_op jit(solution)/shard_map/pick_nodes/pallas_call | solution.py:511
  13.4 24.7 %all_to_all.10.refs_0_ = f32[32,6,128]{2,1,0:T(8,128)S(1)} all-to-all(f32[32,6,128]{2,1,0:T(8,128)S(1)} %pick_nodes.1), channel_id=1, replica_groups=mesh['dev'=32] {'dev'}, dimensions={0} | all-to-all | bytes 196608 | tf_op jit(solution)/shard_map/all_to_all | solution.py:472
  38.1 8.6 %cluster_results.1.refs_0_ = f32[32,6,128]{2,1,0:T(8,128)} custom-call(f32[32,6,128]{2,1,0:T(8,128)S(1)} %all_to_all.10.refs_0_, s32[4,1024]{1,0:T(4,128)S(1)} %get-tuple-element.18.refs_1_, f32[3,4,1024]{2,1,0:T(4,128)S(1)} %get-tuple-element.19.refs_2_, f32[3,4,1024]{2,1,0:T(4,128)S(1)} %get-tuple-element.20.refs_3_, bf16[4,1024,1024]{2,1,0:T(8,128)(2,1)} %refs_4_.1, ...), custom_call_target="tpu_custom_call" | custom-call | tf_op jit(solution)/shard_map/cluster_results/pallas_call | solution.py:549
  46.7 6.1 %all-to-all-start.1 = ((f32[32,6,128]{2,1,0:T(8,128)}), f32[32,6,128]{2,1,0:T(8,128)S(1)}, u32[]{:S(2)}, u32[]{:S(2)}) async-start(f32[32,6,128]{2,1,0:T(8,128)} %cluster_results.1.refs_0_), calls=%async_computation.1 | async-start | bytes 262144 | tf_op jit(solution)/shard_map/all_to_all | solution.py:472
  52.8 0.1 pad_add_fusion.refs_1_
  52.9 0.0 collective-permute-done.refs_3_
  52.9 0.0 collective-permute-done.1.refs_4_
  52.9 17.9 %sweeps.1.refs_0_.base_ref = f32[3,16,96,512]{3,2,1,0:T(8,128)} custom-call(f32[32,6,128]{2,1,0:T(8,128)} %cluster_results.1.refs_0_, s32[2]{0:T(128)S(1)} %pad_add_fusion.refs_1_, f32[3,16,96,512]{3,2,1,0:T(8,128)} %refs_2_.1, f32[3,2,96,512]{3,2,1,0:T(8,128)S(1)} %collective-permute-done.refs_3_, f32[3,2,96,512]{3,2,1,0:T(8,128)S(1)} %collective-permute-done.1.refs_4_), custom_call_target="tpu_custom_call" | custom-call | tf_op jit(solution)/shard_map/sweeps/pallas_call | solution.py:571
  70.8 0.0 all-to-all-done.1.refs_1_
  70.8 3.7 %scatter.1 = (f32[3,64,128]{2,1,0:T(8,128)S(1)}, f32[12,128]{1,0:T(8,128)S(1)}, f32[12,128]{1,0:T(8,128)S(1)}) custom-call(f32[3,16,96,512]{3,2,1,0:T(8,128)} %sweeps.1.refs_0_.base_ref, f32[32,6,128]{2,1,0:T(8,128)S(1)} %all-to-all-done.1.refs_1_, s32[64,128]{1,0:T(8,128)S(1)} %get-tuple-element.27.refs_2_), custom_call_target="tpu_custom_call" | custom-call | tf_op jit(solution)/shard_map/scatter/pallas_call | solution.py:590
  74.5 3.4 %collective-permute-start.2 = (f32[12,128]{1,0:T(8,128)S(1)}, f32[12,128]{1,0:T(8,128)S(1)}, u32[]{:S(2)}, u32[]{:S(2)}) collective-permute-start(f32[12,128]{1,0:T(8,128)S(1)} %get-tuple-element.29), channel_id=1, source_target_pairs={{0,1},{1,2},{2,3},{3,4},{4,5},{5,6},{6,7},{7,8},{8,9},{9,10},{10,1... | collective-permute-start | bytes 18440 | tf_op jit(solution)/shard_map/ppermute | solution.py:600
  77.9 1.9 %collective-permute-start.3 = (f32[12,128]{1,0:T(8,128)S(1)}, f32[12,128]{1,0:T(8,128)S(1)}, u32[]{:S(2)}, u32[]{:S(2)}) collective-permute-start(f32[12,128]{1,0:T(8,128)S(1)} %get-tuple-element.30), channel_id=1, source_target_pairs={{1,0},{2,1},{3,2},{4,3},{5,4},{6,5},{7,6},{8,7},{9,8},{10,9},{11,1... | collective-permute-start | bytes 18440 | tf_op jit(solution)/shard_map/ppermute | solution.py:601
  79.8 0.0 collective-permute-done.2.left_ref
  79.9 4.8 %collective-permute-done.3.right_ref = f32[12,128]{1,0:T(8,128)S(1)} collective-permute-done((f32[12,128]{1,0:T(8,128)S(1)}, f32[12,128]{1,0:T(8,128)S(1)}, u32[]{:S(2)}, u32[]{:S(2)}) %collective-permute-start.3) | collective-permute-done | bytes 6176 | tf_op jit(solution)/shard_map/ppermute | solution.py:601
  84.7 3.0 %finish.1 = f32[3,16,96,512]{3,2,1,0:T(8,128)} custom-call(f32[3,16,96,512]{3,2,1,0:T(8,128)} %sweeps.1.refs_0_.base_ref, f32[3,64,128]{2,1,0:T(8,128)S(1)} %get-tuple-element.28.inter_ref, f32[12,128]{1,0:T(8,128)S(1)} %collective-permute-done.2.left_ref, f32[12,128]{1,0:T(8,128)S(1)} %collective-permute-done.3.right_ref), custom_call_target="tpu_custom_call", output_to_operand_aliasing={{}: (0, {})} | custom-call | tf_op jit(solution)/shard_map/finish/pallas_call | solution.py:604
Async XLA Ops:
  0.0 11.7 %copy-start = (f32[3,4096]{1,0:T(4,128)S(1)}, f32[3,4096]{1,0:T(4,128)}, u32[]{:S(2)}) copy-start(f32[3,4096]{1,0:T(4,128)} %refs_0_.1) | copy-start | bytes 147460
  0.0 11.7 %copy-start.1 = (s32[8192]{0:T(1024)S(1)}, s32[8192]{0:T(1024)}, u32[]{:S(2)}) copy-start(s32[8192]{0:T(1024)} %param.11) | copy-start | bytes 98308
  6.1 46.8 %collective-permute-start = (f32[3,2,96,512]{3,2,1,0:T(8,128)}, f32[3,2,96,512]{3,2,1,0:T(8,128)S(1)}, u32[]{:S(2)}, u32[]{:S(2)}) collective-permute-start(f32[3,2,96,512]{3,2,1,0:T(8,128)} %get-tuple-element.25), channel_id=1, source_target_pairs={{0,1},{1,2},{2,3},{3,4},{4,5},{5,6},{6,7},{7,8},{8,9},{9,10},{10,1... | collective-permute-start | bytes 3538952 | tf_op jit(solution)/shard_map/ppermute | solution.py:546
  9.8 43.1 %collective-permute-start.1 = (f32[3,2,96,512]{3,2,1,0:T(8,128)}, f32[3,2,96,512]{3,2,1,0:T(8,128)S(1)}, u32[]{:S(2)}, u32[]{:S(2)}) collective-permute-start(f32[3,2,96,512]{3,2,1,0:T(8,128)} %get-tuple-element.26), channel_id=1, source_target_pairs={{1,0},{2,1},{3,2},{4,3},{5,4},{6,5},{7,6},{8,7},{9,8},{10,9},{11,1... | collective-permute-start | bytes 3538952 | tf_op jit(solution)/shard_map/ppermute | solution.py:547
  46.7 24.1 %all-to-all-start.1 = ((f32[32,6,128]{2,1,0:T(8,128)}), f32[32,6,128]{2,1,0:T(8,128)S(1)}, u32[]{:S(2)}, u32[]{:S(2)}) async-start(f32[32,6,128]{2,1,0:T(8,128)} %cluster_results.1.refs_0_), calls=%async_computation.1 | async-start | bytes 262144 | tf_op jit(solution)/shard_map/all_to_all | solution.py:472
  74.5 5.3 %collective-permute-start.2 = (f32[12,128]{1,0:T(8,128)S(1)}, f32[12,128]{1,0:T(8,128)S(1)}, u32[]{:S(2)}, u32[]{:S(2)}) collective-permute-start(f32[12,128]{1,0:T(8,128)S(1)} %get-tuple-element.29), channel_id=1, source_target_pairs={{0,1},{1,2},{2,3},{3,4},{4,5},{5,6},{6,7},{7,8},{8,9},{9,10},{10,1... | collective-permute-start | bytes 18440 | tf_op jit(solution)/shard_map/ppermute | solution.py:600
  77.9 6.8 %collective-permute-start.3 = (f32[12,128]{1,0:T(8,128)S(1)}, f32[12,128]{1,0:T(8,128)S(1)}, u32[]{:S(2)}, u32[]{:S(2)}) collective-permute-start(f32[12,128]{1,0:T(8,128)S(1)} %get-tuple-element.30), channel_id=1, source_target_pairs={{1,0},{2,1},{3,2},{4,3},{5,4},{6,5},{7,6},{8,7},{9,8},{10,9},{11,1... | collective-permute-start | bytes 18440 | tf_op jit(solution)/shard_map/ppermute | solution.py:601

commit v3 on v2

--- a/solution.py
+++ b/solution.py
@@ -10,6 +10,8 @@
 
 LANES = 128
 SUB = 8
+TALL = 16
+WIDE = 256
 share = 0.8 / 6.0
 keep = 0.2 / share
 sharpness = 8.0
@@ -70,7 +72,24 @@
     return ref[k, row : row + 1, :]
 
 
-def pick_body(table_ref, index_ref, out_ref, *, per):
+def pick_body(table_hbm, index_hbm, mesh_ref, out_ref, head_out, tail_out, table_ref, index_ref, head, tail, sems, *, per):
+    width = mesh_ref.shape[1]
+    needed = [
+        pltpu.make_async_copy(index_hbm, index_ref, sems.at[0]),
+        pltpu.make_async_copy(table_hbm, table_ref, sems.at[1]),
+    ]
+    side_in = [
+        pltpu.make_async_copy(mesh_ref.at[:, pl.ds(0, 2)], head, sems.at[2]),
+        pltpu.make_async_copy(mesh_ref.at[:, pl.ds(width - 2, 2)], tail, sems.at[3]),
+    ]
+    side_out = [
+        pltpu.make_async_copy(head, head_out, sems.at[4]),
+        pltpu.make_async_copy(tail, tail_out, sems.at[5]),
+    ]
+    for copy in needed + side_in:
+        copy.start()
+    for copy in needed:
+        copy.wait()
     groups = index_ref.shape[0] // SUB
     blocks = table_ref.shape[1] // LANES
     half = max(1, groups // 2)
@@ -83,6 +102,12 @@
         )
         for g in range(half):
             store_rows(out_ref, first + g, got[g], per)
+        if first == 0:
+            for before, after in zip(side_in, side_out):
+                before.wait()
+                after.start()
+    for copy in side_out:
+        copy.wait()
 
 
 def pieces(value, count=3):
@@ -128,30 +153,20 @@
 
 
 def prepare_body(
-    source_ref, target_ref, slot_ref, weight_ref, pick_ref, vertex_ref, mesh_ref,
-    high_out, low_out, slot_out, weight_out, pick_out, vertex_out, source, target, head_out, tail_out,
-    high, low, head, tail, sems, done,
+    source_ref, target_ref, slot_ref, weight_ref, pick_ref, vertex_ref,
+    high_out, low_out, slot_out, weight_out, pick_out, vertex_out, source, target, high, low, sems, done,
 ):
-    width = mesh_ref.shape[1]
     needed = [
         pltpu.make_async_copy(source_ref, source, sems.at[0]),
         pltpu.make_async_copy(target_ref, target, sems.at[1]),
     ]
     others = [
-        pltpu.make_async_copy(slot_ref, slot_out, sems.at[4]),
-        pltpu.make_async_copy(weight_ref, weight_out, sems.at[5]),
-        pltpu.make_async_copy(pick_ref, pick_out, sems.at[6]),
-        pltpu.make_async_copy(vertex_ref, vertex_out, sems.at[7]),
+        pltpu.make_async_copy(slot_ref, slot_out, sems.at[2]),
+        pltpu.make_async_copy(weight_ref, weight_out, sems.at[3]),
+        pltpu.make_async_copy(pick_ref, pick_out, sems.at[4]),
+        pltpu.make_async_copy(vertex_ref, vertex_out, sems.at[5]),
     ]
-    side_in = [
-        pltpu.make_async_copy(mesh_ref.at[:, pl.ds(0, 2)], head, sems.at[2]),
-        pltpu.make_async_copy(mesh_ref.at[:, pl.ds(width - 2, 2)], tail, sems.at[3]),
-    ]
-    side_out = [
-        pltpu.make_async_copy(head, head_out, sems.at[8]),
-        pltpu.make_async_copy(tail, tail_out, sems.at[9]),
-    ]
-    for copy in needed + side_in + others:
+    for copy in needed + others:
         copy.start()
     for copy in needed:
         copy.wait()
@@ -167,11 +182,7 @@
         last.append(pltpu.make_async_copy(low.at[c], low_out.at[c], done.at[1, c]))
         for copy in last[-2:]:
             copy.start()
-        if c == 0:
-            for before, after in zip(side_in, side_out):
-                before.wait()
-                after.start()
-    for copy in others + last + side_out:
+    for copy in others + last:
         copy.wait()
 
 
@@ -251,11 +262,13 @@
             store_rows(out_ref, start + g, got[g], per_out)
 
 
-def mesh_body(_, edge_ref, mesh_ref, left_ref, right_ref, out_ref, field, ring, stage, in_sems, side_sems, out_sems, *, batch):
+def mesh_body(_, edge_ref, mesh_ref, left_ref, right_ref, out_ref, field, ring, stage, in_sems, side_sems, out_sems, sums, *, batch):
     comps, width, height, depth = mesh_ref.shape
     tiles = depth // LANES
-    strips = height // SUB
-    slots = len(stage)
+    strips = height // TALL
+    share_tiles = WIDE // LANES
+    units = len(sums)
+    halves = depth // WIDE // units
     turns = len(ring)
 
     def columns(j):
@@ -305,102 +318,122 @@
 
     lax.fori_loop(0, comps * (width + 4), clear, 0)
 
-    lane = lax.broadcasted_iota(jnp.int32, (SUB, LANES), 1)
-    row = lax.broadcasted_iota(jnp.int32, (SUB, LANES), 0)
+    lane = lax.broadcasted_iota(jnp.int32, (TALL, LANES), 1)
+    row = lax.broadcasted_iota(jnp.int32, (TALL, LANES), 0)
     is_first = lane == 0
     is_last = lane == LANES - 1
-    wall = row == 0
-
-    def sweep_strip(y, center, before, after, put):
-        at = SUB + y * SUB
-        mid = [center[j, pl.ds(at, SUB), :] for j in range(tiles)]
-        down = [pltpu.roll(m, 1, 1) for m in mid]
-        up = [pltpu.roll(m, LANES - 1, 1) for m in mid]
+
+    def terms(center, y, h):
+        value = jnp.concatenate(
+            [center[j, pl.ds(SUB + y * TALL, TALL), :] for j in range(h * share_tiles, (h + 1) * share_tiles)], axis=1
+        )
+        high = value.astype(bf16)
+        return high, (value - high.astype(f32)).astype(bf16)
+
+    def multiply(jobs):
+        later = []
+        for center, y, place in jobs:
+            for h in range(depth // WIDE):
+                high, low = terms(center, y, h)
+                total = sums[h % units][place * halves + h // units]
+                pltpu.matmul_acc_lhs(total, high)
+                later.append((total, low))
+        for total, low in later:
+            pltpu.matmul_acc_lhs(total, low)
+
+    def complete(center, before, after, y, place, put):
+        at = SUB + y * TALL
+        beside = []
+        for h in range(depth // WIDE):
+            beside.append(pltpu.matmul_pop(sums[h % units][place * halves + h // units]))
         for j in range(tiles):
-            lower = center[j, pl.ds(at - 1, SUB), :]
+            lower = center[j, pl.ds(at - 1, TALL), :]
             if y == 0:
                 lower = jnp.where(row < 2, 0.0, lower)
-            near = (before[j, pl.ds(at, SUB), :] + after[j, pl.ds(at, SUB), :]) + (
-                center[j, pl.ds(at + 1, SUB), :] + lower
+            near = (before[j, pl.ds(at, TALL), :] + after[j, pl.ds(at, TALL), :]) + (
+                center[j, pl.ds(at + 1, TALL), :] + lower
             )
-            near = near + keep * mid[j]
-            back = jnp.where(is_first, down[j - 1] if j else 0.0, down[j])
-            fore = jnp.where(is_last, up[j + 1] if j + 1 < tiles else 0.0, up[j])
-            value = near + (back + fore)
+            h, part = j // share_tiles, j % share_tiles
+            value = near + beside[h][:, part * LANES : (part + 1) * LANES]
+            if part == 0 and h:
+                value = value + jnp.where(is_first, pltpu.roll(center[j - 1, pl.ds(at, TALL), :], 1, 1), 0.0)
+            if part == share_tiles - 1 and j + 1 < tiles:
+                value = value + jnp.where(is_last, pltpu.roll(center[j + 1, pl.ds(at, TALL), :], LANES - 1, 1), 0.0)
             if y == 0:
-                value = jnp.where(wall, 0.0, value)
+                value = jnp.where(row == 0, 0.0, value)
             put(j, y, value)
 
+    line = lax.broadcasted_iota(jnp.int32, (WIDE, WIDE), 0)
+    column = lax.broadcasted_iota(jnp.int32, (WIDE, WIDE), 1)
+    apart = jnp.abs(line - column)
+    band = jnp.where(apart == 0, keep, jnp.where(apart == 1, 1.0, 0.0)).astype(bf16)
+    for unit in range(units):
+        first = sums[unit][0]
+        pltpu.matmul_push_rhs(band, 0, unit)
+        pltpu.matmul_acc_lhs(first, jnp.zeros((TALL, WIDE), bf16), load_staged_rhs=0)
+        stage[unit, 0:TALL, 0:WIDE] = pltpu.matmul_pop(first)
+
     def flush(k, x, slot):
-        return pltpu.make_async_copy(stage[slot], out_ref.at[k, x], out_sems.at[slot])
-
-    def work(k, x, phase, second):
+        return pltpu.make_async_copy(stage.at[slot], out_ref.at[k, x], out_sems.at[slot])
+
+    def work(k, x, phase, slot=None, gate=None):
         def put_first(j, y, value):
-            ring[phase % turns][j, pl.ds(SUB + y * SUB, SUB), :] = value
+            if gate is not None:
+                value = value * gate
+            ring[phase % turns][j, pl.ds(SUB + y * TALL, TALL), :] = value
 
         def put_second(j, y, value):
-            stage[phase % slots][y * SUB : (y + 1) * SUB, j * LANES : (j + 1) * LANES] = value * (share * share)
-
-        for y in range(strips):
-            sweep_strip(y, field.at[k, x + 1], field.at[k, x], field.at[k, x + 2], put_first)
-            if second:
-                sweep_strip(
-                    y,
-                    ring[(phase - 2) % turns],
-                    ring[(phase - 3) % turns],
-                    ring[(phase - 1) % turns],
-                    put_second,
-                )
-
-    def zero(place):
-        ring[place % turns][...] = jnp.zeros(ring[0].shape, f32)
+            stage[slot, y * TALL : (y + 1) * TALL, j * LANES : (j + 1) * LANES] = value * (share * share)
+
+        jobs = [(field.at[k, x + 1], field.at[k, x], field.at[k, x + 2], put_first)]
+        if slot is not None:
+            jobs.append((ring[(phase - 2) % turns], ring[(phase - 3) % turns], ring[(phase - 1) % turns], put_second))
+        group = 3
+        for y in range(0, strips + group, group):
+            spot = y // group % 2 * 2 * group
+            if y < strips:
+                multiply([(job[0], y + n, spot + n * 2 + i) for n in range(group) for i, job in enumerate(jobs)])
+            if y >= group:
+                for n in range(group):
+                    for i, (center, before, after, put) in enumerate(jobs):
+                        complete(center, before, after, y - group + n, 2 * group - spot + n * 2 + i, put)
 
     def component(k, _):
         for copy in sides(k):
             copy.wait()
         for copy in load(k, 0):
             copy.wait()
+        first_gate = jnp.where(edge_ref[0] == 0, 0.0, 1.0)
         for phase in range(3):
-            work(k, phase, phase, False)
-            if phase == 0:
-
-                @pl.when(edge_ref[0] == 0)
-                def _():
-                    zero(0)
+            work(k, phase, phase, None, first_gate if phase == 0 else None)
 
         def quad(i, _):
+            @pl.when((i + 1) * turns < width)
+            def _():
+                for copy in load(k, i + 1):
+                    copy.wait()
+
+            turn = k * (width // turns) + i
+            slots = (turn % 2) * turns
+
+            @pl.when(turn >= 2)
+            def _():
+                for sub in range(turns):
+                    flush(k, 0, slots + sub).wait()
+
+            last_gate = jnp.where(jnp.logical_and((i + 1) * turns == width, edge_ref[1] == 0), 0.0, 1.0)
             for sub in range(turns):
-                x = i * turns + sub + 3
-                phase = sub + 3
-
-                if phase % batch == 0:
-
-                    @pl.when(x < width)
-                    def _():
-                        for copy in load(k, x // batch):
-                            copy.wait()
-
-                slot = phase % slots
-
-                @pl.when(k * width + i * turns + sub >= slots)
-                def _():
-                    flush(k, 0, slot).wait()
-
-                work(k, jnp.minimum(x, width + 1), phase, True)
-                if sub == turns - 2:
-
-                    @pl.when(jnp.logical_and(x == width + 1, edge_ref[1] == 0))
-                    def _():
-                        zero(phase)
-
-                flush(k, i * turns + sub, slot).start()
+                x = jnp.minimum(i * turns + sub + 3, width + 1)
+                work(k, x, sub + 3, slots + sub, last_gate if sub == turns - 2 else None)
+            for sub in range(turns):
+                flush(k, i * turns + sub, slots + sub).start()
             return 0
 
         lax.fori_loop(0, width // turns, quad, 0)
         return 0
 
     lax.fori_loop(0, comps, component, 0)
-    for slot in range(slots):
+    for slot in range(2 * turns):
         flush(0, 0, slot).wait()
 
 
@@ -508,43 +541,48 @@
     down = [(i + 1, i) for i in range(count - 1)]
 
     field = in_hbm(mesh_before)
-    outgoing = pl.pallas_call(
+    side = (comps, 2, height, depth)
+    node_rows = send_node.reshape(-1, LANES)
+    outgoing, head, tail = pl.pallas_call(
         lambda *refs: pick_body(*refs, per=send_per),
-        out_shape=packed_shape(send_per, send_node.shape[0]),
-        in_specs=[VMEM, VMEM],
-        out_specs=VMEM,
-        compiler_params=params(2),
+        out_shape=(packed_shape(send_per, send_node.shape[0]), pltpu.HBM(side, f32), pltpu.HBM(side, f32)),
+        in_specs=[HBM] * 3,
+        out_specs=(VMEM, HBM, HBM),
+        scratch_shapes=[
+            pltpu.VMEM(displacement.shape, f32),
+            pltpu.VMEM(node_rows.shape, jnp.int32),
+            pltpu.VMEM(side, f32),
+            pltpu.VMEM(side, f32),
+            pltpu.SemaphoreType.DMA((6,)),
+        ],
+        compiler_params=params(6),
         name="pick_nodes",
-    )(displacement, send_node.reshape(-1, LANES))
+    )(in_hbm(displacement), in_hbm(node_rows), field)
     arrived = exchange(outgoing, send_per, send_cap)
+    halo_left = lax.ppermute(tail, "dev", up)
+    halo_right = lax.ppermute(head, "dev", down)
 
     pair = jax.ShapeDtypeStruct((clusters, points, verts), bf16)
     ahead = min(clusters, AHEAD)
     pair = pltpu.HBM((ahead, points, verts), bf16)
-    side = pltpu.HBM((comps, 2, height, depth), f32)
     source_turned = jnp.transpose(source_coord, (1, 0, 2))
     target_turned = jnp.transpose(target_coord, (1, 0, 2))
     small = (member_slot, unity_weight, result_pick.reshape(-1, LANES), receive_vertex.reshape(-1, LANES))
-    (kernel_high, kernel_low, slots, weight, picks, vertices, source, target, head, tail) = pl.pallas_call(
+    (kernel_high, kernel_low, slots, weight, picks, vertices, source, target) = pl.pallas_call(
         prepare_body,
         out_shape=(pair, pair)
-        + tuple(pltpu.VMEM(x.shape, x.dtype) for x in small + (source_turned, target_turned))
-        + (side, side),
-        in_specs=[HBM] * 7,
-        out_specs=(HBM,) * 2 + (VMEM,) * 6 + (HBM,) * 2,
+        + tuple(pltpu.VMEM(x.shape, x.dtype) for x in small + (source_turned, target_turned)),
+        in_specs=[HBM] * 6,
+        out_specs=(HBM,) * 2 + (VMEM,) * 6,
         scratch_shapes=[
             pltpu.VMEM((ahead, points, verts), bf16),
             pltpu.VMEM((ahead, points, verts), bf16),
-            pltpu.VMEM((comps, 2, height, depth), f32),
-            pltpu.VMEM((comps, 2, height, depth), f32),
-            pltpu.SemaphoreType.DMA((10,)),
+            pltpu.SemaphoreType.DMA((6,)),
             pltpu.SemaphoreType.DMA((2, ahead)),
         ],
         compiler_params=params(28),
         name="prepare",
-    )(*map(in_hbm, (source_turned, target_turned) + small), field)
-    halo_left = lax.ppermute(tail, "dev", up)
-    halo_right = lax.ppermute(head, "dev", down)
+    )(*map(in_hbm, (source_turned, target_turned) + small))
 
     outgoing_results = pl.pallas_call(
         lambda *refs: result_body(*refs, per_in=send_per, per_out=result_per, ahead=ahead),
@@ -566,20 +604,26 @@
 
     edges = jnp.stack([place, count - 1 - place]).astype(jnp.int32)
     batch = turns = 4
-    if width % turns:
-        raise ValueError("width")
+    if width % turns or depth % (2 * WIDE) or height % TALL:
+        raise ValueError("mesh shape")
+
+    def with_sums(*refs):
+        places = 12 * (depth // WIDE // 2)
+        sums = tuple(tuple(pltpu.ACC(unit)((TALL, WIDE), f32) for _ in range(places)) for unit in range(2))
+        pl.run_scoped(lambda *sums: mesh_body(*refs, sums, batch=batch), *sums)
+
     base = pl.pallas_call(
-        lambda *refs: mesh_body(*refs, batch=batch),
+        with_sums,
         out_shape=jax.ShapeDtypeStruct(mesh_before.shape, f32),
         in_specs=[ANY, SMEM, HBM, ANY, ANY],
         out_specs=HBM,
         scratch_shapes=[
             pltpu.VMEM((comps, width + 4, tiles, height + 2 * SUB, LANES), f32),
             tuple(pltpu.VMEM((tiles, height + 2 * SUB, LANES), f32) for _ in range(turns)),
-            tuple(pltpu.VMEM((height, depth), f32) for _ in range(turns)),
+            pltpu.VMEM((2 * turns, height, depth), f32),
             pltpu.SemaphoreType.DMA((comps, width // batch, tiles)),
             pltpu.SemaphoreType.DMA((comps, tiles, 2)),
-            pltpu.SemaphoreType.DMA((turns,)),
+            pltpu.SemaphoreType.DMA((2 * turns,)),
         ],
         compiler_params=params(24),
         name="sweeps",

time: 88 us -> 83.3 us (0.947)
  blocking collectives: 24.7 us -> 0 us
  waiting for transfers between devices: 4.84 us -> 19.5 us
  starting transfers between devices: 17 us -> 23.3 us
  Pallas kernels: 41 us -> 39.9 us
    all_to_all x1 -> x0, blocking collectives: 24.7 us -> none  [exchange(): lax.all_to_all(packed, 'dev', split_axis=0, concat_axis=0, tiled=True)]
    all_to_all x1 -> x2, waiting for transfers between devices: 0.01 us -> 14.6 us  [exchange(): lax.all_to_all(packed, 'dev', split_axis=0, concat_axis=0, tiled=True)]
    all_to_all x1 -> x2, starting transfers between devices: 6.07 us -> 12.4 us  [exchange(): lax.all_to_all(packed, 'dev', split_axis=0, concat_axis=0, tiled=True)]
  transfers between devices with their start and end apart: 5 -> 6, of which waited for: 1 -> 2; matrix products, arithmetic and copies ran while one was open for 0% -> 0% of each run, Pallas kernels for 32% -> 35%
where the time goes in v3:
time: 83.3 us; the launch traced here: 82.9 us
  Pallas kernels  39.9 us (48%)
  starting transfers between devices  23.3 us (28%)
  waiting for transfers between devices  19.5 us (23%)
    pallas_call x1, Pallas kernels, local(): pl.pallas_call(with_sums, out_shape=jax.ShapeDtypeStruct(mesh_before.shap...  15.3 us
    all_to_all x2, waiting for transfers between devices, exchange(): lax.all_to_all(packed, 'dev', split_axis=0, concat_axis=0, tiled=True)  14.6 us
    all_to_all x2, starting transfers between devices, exchange(): lax.all_to_all(packed, 'dev', split_axis=0, concat_axis=0, tiled=True)  12.4 us
    pallas_call x1, Pallas kernels, local(): pl.pallas_call(lambda *refs: result_body(*refs, per_in=send_per, per_out=...  8.6 us
    pallas_call x1, Pallas kernels, local(): pl.pallas_call(prepare_body, out_shape=(pair, pair) + tuple((pltpu.VMEM(x...  5.41 us
    ppermute x1, waiting for transfers between devices, local(): from_right = lax.ppermute(first, 'dev', down)  4.83 us
    pallas_call x1, Pallas kernels, local(): pl.pallas_call(lambda *refs: pick_body(*refs, per=send_per), out_shape=(p...  3.88 us
    pallas_call x1, Pallas kernels, local(): pl.pallas_call(lambda *refs: scatter_body(*refs, per=result_per, width=wi...  3.7 us
  transfers between devices with their start and end apart: 6, of which 2 were waited for; matrix products, arithmetic and copies ran while one was open for 0% of the time, Pallas kernels for 35%

profile of v3, /device:TPU:7, one launch (start us, length us, event | category | flops | bytes accessed | tf_op | source)
XLA Modules:
  0.0 82.9 jit_solution(18243451702720001207)
XLA Ops:
  0.0 3.9 %pick_nodes.1 = (f32[32,6,128]{2,1,0:T(8,128)}, f32[3,2,96,512]{3,2,1,0:T(8,128)}, f32[3,2,96,512]{3,2,1,0:T(8,128)}) custom-call(f32[3,4096]{1,0:T(4,128)} %refs_0_.1, s32[64,128]{1,0:T(8,128)} %bitcast.9, f32[3,16,96,512]{3,2,1,0:T(8,128)} %refs_2_.3), custom_call_target="tpu_custom_call" | custom-call | tf_op jit(solution)/shard_map/pick_nodes/pallas_call | solution.py:546
  3.9 3.7 %collective-permute-start = (f32[3,2,96,512]{3,2,1,0:T(8,128)}, f32[3,2,96,512]{3,2,1,0:T(8,128)S(1)}, u32[]{:S(2)}, u32[]{:S(2)}) collective-permute-start(f32[3,2,96,512]{3,2,1,0:T(8,128)} %get-tuple-element.27), channel_id=1, source_target_pairs={{0,1},{1,2},{2,3},{3,4},{4,5},{5,6},{6,7},{7,8},{8,9},{9,10},{10,1... | collective-permute-start | bytes 3538952 | tf_op jit(solution)/shard_map/ppermute | solution.py:562
  7.6 1.9 %collective-permute-start.1 = (f32[3,2,96,512]{3,2,1,0:T(8,128)}, f32[3,2,96,512]{3,2,1,0:T(8,128)S(1)}, u32[]{:S(2)}, u32[]{:S(2)}) collective-permute-start(f32[3,2,96,512]{3,2,1,0:T(8,128)} %get-tuple-element.28), channel_id=1, source_target_pairs={{1,0},{2,1},{3,2},{4,3},{5,4},{6,5},{7,6},{8,7},{9,8},{10,9},{11,1... | collective-permute-start | bytes 3538952 | tf_op jit(solution)/shard_map/ppermute | solution.py:563
  9.5 6.3 %all-to-all-start = ((f32[32,6,128]{2,1,0:T(8,128)}), f32[32,6,128]{2,1,0:T(8,128)S(1)}, u32[]{:S(2)}, u32[]{:S(2)}) async-start(f32[32,6,128]{2,1,0:T(8,128)} %get-tuple-element.19), calls=%async_computation | async-start | bytes 262144 | tf_op jit(solution)/shard_map/all_to_all | solution.py:505
  15.8 5.4 %prepare.1 = (bf16[2,1024,1024]{2,1,0:T(8,128)(2,1)}, bf16[2,1024,1024]{2,1,0:T(8,128)(2,1)}, s32[4,1024]{1,0:T(4,128)S(1)}, f32[4,1024]{1,0:T(4,128)S(1)}, s32[...) custom-call(f32[3,4,1024]{2,1,0:T(4,128)} %bitcast.7, ...), custom_call_target="tpu_custom_call" | custom-call | tf_op jit(solution)/shard_map/prepare/pallas_call | solution.py:571
  21.3 14.6 %all-to-all-done.refs_0_ = f32[32,6,128]{2,1,0:T(8,128)S(1)} async-done(((f32[32,6,128]{2,1,0:T(8,128)}), f32[32,6,128]{2,1,0:T(8,128)S(1)}, u32[]{:S(2)}, u32[]{:S(2)}) %all-to-all-start) | async-done | bytes 98336 | tf_op jit(solution)/shard_map/all_to_all | solution.py:505
  35.9 8.6 %cluster_results.1.refs_0_ = f32[32,6,128]{2,1,0:T(8,128)} custom-call(f32[32,6,128]{2,1,0:T(8,128)S(1)} %all-to-all-done.refs_0_, s32[4,1024]{1,0:T(4,128)S(1)} %get-tuple-element.20.refs_1_, f32[3,4,1024]{2,1,0:T(4,128)S(1)} %get-tuple-element.21.refs_2_, f32[3,4,1024]{2,1,0:T(4,128)S(1)} %get-tuple-element.22.refs_3_, bf16[4,1024,1024]{2,1,0:T(8,128)(2,1)} %refs_4_.1, ...), custom_call_target="tpu_custom_call" | custom-call | tf_op jit(solution)/shard_map/cluster_results/pallas_call | solution.py:587
  44.5 6.1 %all-to-all-start.1 = ((f32[32,6,128]{2,1,0:T(8,128)}), f32[32,6,128]{2,1,0:T(8,128)S(1)}, u32[]{:S(2)}, u32[]{:S(2)}) async-start(f32[32,6,128]{2,1,0:T(8,128)} %cluster_results.1.refs_0_), calls=%async_computation.1 | async-start | bytes 262144 | tf_op jit(solution)/shard_map/all_to_all | solution.py:505
  50.6 0.1 pad_add_fusion.refs_1_
  50.7 0.0 collective-permute-done.refs_3_
  50.7 0.0 collective-permute-done.1.refs_4_
  50.7 15.3 %sweeps.1.refs_0_.base_ref = f32[3,16,96,512]{3,2,1,0:T(8,128)} custom-call(f32[32,6,128]{2,1,0:T(8,128)} %cluster_results.1.refs_0_, s32[2]{0:T(128)S(1)} %pad_add_fusion.refs_1_, f32[3,16,96,512]{3,2,1,0:T(8,128)} %refs_2_.3, f32[3,2,96,512]{3,2,1,0:T(8,128)S(1)} %collective-permute-done.refs_3_, f32[3,2,96,512]{3,2,1,0:T(8,128)S(1)} %collective-permute-done.1.refs_4_), custom_call_target="tpu_custom_call" | custom-call | tf_op jit(solution)/shard_map/sweeps/pallas_call | solution.py:615
  66.0 0.0 all-to-all-done.1.refs_1_
  66.0 3.7 %scatter.1 = (f32[3,64,128]{2,1,0:T(8,128)S(1)}, f32[12,128]{1,0:T(8,128)S(1)}, f32[12,128]{1,0:T(8,128)S(1)}) custom-call(f32[3,16,96,512]{3,2,1,0:T(8,128)} %sweeps.1.refs_0_.base_ref, f32[32,6,128]{2,1,0:T(8,128)S(1)} %all-to-all-done.1.refs_1_, s32[64,128]{1,0:T(8,128)S(1)} %get-tuple-element.29.refs_2_), custom_call_target="tpu_custom_call" | custom-call | tf_op jit(solution)/shard_map/scatter/pallas_call | solution.py:634
  69.7 3.4 %collective-permute-start.2 = (f32[12,128]{1,0:T(8,128)S(1)}, f32[12,128]{1,0:T(8,128)S(1)}, u32[]{:S(2)}, u32[]{:S(2)}) collective-permute-start(f32[12,128]{1,0:T(8,128)S(1)} %get-tuple-element.31), channel_id=1, source_target_pairs={{0,1},{1,2},{2,3},{3,4},{4,5},{5,6},{6,7},{7,8},{8,9},{9,10},{10,1... | collective-permute-start | bytes 18440 | tf_op jit(solution)/shard_map/ppermute | solution.py:644
  73.1 1.9 %collective-permute-start.3 = (f32[12,128]{1,0:T(8,128)S(1)}, f32[12,128]{1,0:T(8,128)S(1)}, u32[]{:S(2)}, u32[]{:S(2)}) collective-permute-start(f32[12,128]{1,0:T(8,128)S(1)} %get-tuple-element.32), channel_id=1, source_target_pairs={{1,0},{2,1},{3,2},{4,3},{5,4},{6,5},{7,6},{8,7},{9,8},{10,9},{11,1... | collective-permute-start | bytes 18440 | tf_op jit(solution)/shard_map/ppermute | solution.py:645
  75.0 0.0 collective-permute-done.2.left_ref
  75.0 4.8 %collective-permute-done.3.right_ref = f32[12,128]{1,0:T(8,128)S(1)} collective-permute-done((f32[12,128]{1,0:T(8,128)S(1)}, f32[12,128]{1,0:T(8,128)S(1)}, u32[]{:S(2)}, u32[]{:S(2)}) %collective-permute-start.3) | collective-permute-done | bytes 6176 | tf_op jit(solution)/shard_map/ppermute | solution.py:645
  79.9 3.0 %finish.1 = f32[3,16,96,512]{3,2,1,0:T(8,128)} custom-call(f32[3,16,96,512]{3,2,1,0:T(8,128)} %sweeps.1.refs_0_.base_ref, f32[3,64,128]{2,1,0:T(8,128)S(1)} %get-tuple-element.30.inter_ref, f32[12,128]{1,0:T(8,128)S(1)} %collective-permute-done.2.left_ref, f32[12,128]{1,0:T(8,128)S(1)} %collective-permute-done.3.right_ref), custom_call_target="tpu_custom_call", output_to_operand_aliasing={{}: (0, {})} | custom-call | tf_op jit(solution)/shard_map/finish/pallas_call | solution.py:648
Async XLA Ops:
  3.9 46.8 %collective-permute-start = (f32[3,2,96,512]{3,2,1,0:T(8,128)}, f32[3,2,96,512]{3,2,1,0:T(8,128)S(1)}, u32[]{:S(2)}, u32[]{:S(2)}) collective-permute-start(f32[3,2,96,512]{3,2,1,0:T(8,128)} %get-tuple-element.27), channel_id=1, source_target_pairs={{0,1},{1,2},{2,3},{3,4},{4,5},{5,6},{6,7},{7,8},{8,9},{9,10},{10,1... | collective-permute-start | bytes 3538952 | tf_op jit(solution)/shard_map/ppermute | solution.py:562
  7.6 43.1 %collective-permute-start.1 = (f32[3,2,96,512]{3,2,1,0:T(8,128)}, f32[3,2,96,512]{3,2,1,0:T(8,128)S(1)}, u32[]{:S(2)}, u32[]{:S(2)}) collective-permute-start(f32[3,2,96,512]{3,2,1,0:T(8,128)} %get-tuple-element.28), channel_id=1, source_target_pairs={{1,0},{2,1},{3,2},{4,3},{5,4},{6,5},{7,6},{8,7},{9,8},{10,9},{11,1... | collective-permute-start | bytes 3538952 | tf_op jit(solution)/shard_map/ppermute | solution.py:563
  9.5 26.4 %all-to-all-start = ((f32[32,6,128]{2,1,0:T(8,128)}), f32[32,6,128]{2,1,0:T(8,128)S(1)}, u32[]{:S(2)}, u32[]{:S(2)}) async-start(f32[32,6,128]{2,1,0:T(8,128)} %get-tuple-element.19), calls=%async_computation | async-start | bytes 262144 | tf_op jit(solution)/shard_map/all_to_all | solution.py:505
  44.5 21.5 %all-to-all-start.1 = ((f32[32,6,128]{2,1,0:T(8,128)}), f32[32,6,128]{2,1,0:T(8,128)S(1)}, u32[]{:S(2)}, u32[]{:S(2)}) async-start(f32[32,6,128]{2,1,0:T(8,128)} %cluster_results.1.refs_0_), calls=%async_computation.1 | async-start | bytes 262144 | tf_op jit(solution)/shard_map/all_to_all | solution.py:505
  69.7 5.3 %collective-permute-start.2 = (f32[12,128]{1,0:T(8,128)S(1)}, f32[12,128]{1,0:T(8,128)S(1)}, u32[]{:S(2)}, u32[]{:S(2)}) collective-permute-start(f32[12,128]{1,0:T(8,128)S(1)} %get-tuple-element.31), channel_id=1, source_target_pairs={{0,1},{1,2},{2,3},{3,4},{4,5},{5,6},{6,7},{7,8},{8,9},{9,10},{10,1... | collective-permute-start | bytes 18440 | tf_op jit(solution)/shard_map/ppermute | solution.py:644
  73.1 6.8 %collective-permute-start.3 = (f32[12,128]{1,0:T(8,128)S(1)}, f32[12,128]{1,0:T(8,128)S(1)}, u32[]{:S(2)}, u32[]{:S(2)}) collective-permute-start(f32[12,128]{1,0:T(8,128)S(1)} %get-tuple-element.32), channel_id=1, source_target_pairs={{1,0},{2,1},{3,2},{4,3},{5,4},{6,5},{7,6},{8,7},{9,8},{10,9},{11,1... | collective-permute-start | bytes 18440 | tf_op jit(solution)/shard_map/ppermute | solution.py:645

commit v4 on v0

v4 whole, which is shorter than its diff:
```python
import math

import jax
import jax.numpy as jnp
from jax import lax
from jax.experimental import pallas as pl
from jax.experimental.pallas import tpu as pltpu
from jax.sharding import PartitionSpec as P


LANES = 128
SUB = 8
TALL = 16
WIDE = 256
share = 0.8 / 6.0
keep = 0.2 / share
sharpness = 8.0
VMEM = pl.BlockSpec(memory_space=pltpu.VMEM)
ANY = pl.BlockSpec(memory_space=pl.ANY)
HBM = pl.BlockSpec(memory_space=pltpu.HBM)
SMEM = pl.BlockSpec(memory_space=pltpu.SMEM)
f32 = jnp.float32
bf16 = jnp.bfloat16


def in_hbm(value):
    return pltpu.with_memory_space_constraint(value, pltpu.HBM)


def params(limit, **more):
    return pltpu.CompilerParams(vmem_limit_bytes=limit << 20, **more)


def lane_gather(row, lane):
    return jnp.take_along_axis(row, lane, axis=1, mode="promise_in_bounds")


def gather_rows(row_of, blocks, index_of, groups):
    index = [index_of(g) for g in range(groups)]
    high = [lax.shift_right_arithmetic(i, 7) for i in index]
    low = [jnp.bitwise_and(i, LANES - 1) for i in index]
    out = [[jnp.zeros((SUB, LANES), f32) for _ in range(3)] for _ in range(groups)]
    for block in range(blocks):
        rows = [jnp.broadcast_to(row_of(k, block), (SUB, LANES)) for k in range(3)]
        for g in range(groups):
            here = high[g] == block
            for k in range(3):
                out[g][k] = jnp.where(here, lane_gather(rows[k], low[g]), out[g][k])
    return out


def slot_row(ref, k, row, per, group=0):
    if per:
        at = group * 3 * per + k * per + row % per
        return ref[row // per, at : at + 1, :]
    return ref[group * 3 + k, row : row + 1, :]


def store_rows(out_ref, g, values, per, beside=False):
    for k in range(3):
        for s in range(SUB):
            row = g * SUB + s
            value = values[k][s : s + 1, :]
            if per:
                d, at = row // per, k * per + row % per
                out_ref[d, at : at + 1, :] = value
                if beside and d + 1 < out_ref.shape[0]:
                    out_ref[d + 1, 3 * per + at : 3 * per + at + 1, :] = value
                if beside and d > 0:
                    out_ref[d - 1, 6 * per + at : 6 * per + at + 1, :] = value
            else:
                out_ref[k, row : row + 1, :] = value


def pick_body(
    table_hbm, index_hbm, mesh_ref, vertex_hbm, slot_hbm, weight_hbm, pick_hbm, source_hbm, target_hbm,
    out_ref, head, tail, vertex_ref, slot_ref, weight_ref, pick_ref, source_ref, target_ref,
    table_ref, index_ref, sems, side_sems, *, per,
):
    comps, width, height, depth = mesh_ref.shape
    tiles = depth // LANES
    pairs = (
        (index_hbm, index_ref), (table_hbm, table_ref), (vertex_hbm, vertex_ref), (slot_hbm, slot_ref),
        (weight_hbm, weight_ref), (pick_hbm, pick_ref), (source_hbm, source_ref), (target_hbm, target_ref),
    )
    needed = [pltpu.make_async_copy(a, b, sems.at[i]) for i, (a, b) in enumerate(pairs)]
    side = []
    for k in range(comps):
        for p in range(2):
            rows = pl.ds((k * 2 + p) * height, height)
            side.append(pltpu.make_async_copy(mesh_ref.at[k, p], head.at[rows], side_sems.at[0, k, p]))
            side.append(
                pltpu.make_async_copy(mesh_ref.at[k, width - 2 + p], tail.at[rows], side_sems.at[1, k, p])
            )
    for copy in needed + side:
        copy.start()
    for copy in needed[:2]:
        copy.wait()
    groups = index_ref.shape[0] // SUB
    blocks = table_ref.shape[1] // LANES
    half = max(1, groups // 2)
    for first in range(0, groups, half):
        got = gather_rows(
            lambda k, b: table_ref[k : k + 1, b * LANES : (b + 1) * LANES],
            blocks,
            lambda g: index_ref[(first + g) * SUB : (first + g + 1) * SUB, :],
            half,
        )
        for g in range(half):
            store_rows(out_ref, first + g, got[g], per)
    for copy in needed[2:]:
        copy.wait()
    start = comps * 2 * height
    for row in range(vertex_ref.shape[0]):
        value = vertex_ref[row : row + 1, :].astype(f32)
        at, j = start + row // tiles, row % tiles * LANES
        head[at : at + 1, j : j + LANES] = value
        tail[at : at + 1, j : j + LANES] = value
    for copy in side:
        copy.wait()


def pieces(value, count=3):
    found = []
    for _ in range(count):
        top = value.astype(bf16).astype(f32)
        found.append(top)
        value = value - top
    return found


def factor(points, target):
    square = points * points
    norm = jnp.broadcast_to(jnp.sum(square, axis=0, keepdims=True), square.shape)
    row = lax.broadcasted_iota(jnp.int32, square.shape, 0)
    a, b, c = pieces(norm)
    p, q, r = pieces(points)
    if target:
        edge = jnp.where(row < 3, -1.0, jnp.where(row == 3, -a, jnp.where(row == 4, -b, jnp.where(row == 5, -c, 0.0))))
        blocks = [2.0 * p, 2.0 * q, 2.0 * p, 2.0 * q, 2.0 * r, 2.0 * p, edge]
    else:
        edge = jnp.where(row == 0, a, jnp.where(row == 1, b, jnp.where(row == 2, c, jnp.where(row < 6, 1.0, 0.0))))
        blocks = [p, p, q, q, p, r, edge]
    blocks.append(jnp.zeros(square.shape, f32))
    return jnp.concatenate(blocks, axis=0)


def rbf_matrix(source, target, put):
    scale = math.sqrt(sharpness * math.log2(math.e))
    points = source[0].shape[1]
    step = LANES

    def centred(rows):
        blank = jnp.zeros((SUB - 3, rows[0].shape[1]), f32)
        return jnp.concatenate([(row - 0.5) * scale for row in rows] + [blank], axis=0)

    turned = jnp.transpose(factor(centred(source), False)).astype(bf16)
    right = factor(centred(target), True).astype(bf16)
    for at in range(0, points, step):
        value = jnp.exp2(jnp.dot(turned[at : at + step], right, preferred_element_type=f32))
        high = value.astype(bf16)
        put(at, step, high, (value - high.astype(f32)).astype(bf16))


def result_body(
    arrived_ref, slot_ref, source_ref, target_ref, inverse_ref, weight_ref, pick_ref,
    out_ref, inverse, high, low, members, results, sems, *, per_in, per_out,
):
    clusters, points = slot_ref.shape
    verts = weight_ref.shape[1]
    blocks = (arrived_ref.shape[0] * per_in) if per_in else arrived_ref.shape[1]
    per_cluster = verts // LANES
    groups = pick_ref.shape[0] // SUB
    fold = points // LANES // SUB
    copies = [pltpu.make_async_copy(inverse_ref.at[c], inverse.at[c], sems.at[c]) for c in range(clusters)]
    for copy in copies:
        copy.start()
    members[...] = jnp.zeros(members.shape, f32)

    def gather_members(c):
        got = gather_rows(
            lambda k, b: slot_row(arrived_ref, k, b, per_in),
            blocks,
            lambda g: jnp.concatenate(
                [slot_ref[c : c + 1, (g * SUB + j) * LANES : (g * SUB + j + 1) * LANES] for j in range(SUB)], axis=0
            ),
            fold,
        )
        for g in range(fold):
            for j in range(SUB):
                at = (g * SUB + j) * LANES
                for k in range(3):
                    members[c, k : k + 1, at : at + LANES] = got[g][k][j : j + 1, :]

    def joined(ref, c):
        return jnp.concatenate([ref[c, j] for j in range(per_cluster)], axis=1)

    def evaluate(c):
        mine = members[c]
        copies[c].wait()
        coupling = lax.dot_general(
            mine.astype(bf16), inverse[c], (((1,), (1,)), ((), ())), preferred_element_type=f32
        )
        coefficient = mine + coupling
        c_high = coefficient.astype(bf16)
        c_low = (coefficient - c_high.astype(f32)).astype(bf16)
        both = jnp.concatenate([c_high, c_low], axis=0)
        first = jnp.dot(both, joined(high, c), preferred_element_type=f32)
        second = jnp.dot(c_high, joined(low, c), preferred_element_type=f32)
        total = first[:SUB] + (first[SUB:] + second)
        results[c] = total * weight_ref[c : c + 1, :]

    for c in range(clusters):

        def put(at, step, upper, lower):
            for j in range(per_cluster):
                high[c, j, at : at + step, :] = upper[:, j * LANES : (j + 1) * LANES]
                low[c, j, at : at + step, :] = lower[:, j * LANES : (j + 1) * LANES]

        rbf_matrix(*(tuple(ref[k, c : c + 1, :] for k in range(3)) for ref in (source_ref, target_ref)), put)
        gather_members(c)
        evaluate(c)
    if per_out:
        blank = jnp.zeros((3 * per_out, LANES), f32)
        out_ref[0, 3 * per_out : 6 * per_out, :] = blank
        out_ref[out_ref.shape[0] - 1, 6 * per_out : 9 * per_out, :] = blank
    half = max(1, groups // 2)
    for start in range(0, groups, half):
        got = gather_rows(
            lambda k, b: results[
                b // per_cluster, k : k + 1, (b % per_cluster) * LANES : (b % per_cluster + 1) * LANES
            ],
            clusters * per_cluster,
            lambda g: pick_ref[(start + g) * SUB : (start + g + 1) * SUB, :],
            half,
        )
        for g in range(half):
            store_rows(out_ref, start + g, got[g], per_out, True)


def columns(j):
    return pl.ds(j * LANES, LANES)


def start_band(sums):
    line = lax.broadcasted_iota(jnp.int32, (WIDE, WIDE), 0)
    column = lax.broadcasted_iota(jnp.int32, (WIDE, WIDE), 1)
    apart = jnp.abs(line - column)
    band = jnp.where(apart == 0, keep, jnp.where(apart == 1, 1.0, 0.0)).astype(bf16)
    ends = []
    for unit in range(len(sums)):
        pltpu.matmul_push_rhs(band, 0, unit)
        pltpu.matmul_acc_lhs(sums[unit][0], jnp.zeros((TALL, WIDE), bf16), load_staged_rhs=0)
        ends.append(pltpu.matmul_pop(sums[unit][0]))
    return ends


def sweep_planes(jobs, height, depth, sums):
    tiles, strips = depth // LANES, height // TALL
    wides, part = depth // WIDE, WIDE // LANES
    units = len(sums)
    halves = wides // units
    lane = lax.broadcasted_iota(jnp.int32, (TALL, LANES), 1)
    row = lax.broadcasted_iota(jnp.int32, (TALL, LANES), 0)

    def place(spot, h):
        return sums[h % units][spot * halves + h // units]

    def multiply(todo):
        later = []
        for center, y, spot in todo:
            for h in range(wides):
                value = jnp.concatenate(
                    [center[j, pl.ds(SUB + y * TALL, TALL), :] for j in range(h * part, (h + 1) * part)], axis=1
                )
                high = value.astype(bf16)
                pltpu.matmul_acc_lhs(place(spot, h), high)
                later.append((place(spot, h), (value - high.astype(f32)).astype(bf16)))
        for total, low in later:
            pltpu.matmul_acc_lhs(total, low)

    def complete(center, before, after, y, spot, put):
        at = SUB + y * TALL
        beside = [pltpu.matmul_pop(place(spot, h)) for h in range(wides)]
        for j in range(tiles):
            lower = center[j, pl.ds(at - 1, TALL), :]
            if y == 0:
                lower = jnp.where(row < 2, 0.0, lower)
            near = (before[j, pl.ds(at, TALL), :] + after[j, pl.ds(at, TALL), :]) + (
                center[j, pl.ds(at + 1, TALL), :] + lower
            )
            h, p = j // part, j % part
            value = near + beside[h][:, p * LANES : (p + 1) * LANES]
            if p == 0 and h:
                value = value + jnp.where(lane == 0, pltpu.roll(center[j - 1, pl.ds(at, TALL), :], 1, 1), 0.0)
            if p == part - 1 and j + 1 < tiles:
                other = pltpu.roll(center[j + 1, pl.ds(at, TALL), :], LANES - 1, 1)
                value = value + jnp.where(lane == LANES - 1, other, 0.0)
            if y == 0:
                value = jnp.where(row == 0, 0.0, value)
            put(j, y, value)

    group = 3
    for y in range(0, strips + group, group):
        base = y // group % 2 * 2 * group
        if y < strips:
            multiply([(job[0], y + n, base + n * 2 + i) for n in range(group) for i, job in enumerate(jobs)])
        if y >= group:
            for n in range(group):
                for i, (center, before, after, put) in enumerate(jobs):
                    complete(center, before, after, y - group + n, 2 * group - base + n * 2 + i, put)


def mesh_body(_, mesh_ref, out_ref, field, ring, stage, in_sems, out_sems, sums):
    comps, width, height, depth = mesh_ref.shape
    tiles = depth // LANES
    turns = len(ring)
    quads = width // turns - 1

    def load(k, b):
        return [
            pltpu.make_async_copy(
                mesh_ref.at[k, pl.ds(b * turns, turns), :, columns(j)],
                field.at[k, pl.ds(b * turns, turns), j, pl.ds(SUB, height), :],
                in_sems.at[k, b, j],
            )
            for j in range(tiles)
        ]

    for k in range(comps):
        for b in range(width // turns):
            for copy in load(k, b):
                copy.start()

    blank = jnp.zeros((SUB, LANES), f32)
    for j in range(tiles):
        for plane in ring:
            plane[j, SUB + height : 2 * SUB + height, :] = blank

    def clear(i, _):
        for j in range(tiles):
            field[i // width, i % width, j, SUB + height : 2 * SUB + height, :] = blank
        return 0

    lax.fori_loop(0, comps * width, clear, 0)
    for unit, value in enumerate(start_band(sums)):
        stage[unit, 0:TALL, 0:WIDE] = value

    def flush(k, x, slot):
        return pltpu.make_async_copy(stage.at[slot], out_ref.at[k, x], out_sems.at[slot])

    def work(k, x, phase, slot=None):
        def put_first(j, y, value):
            ring[phase % turns][j, pl.ds(SUB + y * TALL, TALL), :] = value

        def put_second(j, y, value):
            stage[slot, y * TALL : (y + 1) * TALL, j * LANES : (j + 1) * LANES] = value * (share * share)

        jobs = [(field.at[k, x], field.at[k, x - 1], field.at[k, x + 1], put_first)]
        if slot is not None:
            jobs.append((ring[(phase - 2) % turns], ring[(phase - 3) % turns], ring[(phase - 1) % turns], put_second))
        sweep_planes(jobs, height, depth, sums)

    def component(k, _):
        for b in range(2):
            for copy in load(k, b):
                copy.wait()
        for phase in range(3):
            work(k, phase + 1, phase)

        def quad(i, _):
            @pl.when(i + 2 < width // turns)
            def _():
                for copy in load(k, i + 2):
                    copy.wait()

            turn = k * quads + i
            slots = (turn % 2) * turns

            @pl.when(turn >= 2)
            def _():
                for sub in range(turns):
                    flush(k, 0, slots + sub).wait()

            for sub in range(turns):
                work(k, jnp.minimum(i * turns + sub + 4, width - 2), sub + 3, slots + sub)
            for sub in range(turns):
                flush(k, i * turns + sub + 2, slots + sub).start()
            return 0

        lax.fori_loop(0, quads, quad, 0)
        return 0

    lax.fori_loop(0, comps, component, 0)
    for slot in range(2 * turns):
        flush(0, 0, slot).wait()


def edges_body(_, edge_ref, mesh_ref, left_ref, right_ref, out_ref, field, swept, stage, in_sems, out_sems, sums):
    comps, width, height, depth = mesh_ref.shape
    tiles = depth // LANES

    def outer(k):
        found = []
        for j in range(tiles):
            for side, ref in enumerate((left_ref, right_ref)):
                own, other = (2, 0) if side == 0 else (0, 4)
                found.append(
                    pltpu.make_async_copy(
                        mesh_ref.at[k, pl.ds(side * (width - 4), 4), :, columns(j)],
                        field.at[k, side, pl.ds(own, 4), j, pl.ds(SUB, height), :],
                        in_sems.at[k, j, side, 0],
                    )
                )
                for p in range(2):
                    found.append(
                        pltpu.make_async_copy(
                            ref.at[pl.ds((k * 2 + p) * height, height), columns(j)],
                            field.at[k, side, other + p, j, pl.ds(SUB, height), :],
                            in_sems.at[k, j, side, 1 + p],
                        )
                    )
        return found

    for k in range(comps):
        for copy in outer(k):
            copy.start()

    blank = jnp.zeros((SUB, LANES), f32)
    for j in range(tiles):
        for side in range(2):
            for p in range(4):
                swept[side][p][j, SUB + height : 2 * SUB + height, :] = blank

    def clear(i, _):
        for side in range(2):
            for p in range(6):
                for j in range(tiles):
                    field[i, side, p, j, SUB + height : 2 * SUB + height, :] = blank
        return 0

    lax.fori_loop(0, comps, clear, 0)
    for unit, value in enumerate(start_band(sums)):
        stage[0, unit, 0:TALL, 0:WIDE] = value
    gates = [jnp.where(edge_ref[side] == 0, 0.0, 1.0) for side in range(2)]

    def save(k):
        return [
            pltpu.make_async_copy(
                stage.at[k, side * 2 + p],
                out_ref.at[k, side * (width - 2) + p],
                out_sems.at[k, side, p],
            )
            for side in range(2)
            for p in range(2)
        ]

    def component(k, _):
        for copy in outer(k):
            copy.wait()
        for p in range(4):
            jobs = []
            for side in range(2):

                def put(j, y, value, side=side):
                    if p == side * 3:
                        value = value * gates[side]
                    swept[side][p][j, pl.ds(SUB + y * TALL, TALL), :] = value

                jobs.append((field.at[k, side, p + 1], field.at[k, side, p], field.at[k, side, p + 2], put))
            sweep_planes(jobs, height, depth, sums)
        for p in range(2):
            jobs = []
            for side in range(2):

                def put(j, y, value, side=side):
                    value = value * (share * share)
                    span = slice(j * LANES, (j + 1) * LANES)
                    stage[k, side * 2 + p, y * TALL : (y + 1) * TALL, span] = value

                jobs.append((swept[side][p + 1], swept[side][p], swept[side][p + 2], put))
            sweep_planes(jobs, height, depth, sums)
        for copy in save(k):
            copy.start()
        return 0

    lax.fori_loop(0, comps, component, 0)
    for k in range(comps):
        for copy in save(k):
            copy.wait()


def finish_body(
    base_ref, returned_ref, vertex_ref, left_ref, right_ref, out_ref,
    wall, left, right, split, high_sc, low_sc, rows_sc, ones_sc, sems, *, per,
):
    comps, width, _, depth = wall.shape
    tiles = depth // LANES
    rows = vertex_ref.shape[0]
    count = left.shape[0]
    start = left_ref.shape[0] - count
    fetch = [pltpu.make_async_copy(base_ref.at[k, :, pl.ds(0, SUB), :], wall.at[k], sems.at[k]) for k in range(comps)]
    beside = [
        pltpu.make_async_copy(left_ref.at[pl.ds(start, count), :], left, sems.at[comps]),
        pltpu.make_async_copy(right_ref.at[pl.ds(start, count), :], right, sems.at[comps + 1]),
    ]
    for copy in beside + fetch:
        copy.start()
    whole = returned_ref[...]
    top = whole.astype(bf16).astype(f32)
    split[0] = top
    split[1] = whole - top
    for copy in beside:
        copy.wait()

    def spread(row, size):
        tile = jnp.broadcast_to(row, (TALL, LANES)).astype(bf16)
        return jnp.concatenate([tile] * (size // TALL), axis=0)

    def lines(size):
        return lax.broadcasted_iota(jnp.int32, (size, LANES), 0)

    def gathered(vertices, group, home, lows):
        size = home.shape[0]
        shift = lows.bit_length() - 1
        vertices = jnp.concatenate(vertices, axis=0) if isinstance(vertices, list) else vertices
        high_sc[...] = lax.shift_right_arithmetic(vertices, shift).astype(f32)
        low_sc[...] = jnp.bitwise_and(vertices, lows - 1).astype(f32)
        home = home.astype(f32).astype(bf16)
        line = lines(lows).astype(f32).astype(bf16)
        one = jnp.ones((lows, LANES), bf16)
        nothing = jnp.zeros((lows, LANES), bf16)
        empty = jnp.zeros((size, LANES), bf16)
        for row in range(rows):
            match = line == spread(low_sc[row : row + 1, :], lows)
            ones_sc[row, :lows] = jnp.where(match, one, nothing)
            here = home == spread(high_sc[row : row + 1, :], size)
            for term in range(2):
                for k in range(comps):
                    value = spread(slot_row(split.at[term], k, row, per, group), size)
                    at = (term * comps + k) * size
                    rows_sc[row, at : at + size] = jnp.where(here, value, empty)
        total = lax.dot_general(
            jnp.concatenate([rows_sc[row, : 2 * comps * size] for row in range(rows)], axis=1),
            jnp.concatenate([ones_sc[row, :lows] for row in range(rows)], axis=1),
            (((1,), (1,)), ((), ())),
            preferred_element_type=f32,
        )
        total = total[: comps * size] + total[comps * size :]
        return [total[k * size : (k + 1) * size] for k in range(comps)]

    blocks = depth // WIDE
    line = lines(width * blocks)
    own = gathered(vertex_ref[...], 0, (line % width) * blocks + line // width, WIDE)
    line = lines(TALL)

    def unfold(ref):
        return [ref[at : at + 1, j * LANES : (j + 1) * LANES].astype(jnp.int32) for at in range(count) for j in range(tiles)]

    last = gathered(unfold(left), 1, jnp.where(line < tiles, (width - 1) * tiles + line, -1), LANES)
    first = gathered(unfold(right), 2, jnp.where(line < tiles, line, -1), LANES)

    lane = lax.broadcasted_iota(jnp.int32, (width, LANES), 1)
    line = lax.broadcasted_iota(jnp.int32, (width, LANES), 0)
    row = lax.broadcasted_iota(jnp.int32, (SUB, LANES), 0)
    flush = [pltpu.make_async_copy(wall.at[k], out_ref.at[k, :, pl.ds(0, SUB), :], sems.at[comps + 2 + k]) for k in range(comps)]
    per_wide = WIDE // LANES
    for k in range(comps):
        parts = []
        for j in range(tiles):
            block, lanes = j // per_wide * width, j % per_wide * LANES
            parts.append(own[k][block : block + width, lanes : lanes + LANES])
        down = [pltpu.roll(p, 1, 1) for p in parts]
        up = [pltpu.roll(p, LANES - 1, 1) for p in parts]
        fetch[k].wait()
        for j in range(tiles):
            mid = parts[j]
            back = jnp.where(lane == 0, down[j - 1] if j else 0.0, down[j])
            fore = jnp.where(lane == LANES - 1, up[j + 1] if j + 1 < tiles else 0.0, up[j])
            prev = jnp.where(line == 0, last[k][j : j + 1], pltpu.roll(mid, 1, 0))
            after = jnp.where(line == width - 1, first[k][j : j + 1], pltpu.roll(mid, width - 1, 0))
            near = ((prev + after) + (back + fore)) * (share * share)
            one = mid * (1.2 * share) + near
            two = mid * (share * share)
            span = slice(j * LANES, (j + 1) * LANES)
            for x in range(width):
                add = jnp.where(row == 1, one[x : x + 1], jnp.where(row == 2, two[x : x + 1], 0.0))
                wall[k, x, :, span] = jnp.where(row == 0, mid[x : x + 1], wall[k, x, :, span] + add)
        flush[k].start()
    for copy in flush:
        copy.wait()


def exchange(packed, per, cap, beside=False):
    if per:
        return lax.all_to_all(packed, "dev", split_axis=0, concat_axis=0, tiled=True)
    count = lax.axis_size("dev")
    split = packed.reshape(3, count, cap)
    if beside:
        blank = jnp.zeros((3, 1, cap), f32)
        before = jnp.concatenate([blank, split[:, :-1]], axis=1)
        after = jnp.concatenate([split[:, 1:], blank], axis=1)
        split = jnp.concatenate([split, before, after], axis=0)
    moved = lax.all_to_all(split, "dev", split_axis=1, concat_axis=1, tiled=True)
    return moved.reshape((split.shape[0],) + packed.shape[1:])


def local(
    displacement,
    send_node,
    member_slot,
    inverse_part,
    source_coord,
    target_coord,
    unity_weight,
    result_pick,
    receive_vertex,
    mesh_before,
):
    count = lax.axis_size("dev")
    place = lax.axis_index("dev")
    send_cap = send_node.shape[0] // count
    result_cap = result_pick.shape[0] // count
    send_per = send_cap // LANES if send_cap % LANES == 0 else 0
    result_per = result_cap // LANES if result_cap % LANES == 0 else 0
    clusters, points = member_slot.shape
    verts = unity_weight.shape[1]
    comps, width, height, depth = mesh_before.shape
    tiles = depth // LANES
    count_rows = receive_vertex.shape[0] // depth

    def packed_shape(per, size, parts=1):
        shape = (count, 3 * per * parts, LANES) if per else (3, size // LANES, LANES)
        return jax.ShapeDtypeStruct(shape, f32)

    up = [(i, i + 1) for i in range(count - 1)]
    down = [(i + 1, i) for i in range(count - 1)]

    field = in_hbm(mesh_before)
    side = pltpu.VMEM((comps * 2 * height + count_rows, depth), f32)
    node_rows = send_node.reshape(-1, LANES)
    small = (
        receive_vertex.reshape(-1, LANES),
        member_slot,
        unity_weight,
        result_pick.reshape(-1, LANES),
        jnp.transpose(source_coord, (1, 0, 2)),
        jnp.transpose(target_coord, (1, 0, 2)),
    )
    outgoing, head, tail, vertices, slots, weight, picks, source, target = pl.pallas_call(
        lambda *refs: pick_body(*refs, per=send_per),
        out_shape=(packed_shape(send_per, send_node.shape[0]), side, side)
        + tuple(pltpu.VMEM(x.shape, x.dtype) for x in small),
        in_specs=[HBM] * 9,
        out_specs=(VMEM,) * 9,
        scratch_shapes=[
            pltpu.VMEM(displacement.shape, f32),
            pltpu.VMEM(node_rows.shape, jnp.int32),
            pltpu.SemaphoreType.DMA((8,)),
            pltpu.SemaphoreType.DMA((2, comps, 2)),
        ],
        compiler_params=params(4),
        name="pick_nodes",
    )(in_hbm(displacement), in_hbm(node_rows), field, *map(in_hbm, small))
    arrived = exchange(outgoing, send_per, send_cap)
    halo_left = lax.ppermute(tail, "dev", up)
    halo_right = lax.ppermute(head, "dev", down)

    outgoing_results = pl.pallas_call(
        lambda *refs: result_body(*refs, per_in=send_per, per_out=result_per),
        out_shape=packed_shape(result_per, result_pick.shape[0], 3),
        in_specs=[VMEM] * 4 + [HBM] + [VMEM] * 2,
        out_specs=VMEM,
        scratch_shapes=[
            pltpu.VMEM(inverse_part.shape, bf16),
            pltpu.VMEM((clusters, verts // LANES, points, LANES), bf16),
            pltpu.VMEM((clusters, verts // LANES, points, LANES), bf16),
            pltpu.VMEM((clusters, SUB, points), f32),
            pltpu.VMEM((clusters, SUB, verts), f32),
            pltpu.SemaphoreType.DMA((clusters,)),
        ],
        compiler_params=params(40),
        name="cluster_results",
    )(arrived, slots, source, target, in_hbm(inverse_part), weight, picks)
    returned = exchange(outgoing_results, result_per, result_cap, True)

    edges = jnp.stack([place, count - 1 - place]).astype(jnp.int32)
    turns = 4
    if width % turns or width < 2 * turns or depth % (2 * WIDE) or height % TALL or tiles > TALL:
        raise ValueError("mesh shape")

    def with_sums(body):
        places = 12 * (depth // WIDE // 2)
        sums = tuple(tuple(pltpu.ACC(unit)((TALL, WIDE), f32) for _ in range(places)) for unit in range(2))
        return lambda *refs: pl.run_scoped(lambda *sums: body(*refs, sums), *sums)

    tall = height + 2 * SUB
    base = pl.pallas_call(
        with_sums(mesh_body),
        out_shape=jax.ShapeDtypeStruct(mesh_before.shape, f32),
        in_specs=[ANY, HBM],
        out_specs=HBM,
        scratch_shapes=[
            pltpu.VMEM((comps, width, tiles, tall, LANES), f32),
            tuple(pltpu.VMEM((tiles, tall, LANES), f32) for _ in range(turns)),
            pltpu.VMEM((2 * turns, height, depth), f32),
            pltpu.SemaphoreType.DMA((comps, width // turns, tiles)),
            pltpu.SemaphoreType.DMA((2 * turns,)),
        ],
        compiler_params=params(20),
        name="sweeps",
    )(outgoing_results, field)

    swept = pl.pallas_call(
        with_sums(edges_body),
        out_shape=jax.ShapeDtypeStruct(mesh_before.shape, f32),
        in_specs=[HBM, SMEM, HBM, ANY, ANY],
        out_specs=HBM,
        scratch_shapes=[
            pltpu.VMEM((comps, 2, 6, tiles, tall, LANES), f32),
            tuple(tuple(pltpu.VMEM((tiles, tall, LANES), f32) for _ in range(4)) for _ in range(2)),
            pltpu.VMEM((comps, 4, height, depth), f32),
            pltpu.SemaphoreType.DMA((comps, tiles, 2, 3)),
            pltpu.SemaphoreType.DMA((comps, 2, 2)),
        ],
        input_output_aliases={0: 0},
        compiler_params=params(20),
        name="edges",
    )(in_hbm(base), edges, field, halo_left, halo_right)

    slot_rows = receive_vertex.shape[0] // LANES
    size = width * (depth // WIDE)
    return pl.pallas_call(
        lambda *refs: finish_body(*refs, per=result_per),
        out_shape=jax.ShapeDtypeStruct(mesh_before.shape, f32),
        in_specs=[HBM, VMEM, VMEM, ANY, ANY],
        out_specs=HBM,
        scratch_shapes=[
            pltpu.VMEM((comps, width, SUB, depth), f32),
            pltpu.VMEM((count_rows, depth), f32),
            pltpu.VMEM((count_rows, depth), f32),
            pltpu.VMEM((2,) + returned.shape, f32),
            pltpu.VMEM((slot_rows, LANES), f32),
            pltpu.VMEM((slot_rows, LANES), f32),
            pltpu.VMEM((slot_rows, 2 * comps * max(size, TALL), LANES), bf16),
            pltpu.VMEM((slot_rows, WIDE, LANES), bf16),
            pltpu.SemaphoreType.DMA((2 * comps + 2,)),
        ],
        input_output_aliases={0: 0},
        compiler_params=params(24),
        name="finish",
    )(in_hbm(swept), returned, vertices, halo_left, halo_right)


def solution(mesh):
    in_specs = (
        P(None, "dev"),
        P("dev"),
        P("dev", None),
        P("dev", None, None),
        P("dev", None, None),
        P("dev", None, None),
        P("dev", None),
        P("dev"),
        P("dev"),
        P(None, "dev", None, None),
    )
    out_specs = P(None, "dev", None, None)

    return jax.shard_map(local, mesh=mesh, in_specs=in_specs, out_specs=out_specs, check_vma=False)
```

time: 306 us -> 80 us (0.26)
  the two profiles are of different devices: /device:TPU:4 before, /device:TPU:0 now
where the time goes in v4:
time: 80 us; the launch traced here: 79.7 us
  Pallas kernels  39.5 us (49%)
  blocking collectives  31 us (39%)
  starting transfers between devices  8.91 us (11%)
    all_to_all x1, blocking collectives, exchange(): lax.all_to_all(packed, 'dev', split_axis=0, concat_axis=0, tiled=True)  31 us
    pallas_call x1, Pallas kernels, local(): pl.pallas_call(with_sums(mesh_body), out_shape=jax.ShapeDtypeStruct(mesh_...  11.7 us
    pallas_call x1, Pallas kernels, local(): pl.pallas_call(lambda *refs: result_body(*refs, per_in=send_per, per_out=...  10.2 us
    pallas_call x1, Pallas kernels, local(): pl.pallas_call(with_sums(edges_body), out_shape=jax.ShapeDtypeStruct(mesh...  7.23 us
    pallas_call x1, Pallas kernels, local(): pl.pallas_call(lambda *refs: finish_body(*refs, per=result_per), out_shap...  5.6 us
    all_to_all x1, starting transfers between devices, exchange(): lax.all_to_all(packed, 'dev', split_axis=0, concat_axis=0, tiled=True)  5.14 us
    pallas_call x1, Pallas kernels, local(): pl.pallas_call(lambda *refs: pick_body(*refs, per=send_per), out_shape=(p...  4.67 us
    ppermute x1, starting transfers between devices, local(): halo_left = lax.ppermute(tail, 'dev', up)  2.47 us
  transfers between devices with their start and end apart: 3, of which 0 were waited for; matrix products, arithmetic and copies ran while one was open for 0% of the time, Pallas kernels for 37%

profile of v4, /device:TPU:0, one launch (start us, length us, event | category | flops | bytes accessed | tf_op | source)
XLA Modules:
  0.0 79.7 jit_solution(15639376513034708340)
XLA Ops:
  0.0 4.7 %pick_nodes.1 = (f32[32,6,128]{2,1,0:T(8,128)S(1)}, f32[592,512]{1,0:T(8,128)}, f32[592,512]{1,0:T(8,128)}, s32[64,128]{1,0:T(8,128)S(1)}, s32[4,1024]{1,0:T(4,1...) custom-call(f32[3,4096]{1,0:T(4,128)} %refs_0_.1, ...), custom_call_target="tpu_custom_call" | custom-call | tf_op jit(solution)/shard_map/pick_nodes/pallas_call | solution.py:650
  4.7 2.5 %collective-permute-start = (f32[592,512]{1,0:T(8,128)}, f32[592,512]{1,0:T(8,128)S(1)}, u32[]{:S(2)}, u32[]{:S(2)}) collective-permute-start(f32[592,512]{1,0:T(8,128)} %get-tuple-element.20), channel_id=1, source_target_pairs={{0,1},{1,2},{2,3},{3,4},{4,5},{5,6},{6,7},{7,8},{8,9},{9,10},{10,1... | collective-permute-start | bytes 3637256 | tf_op jit(solution)/shard_map/ppermute | solution.py:666
  7.2 1.3 %collective-permute-start.1 = (f32[592,512]{1,0:T(8,128)}, f32[592,512]{1,0:T(8,128)S(1)}, u32[]{:S(2)}, u32[]{:S(2)}) collective-permute-start(f32[592,512]{1,0:T(8,128)} %get-tuple-element.21), channel_id=1, source_target_pairs={{1,0},{2,1},{3,2},{4,3},{5,4},{6,5},{7,6},{8,7},{9,8},{10,9},{11,1... | collective-permute-start | bytes 3637256 | tf_op jit(solution)/shard_map/ppermute | solution.py:667
  8.5 31.0 %all_to_all.10.refs_0_ = f32[32,6,128]{2,1,0:T(8,128)S(1)} all-to-all(f32[32,6,128]{2,1,0:T(8,128)S(1)} %get-tuple-element.14), channel_id=1, replica_groups=mesh['dev'=32] {'dev'}, dimensions={0} | all-to-all | bytes 196608 | tf_op jit(solution)/shard_map/all_to_all | solution.py:596
  39.5 10.2 %cluster_results.1.refs_0_ = f32[32,18,128]{2,1,0:T(8,128)} custom-call(f32[32,6,128]{2,1,0:T(8,128)S(1)} %all_to_all.10.refs_0_, s32[4,1024]{1,0:T(4,128)S(1)} %get-tuple-element.15.refs_1_, f32[3,4,1024]{2,1,0:T(4,128)S(1)} %get-tuple-element.16.refs_2_, f32[3,4,1024]{2,1,0:T(4,128)S(1)} %get-tuple-element.17.refs_3_, bf16[4,1024,1024]{2,1,0:T(8,128)(2,1)} %refs_4_.3, ...), custom_call_target="tpu_custom_call" | custom-call | tf_op jit(solution)/shard_map/cluster_results/pallas_call | solution.py:669
  49.7 5.1 %all-to-all-start.1 = ((f32[32,18,128]{2,1,0:T(8,128)}), f32[32,18,128]{2,1,0:T(8,128)S(1)}, u32[]{:S(2)}, u32[]{:S(2)}) async-start(f32[32,18,128]{2,1,0:T(8,128)} %cluster_results.1.refs_0_), calls=%async_computation.1 | async-start | bytes 786432 | tf_op jit(solution)/shard_map/all_to_all | solution.py:596
  54.9 0.1 pad_add_fusion.refs_1_
  54.9 11.7 %sweeps.1.refs_0_ = f32[3,16,96,512]{3,2,1,0:T(8,128)} custom-call(f32[32,18,128]{2,1,0:T(8,128)} %cluster_results.1.refs_0_, f32[3,16,96,512]{3,2,1,0:T(8,128)} %refs_2_.3), custom_call_target="tpu_custom_call" | custom-call | tf_op jit(solution)/shard_map/sweeps/pallas_call | solution.py:698
  66.7 0.0 collective-permute-done.refs_3_
  66.7 0.0 collective-permute-done.1.refs_4_
  66.7 7.2 %edges.1.refs_0_ = f32[3,16,96,512]{3,2,1,0:T(8,128)} custom-call(f32[3,16,96,512]{3,2,1,0:T(8,128)} %sweeps.1.refs_0_, s32[2]{0:T(128)S(1)} %pad_add_fusion.refs_1_, f32[3,16,96,512]{3,2,1,0:T(8,128)} %refs_2_.3, f32[592,512]{1,0:T(8,128)S(1)} %collective-permute-done.refs_3_, ...), custom_call_target="tpu_custom_call", output_to_operand_aliasing={{}: (0, {})} | custom-call | tf_op jit(solution)/shard_map/edges/pallas_call | solution.py:714
  73.9 0.0 all-to-all-done.1.refs_1_
  73.9 5.6 %finish.1 = f32[3,16,96,512]{3,2,1,0:T(8,128)} custom-call(f32[3,16,96,512]{3,2,1,0:T(8,128)} %edges.1.refs_0_, f32[32,18,128]{2,1,0:T(8,128)S(1)} %all-to-all-done.1.refs_1_, s32[64,128]{1,0:T(8,128)S(1)} %get-tuple-element.22.refs_2_, f32[592,512]{1,0:T(8,128)S(1)} %collective-permute-done.refs_3_, ...), custom_call_target="tpu_custom_call", output_to_operand_aliasing={{}: (0, {})} | custom-call | tf_op jit(solution)/shard_map/finish/pallas_call | solution.py:733
Async XLA Ops:
  4.7 62.0 %collective-permute-start = (f32[592,512]{1,0:T(8,128)}, f32[592,512]{1,0:T(8,128)S(1)}, u32[]{:S(2)}, u32[]{:S(2)}) collective-permute-start(f32[592,512]{1,0:T(8,128)} %get-tuple-element.20), channel_id=1, source_target_pairs={{0,1},{1,2},{2,3},{3,4},{4,5},{5,6},{6,7},{7,8},{8,9},{9,10},{10,1... | collective-permute-start | bytes 3637256 | tf_op jit(solution)/shard_map/ppermute | solution.py:666
  7.2 59.5 %collective-permute-start.1 = (f32[592,512]{1,0:T(8,128)}, f32[592,512]{1,0:T(8,128)S(1)}, u32[]{:S(2)}, u32[]{:S(2)}) collective-permute-start(f32[592,512]{1,0:T(8,128)} %get-tuple-element.21), channel_id=1, source_target_pairs={{1,0},{2,1},{3,2},{4,3},{5,4},{6,5},{7,6},{8,7},{9,8},{10,9},{11,1... | collective-permute-start | bytes 3637256 | tf_op jit(solution)/shard_map/ppermute | solution.py:667
  49.7 24.2 %all-to-all-start.1 = ((f32[32,18,128]{2,1,0:T(8,128)}), f32[32,18,128]{2,1,0:T(8,128)S(1)}, u32[]{:S(2)}, u32[]{:S(2)}) async-start(f32[32,18,128]{2,1,0:T(8,128)} %cluster_results.1.refs_0_), calls=%async_computation.1 | async-start | bytes 786432 | tf_op jit(solution)/shard_map/all_to_all | solution.py:596

commit v5 on v4

--- a/solution.py
+++ b/solution.py
@@ -74,8 +74,8 @@
 
 def pick_body(
     table_hbm, index_hbm, mesh_ref, vertex_hbm, slot_hbm, weight_hbm, pick_hbm, source_hbm, target_hbm,
-    out_ref, head, tail, vertex_ref, slot_ref, weight_ref, pick_ref, source_ref, target_ref,
-    table_ref, index_ref, sems, side_sems, *, per,
+    out_ref, head_out, tail_out, vertex_ref, slot_ref, weight_ref, pick_ref, source_ref, target_ref,
+    table_ref, index_ref, head, tail, sems, side_sems, *, per,
 ):
     comps, width, height, depth = mesh_ref.shape
     tiles = depth // LANES
@@ -92,7 +92,7 @@
             side.append(
                 pltpu.make_async_copy(mesh_ref.at[k, width - 2 + p], tail.at[rows], side_sems.at[1, k, p])
             )
-    for copy in needed + side:
+    for copy in needed[:3] + side + needed[3:]:
         copy.start()
     for copy in needed[:2]:
         copy.wait()
@@ -108,15 +108,23 @@
         )
         for g in range(half):
             store_rows(out_ref, first + g, got[g], per)
-    for copy in needed[2:]:
-        copy.wait()
-    start = comps * 2 * height
-    for row in range(vertex_ref.shape[0]):
-        value = vertex_ref[row : row + 1, :].astype(f32)
-        at, j = start + row // tiles, row % tiles * LANES
-        head[at : at + 1, j : j + LANES] = value
-        tail[at : at + 1, j : j + LANES] = value
-    for copy in side:
+        if first == 0:
+            needed[2].wait()
+            start = comps * 2 * height
+            for row in range(vertex_ref.shape[0]):
+                value = vertex_ref[row : row + 1, :].astype(f32)
+                at, j = start + row // tiles, row % tiles * LANES
+                head[at : at + 1, j : j + LANES] = value
+                tail[at : at + 1, j : j + LANES] = value
+            for copy in side:
+                copy.wait()
+            leave = [
+                pltpu.make_async_copy(head, head_out, sems.at[8]),
+                pltpu.make_async_copy(tail, tail_out, sems.at[9]),
+            ]
+            for copy in leave:
+                copy.start()
+    for copy in needed[3:] + leave:
         copy.wait()
 
 
@@ -145,26 +153,19 @@
     return jnp.concatenate(blocks, axis=0)
 
 
-def rbf_matrix(source, target, put):
+def rbf_factors(source, target):
     scale = math.sqrt(sharpness * math.log2(math.e))
-    points = source[0].shape[1]
-    step = LANES
 
     def centred(rows):
         blank = jnp.zeros((SUB - 3, rows[0].shape[1]), f32)
         return jnp.concatenate([(row - 0.5) * scale for row in rows] + [blank], axis=0)
 
-    turned = jnp.transpose(factor(centred(source), False)).astype(bf16)
-    right = factor(centred(target), True).astype(bf16)
-    for at in range(0, points, step):
-        value = jnp.exp2(jnp.dot(turned[at : at + step], right, preferred_element_type=f32))
-        high = value.astype(bf16)
-        put(at, step, high, (value - high.astype(f32)).astype(bf16))
+    return jnp.transpose(factor(centred(source), False)).astype(bf16), factor(centred(target), True).astype(bf16)
 
 
 def result_body(
     arrived_ref, slot_ref, source_ref, target_ref, inverse_ref, weight_ref, pick_ref,
-    out_ref, inverse, high, low, members, results, sems, *, per_in, per_out,
+    out_ref, inverse, members, results, sems, *, per_in, per_out,
 ):
     clusters, points = slot_ref.shape
     verts = weight_ref.shape[1]
@@ -192,10 +193,15 @@
                 for k in range(3):
                     members[c, k : k + 1, at : at + LANES] = got[g][k][j : j + 1, :]
 
-    def joined(ref, c):
-        return jnp.concatenate([ref[c, j] for j in range(per_cluster)], axis=1)
-
     def evaluate(c):
+        turned, right = rbf_factors(*(tuple(ref[k, c : c + 1, :] for k in range(3)) for ref in (source_ref, target_ref)))
+
+        def block(at):
+            value = jnp.exp2(jnp.dot(turned[at : at + WIDE], right, preferred_element_type=f32))
+            high = value.astype(bf16)
+            return high, (value - high.astype(f32)).astype(bf16)
+
+        ready = block(0)
         mine = members[c]
         copies[c].wait()
         coupling = lax.dot_general(
@@ -205,19 +211,18 @@
         c_high = coefficient.astype(bf16)
         c_low = (coefficient - c_high.astype(f32)).astype(bf16)
         both = jnp.concatenate([c_high, c_low], axis=0)
-        first = jnp.dot(both, joined(high, c), preferred_element_type=f32)
-        second = jnp.dot(c_high, joined(low, c), preferred_element_type=f32)
+        first = jnp.zeros((2 * SUB, verts), f32)
+        second = jnp.zeros((SUB, verts), f32)
+        for at in range(0, points, WIDE):
+            high, low = ready
+            if at + WIDE < points:
+                ready = block(at + WIDE)
+            first = first + jnp.dot(both[:, at : at + WIDE], high, preferred_element_type=f32)
+            second = second + jnp.dot(c_high[:, at : at + WIDE], low, preferred_element_type=f32)
         total = first[:SUB] + (first[SUB:] + second)
         results[c] = total * weight_ref[c : c + 1, :]
 
     for c in range(clusters):
-
-        def put(at, step, upper, lower):
-            for j in range(per_cluster):
-                high[c, j, at : at + step, :] = upper[:, j * LANES : (j + 1) * LANES]
-                low[c, j, at : at + step, :] = lower[:, j * LANES : (j + 1) * LANES]
-
-        rbf_matrix(*(tuple(ref[k, c : c + 1, :] for k in range(3)) for ref in (source_ref, target_ref)), put)
         gather_members(c)
         evaluate(c)
     if per_out:
@@ -311,7 +316,7 @@
                     complete(center, before, after, y - group + n, 2 * group - base + n * 2 + i, put)
 
 
-def mesh_body(_, mesh_ref, out_ref, field, ring, stage, in_sems, out_sems, sums):
+def mesh_body(_, mesh_ref, out_ref, kept_out, field, ring, stage, kept, in_sems, out_sems, kept_sems, sums):
     comps, width, height, depth = mesh_ref.shape
     tiles = depth // LANES
     turns = len(ring)
@@ -349,9 +354,14 @@
     def flush(k, x, slot):
         return pltpu.make_async_copy(stage.at[slot], out_ref.at[k, x], out_sems.at[slot])
 
-    def work(k, x, phase, slot=None):
+    def keep_planes(k):
+        return pltpu.make_async_copy(kept.at[k], kept_out.at[k], kept_sems.at[k])
+
+    def work(k, x, phase, slot=None, copy_to=None):
         def put_first(j, y, value):
             ring[phase % turns][j, pl.ds(SUB + y * TALL, TALL), :] = value
+            if copy_to is not None:
+                kept[k, copy_to, j, pl.ds(y * TALL, TALL), :] = value
 
         def put_second(j, y, value):
             stage[slot, y * TALL : (y + 1) * TALL, j * LANES : (j + 1) * LANES] = value * (share * share)
@@ -366,7 +376,7 @@
             for copy in load(k, b):
                 copy.wait()
         for phase in range(3):
-            work(k, phase + 1, phase)
+            work(k, phase + 1, phase, None, phase if phase < 2 else None)
 
         def quad(i, _):
             @pl.when(i + 2 < width // turns)
@@ -383,32 +393,39 @@
                     flush(k, 0, slots + sub).wait()
 
             for sub in range(turns):
-                work(k, jnp.minimum(i * turns + sub + 4, width - 2), sub + 3, slots + sub)
+                place = {1: 2, 2: 3}.get(sub)
+                work(k, jnp.minimum(i * turns + sub + 4, width - 2), sub + 3, slots + sub, place)
             for sub in range(turns):
                 flush(k, i * turns + sub + 2, slots + sub).start()
             return 0
 
         lax.fori_loop(0, quads, quad, 0)
+        keep_planes(k).start()
         return 0
 
     lax.fori_loop(0, comps, component, 0)
     for slot in range(2 * turns):
         flush(0, 0, slot).wait()
-
-
-def edges_body(_, edge_ref, mesh_ref, left_ref, right_ref, out_ref, field, swept, stage, in_sems, out_sems, sums):
+    for k in range(comps):
+        keep_planes(k).wait()
+
+
+def edges_body(
+    base_ref, edge_ref, mesh_ref, kept_ref, left_ref, right_ref, out_ref,
+    field, fetched, computed, stage, in_sems, kept_sems, out_sems, sums,
+):
     comps, width, height, depth = mesh_ref.shape
     tiles = depth // LANES
 
     def outer(k):
         found = []
-        for j in range(tiles):
-            for side, ref in enumerate((left_ref, right_ref)):
-                own, other = (2, 0) if side == 0 else (0, 4)
+        for side, ref in enumerate((left_ref, right_ref)):
+            own, other = (2, 0) if side == 0 else (0, 2)
+            for j in range(tiles):
                 found.append(
                     pltpu.make_async_copy(
-                        mesh_ref.at[k, pl.ds(side * (width - 4), 4), :, columns(j)],
-                        field.at[k, side, pl.ds(own, 4), j, pl.ds(SUB, height), :],
+                        mesh_ref.at[k, pl.ds(side * (width - 2), 2), :, columns(j)],
+                        field.at[k, side, pl.ds(own, 2), j, pl.ds(SUB, height), :],
                         in_sems.at[k, j, side, 0],
                     )
                 )
@@ -420,6 +437,14 @@
                             in_sems.at[k, j, side, 1 + p],
                         )
                     )
+            for p in range(2):
+                found.append(
+                    pltpu.make_async_copy(
+                        kept_ref.at[k, side * 2 + p],
+                        fetched.at[k, side, p, :, pl.ds(SUB, height), :],
+                        kept_sems.at[k, side, p],
+                    )
+                )
         return found
 
     for k in range(comps):
@@ -428,15 +453,16 @@
 
     blank = jnp.zeros((SUB, LANES), f32)
     for j in range(tiles):
-        for side in range(2):
-            for p in range(4):
-                swept[side][p][j, SUB + height : 2 * SUB + height, :] = blank
+        for place in computed:
+            place[j, SUB + height : 2 * SUB + height, :] = blank
 
     def clear(i, _):
         for side in range(2):
-            for p in range(6):
-                for j in range(tiles):
+            for j in range(tiles):
+                for p in range(4):
                     field[i, side, p, j, SUB + height : 2 * SUB + height, :] = blank
+                for p in range(2):
+                    fetched[i, side, p, j, SUB + height : 2 * SUB + height, :] = blank
         return 0
 
     lax.fori_loop(0, comps, clear, 0)
@@ -458,14 +484,18 @@
     def component(k, _):
         for copy in outer(k):
             copy.wait()
-        for p in range(4):
+        swept = (
+            (computed[0], computed[1], fetched.at[k, 0, 0], fetched.at[k, 0, 1]),
+            (fetched.at[k, 1, 0], fetched.at[k, 1, 1], computed[2], computed[3]),
+        )
+        for p in range(2):
             jobs = []
             for side in range(2):
 
                 def put(j, y, value, side=side):
-                    if p == side * 3:
+                    if p == side:
                         value = value * gates[side]
-                    swept[side][p][j, pl.ds(SUB + y * TALL, TALL), :] = value
+                    computed[side * 2 + p][j, pl.ds(SUB + y * TALL, TALL), :] = value
 
                 jobs.append((field.at[k, side, p + 1], field.at[k, side, p], field.at[k, side, p + 2], put))
             sweep_planes(jobs, height, depth, sums)
@@ -637,7 +667,7 @@
     down = [(i + 1, i) for i in range(count - 1)]
 
     field = in_hbm(mesh_before)
-    side = pltpu.VMEM((comps * 2 * height + count_rows, depth), f32)
+    side = (comps * 2 * height + count_rows, depth)
     node_rows = send_node.reshape(-1, LANES)
     small = (
         receive_vertex.reshape(-1, LANES),
@@ -649,23 +679,36 @@
     )
     outgoing, head, tail, vertices, slots, weight, picks, source, target = pl.pallas_call(
         lambda *refs: pick_body(*refs, per=send_per),
-        out_shape=(packed_shape(send_per, send_node.shape[0]), side, side)
+        out_shape=(packed_shape(send_per, send_node.shape[0]), pltpu.HBM(side, f32), pltpu.HBM(side, f32))
         + tuple(pltpu.VMEM(x.shape, x.dtype) for x in small),
         in_specs=[HBM] * 9,
-        out_specs=(VMEM,) * 9,
+        out_specs=(VMEM, HBM, HBM) + (VMEM,) * 6,
         scratch_shapes=[
             pltpu.VMEM(displacement.shape, f32),
             pltpu.VMEM(node_rows.shape, jnp.int32),
-            pltpu.SemaphoreType.DMA((8,)),
+            pltpu.VMEM(side, f32),
+            pltpu.VMEM(side, f32),
+            pltpu.SemaphoreType.DMA((10,)),
             pltpu.SemaphoreType.DMA((2, comps, 2)),
         ],
-        compiler_params=params(4),
+        compiler_params=params(6),
         name="pick_nodes",
     )(in_hbm(displacement), in_hbm(node_rows), field, *map(in_hbm, small))
     arrived = exchange(outgoing, send_per, send_cap)
     halo_left = lax.ppermute(tail, "dev", up)
     halo_right = lax.ppermute(head, "dev", down)
 
+    edges = jnp.stack([place, count - 1 - place]).astype(jnp.int32)
+    turns = 4
+    if width % turns or width < 2 * turns or depth % (2 * WIDE) or height % TALL or tiles > TALL:
+        raise ValueError("mesh shape")
+
+    def with_sums(body):
+        places = 12 * (depth // WIDE // 2)
+        sums = tuple(tuple(pltpu.ACC(unit)((TALL, WIDE), f32) for _ in range(places)) for unit in range(2))
+        return lambda *refs: pl.run_scoped(lambda *sums: body(*refs, sums), *sums)
+
+    tall = height + 2 * SUB
     outgoing_results = pl.pallas_call(
         lambda *refs: result_body(*refs, per_in=send_per, per_out=result_per),
         out_shape=packed_shape(result_per, result_pick.shape[0], 3),
@@ -673,60 +716,54 @@
         out_specs=VMEM,
         scratch_shapes=[
             pltpu.VMEM(inverse_part.shape, bf16),
-            pltpu.VMEM((clusters, verts // LANES, points, LANES), bf16),
-            pltpu.VMEM((clusters, verts // LANES, points, LANES), bf16),
             pltpu.VMEM((clusters, SUB, points), f32),
             pltpu.VMEM((clusters, SUB, verts), f32),
             pltpu.SemaphoreType.DMA((clusters,)),
         ],
-        compiler_params=params(40),
+        compiler_params=params(24),
         name="cluster_results",
     )(arrived, slots, source, target, in_hbm(inverse_part), weight, picks)
     returned = exchange(outgoing_results, result_per, result_cap, True)
 
-    edges = jnp.stack([place, count - 1 - place]).astype(jnp.int32)
-    turns = 4
-    if width % turns or width < 2 * turns or depth % (2 * WIDE) or height % TALL or tiles > TALL:
-        raise ValueError("mesh shape")
-
-    def with_sums(body):
-        places = 12 * (depth // WIDE // 2)
-        sums = tuple(tuple(pltpu.ACC(unit)((TALL, WIDE), f32) for _ in range(places)) for unit in range(2))
-        return lambda *refs: pl.run_scoped(lambda *sums: body(*refs, sums), *sums)
-
-    tall = height + 2 * SUB
-    base = pl.pallas_call(
+    base, kept = pl.pallas_call(
         with_sums(mesh_body),
-        out_shape=jax.ShapeDtypeStruct(mesh_before.shape, f32),
+        out_shape=(
+            jax.ShapeDtypeStruct(mesh_before.shape, f32),
+            pltpu.HBM((comps, 4, tiles, height, LANES), f32),
+        ),
         in_specs=[ANY, HBM],
-        out_specs=HBM,
+        out_specs=(HBM, HBM),
         scratch_shapes=[
             pltpu.VMEM((comps, width, tiles, tall, LANES), f32),
             tuple(pltpu.VMEM((tiles, tall, LANES), f32) for _ in range(turns)),
             pltpu.VMEM((2 * turns, height, depth), f32),
+            pltpu.VMEM((comps, 4, tiles, height, LANES), f32),
             pltpu.SemaphoreType.DMA((comps, width // turns, tiles)),
             pltpu.SemaphoreType.DMA((2 * turns,)),
+            pltpu.SemaphoreType.DMA((comps,)),
         ],
-        compiler_params=params(20),
+        compiler_params=params(24),
         name="sweeps",
     )(outgoing_results, field)
 
-    swept = pl.pallas_call(
+    outer = pl.pallas_call(
         with_sums(edges_body),
         out_shape=jax.ShapeDtypeStruct(mesh_before.shape, f32),
-        in_specs=[HBM, SMEM, HBM, ANY, ANY],
+        in_specs=[HBM, SMEM, HBM, HBM, ANY, ANY],
         out_specs=HBM,
         scratch_shapes=[
-            pltpu.VMEM((comps, 2, 6, tiles, tall, LANES), f32),
-            tuple(tuple(pltpu.VMEM((tiles, tall, LANES), f32) for _ in range(4)) for _ in range(2)),
+            pltpu.VMEM((comps, 2, 4, tiles, tall, LANES), f32),
+            pltpu.VMEM((comps, 2, 2, tiles, tall, LANES), f32),
+            tuple(pltpu.VMEM((tiles, tall, LANES), f32) for _ in range(4)),
             pltpu.VMEM((comps, 4, height, depth), f32),
             pltpu.SemaphoreType.DMA((comps, tiles, 2, 3)),
+            pltpu.SemaphoreType.DMA((comps, 2, 2)),
             pltpu.SemaphoreType.DMA((comps, 2, 2)),
         ],
         input_output_aliases={0: 0},
         compiler_params=params(20),
         name="edges",
-    )(in_hbm(base), edges, field, halo_left, halo_right)
+    )(in_hbm(base), edges, field, in_hbm(kept), halo_left, halo_right)
 
     slot_rows = receive_vertex.shape[0] // LANES
     size = width * (depth // WIDE)
@@ -749,7 +786,7 @@
         input_output_aliases={0: 0},
         compiler_params=params(24),
         name="finish",
-    )(in_hbm(swept), returned, vertices, halo_left, halo_right)
+    )(in_hbm(outer), returned, vertices, halo_left, halo_right)
 
 
 def solution(mesh):

time: 80 us -> 78.4 us (0.980)
  Pallas kernels: 39.5 us -> 37.9 us
    pallas_call x1, Pallas kernels: 7.23 us -> 6.33 us  [local(): pl.pallas_call(with_sums(edges_body), out_shape=jax.ShapeDtypeStruct(mesh...]
    pallas_call x1, Pallas kernels: 4.67 us -> 3.81 us  [local(): pl.pallas_call(lambda *refs: pick_body(*refs, per=send_per), out_shape=(p...]
  transfers between devices with their start and end apart: 3 -> 3, of which waited for: 0 -> 0; matrix products, arithmetic and copies ran while one was open for 0% -> 0% of each run, Pallas kernels for 37% -> 36%
where the time goes in v5:
time: 78.4 us; the launch traced here: 78.1 us
  Pallas kernels  37.9 us (48%)
  blocking collectives  31 us (40%)
  starting transfers between devices  8.92 us (11%)
    all_to_all x1, blocking collectives, exchange(): lax.all_to_all(packed, 'dev', split_axis=0, concat_axis=0, tiled=True)  31 us
    pallas_call x1, Pallas kernels, local(): pl.pallas_call(with_sums(mesh_body), out_shape=(jax.ShapeDtypeStruct(mesh...  12.1 us
    pallas_call x1, Pallas kernels, local(): pl.pallas_call(lambda *refs: result_body(*refs, per_in=send_per, per_out=...  10.1 us
    pallas_call x1, Pallas kernels, local(): pl.pallas_call(with_sums(edges_body), out_shape=jax.ShapeDtypeStruct(mesh...  6.33 us
    pallas_call x1, Pallas kernels, local(): pl.pallas_call(lambda *refs: finish_body(*refs, per=result_per), out_shap...  5.6 us
    all_to_all x1, starting transfers between devices, exchange(): lax.all_to_all(packed, 'dev', split_axis=0, concat_axis=0, tiled=True)  5.15 us
    pallas_call x1, Pallas kernels, local(): pl.pallas_call(lambda *refs: pick_body(*refs, per=send_per), out_shape=(p...  3.81 us
    ppermute x1, starting transfers between devices, local(): halo_left = lax.ppermute(tail, 'dev', up)  2.47 us
  transfers between devices with their start and end apart: 3, of which 0 were waited for; matrix products, arithmetic and copies ran while one was open for 0% of the time, Pallas kernels for 36%

profile of v5, /device:TPU:0, one launch (start us, length us, event | category | flops | bytes accessed | tf_op | source)
XLA Modules:
  0.0 78.1 jit_solution(13548949604505511712)
XLA Ops:
  0.0 3.8 %pick_nodes.1 = (f32[32,6,128]{2,1,0:T(8,128)S(1)}, f32[592,512]{1,0:T(8,128)}, f32[592,512]{1,0:T(8,128)}, s32[64,128]{1,0:T(8,128)S(1)}, s32[4,1024]{1,0:T(4,1...) custom-call(f32[3,4096]{1,0:T(4,128)} %refs_0_.1, ...), custom_call_target="tpu_custom_call" | custom-call | tf_op jit(solution)/shard_map/pick_nodes/pallas_call | solution.py:680
  3.8 2.5 %collective-permute-start = (f32[592,512]{1,0:T(8,128)}, f32[592,512]{1,0:T(8,128)S(1)}, u32[]{:S(2)}, u32[]{:S(2)}) collective-permute-start(f32[592,512]{1,0:T(8,128)} %get-tuple-element.24), channel_id=1, source_target_pairs={{0,1},{1,2},{2,3},{3,4},{4,5},{5,6},{6,7},{7,8},{8,9},{9,10},{10,1... | collective-permute-start | bytes 3637256 | tf_op jit(solution)/shard_map/ppermute | solution.py:698
  6.3 1.3 %collective-permute-start.1 = (f32[592,512]{1,0:T(8,128)}, f32[592,512]{1,0:T(8,128)S(1)}, u32[]{:S(2)}, u32[]{:S(2)}) collective-permute-start(f32[592,512]{1,0:T(8,128)} %get-tuple-element.25), channel_id=1, source_target_pairs={{1,0},{2,1},{3,2},{4,3},{5,4},{6,5},{7,6},{8,7},{9,8},{10,9},{11,1... | collective-permute-start | bytes 3637256 | tf_op jit(solution)/shard_map/ppermute | solution.py:699
  7.6 31.0 %all_to_all.10.refs_0_ = f32[32,6,128]{2,1,0:T(8,128)S(1)} all-to-all(f32[32,6,128]{2,1,0:T(8,128)S(1)} %get-tuple-element.16), channel_id=1, replica_groups=mesh['dev'=32] {'dev'}, dimensions={0} | all-to-all | bytes 196608 | tf_op jit(solution)/shard_map/all_to_all | solution.py:626
  38.6 10.1 %cluster_results.1.refs_0_ = f32[32,18,128]{2,1,0:T(8,128)} custom-call(f32[32,6,128]{2,1,0:T(8,128)S(1)} %all_to_all.10.refs_0_, s32[4,1024]{1,0:T(4,128)S(1)} %get-tuple-element.17.refs_1_, f32[3,4,1024]{2,1,0:T(4,128)S(1)} %get-tuple-element.18.refs_2_, f32[3,4,1024]{2,1,0:T(4,128)S(1)} %get-tuple-element.19.refs_3_, bf16[4,1024,1024]{2,1,0:T(8,128)(2,1)} %refs_4_.3, ...), custom_call_target="tpu_custom_call" | custom-call | tf_op jit(solution)/shard_map/cluster_results/pallas_call | solution.py:712
  48.7 5.2 %all-to-all-start.1 = ((f32[32,18,128]{2,1,0:T(8,128)}), f32[32,18,128]{2,1,0:T(8,128)S(1)}, u32[]{:S(2)}, u32[]{:S(2)}) async-start(f32[32,18,128]{2,1,0:T(8,128)} %cluster_results.1.refs_0_), calls=%async_computation.1 | async-start | bytes 786432 | tf_op jit(solution)/shard_map/all_to_all | solution.py:626
  53.8 0.1 pad_add_fusion.refs_1_
  53.9 12.1 %sweeps.1 = (f32[3,16,96,512]{3,2,1,0:T(8,128)}, f32[3,4,4,96,128]{4,3,2,1,0:T(8,128)}) custom-call(f32[32,18,128]{2,1,0:T(8,128)} %cluster_results.1.refs_0_, f32[3,16,96,512]{3,2,1,0:T(8,128)} %refs_2_.3), custom_call_target="tpu_custom_call" | custom-call | tf_op jit(solution)/shard_map/sweeps/pallas_call | solution.py:728
  66.0 0.0 collective-permute-done.refs_4_.refs_3_
  66.0 0.0 collective-permute-done.1.refs_5_.refs_4_
  66.0 6.3 %edges.1.refs_0_ = f32[3,16,96,512]{3,2,1,0:T(8,128)} custom-call(f32[3,16,96,512]{3,2,1,0:T(8,128)} %get-tuple-element.22.refs_0_, s32[2]{0:T(128)S(1)} %pad_add_fusion.refs_1_, f32[3,16,96,512]{3,2,1,0:T(8,128)} %refs_2_.3, f32[3,4,4,96,128]{4,3,2,1,0:T(8,128)} %get-tuple-element.23.refs_3_, ...), custom_call_target="tpu_custom_call", output_to_operand_aliasing={{}: (0, {})} | custom-call | tf_op jit(solution)/shard_map/edges/pallas_call | solution.py:749
  72.4 0.0 all-to-all-done.1.refs_1_
  72.4 5.6 %finish.1 = f32[3,16,96,512]{3,2,1,0:T(8,128)} custom-call(f32[3,16,96,512]{3,2,1,0:T(8,128)} %edges.1.refs_0_, f32[32,18,128]{2,1,0:T(8,128)S(1)} %all-to-all-done.1.refs_1_, s32[64,128]{1,0:T(8,128)S(1)} %get-tuple-element.26.refs_2_, f32[592,512]{1,0:T(8,128)S(1)} %collective-permute-done.refs_4_.refs_3_, ...), custom_call_target="tpu_custom_call", output_to_operand_aliasing={{}: (0, {})} | custom-call | tf_op jit(solution)/shard_map/finish/pallas_call | solution.py:770
Async XLA Ops:
  3.8 62.2 %collective-permute-start = (f32[592,512]{1,0:T(8,128)}, f32[592,512]{1,0:T(8,128)S(1)}, u32[]{:S(2)}, u32[]{:S(2)}) collective-permute-start(f32[592,512]{1,0:T(8,128)} %get-tuple-element.24), channel_id=1, source_target_pairs={{0,1},{1,2},{2,3},{3,4},{4,5},{5,6},{6,7},{7,8},{8,9},{9,10},{10,1... | collective-permute-start | bytes 3637256 | tf_op jit(solution)/shard_map/ppermute | solution.py:698
  6.3 59.7 %collective-permute-start.1 = (f32[592,512]{1,0:T(8,128)}, f32[592,512]{1,0:T(8,128)S(1)}, u32[]{:S(2)}, u32[]{:S(2)}) collective-permute-start(f32[592,512]{1,0:T(8,128)} %get-tuple-element.25), channel_id=1, source_target_pairs={{1,0},{2,1},{3,2},{4,3},{5,4},{6,5},{7,6},{8,7},{9,8},{10,9},{11,1... | collective-permute-start | bytes 3637256 | tf_op jit(solution)/shard_map/ppermute | solution.py:699
  48.7 23.7 %all-to-all-start.1 = ((f32[32,18,128]{2,1,0:T(8,128)}), f32[32,18,128]{2,1,0:T(8,128)S(1)}, u32[]{:S(2)}, u32[]{:S(2)}) async-start(f32[32,18,128]{2,1,0:T(8,128)} %cluster_results.1.refs_0_), calls=%async_computation.1 | async-start | bytes 786432 | tf_op jit(solution)/shard_map/all_to_all | solution.py:626

commit v6 on v5

--- a/solution.py
+++ b/solution.py
@@ -84,10 +84,12 @@
         (weight_hbm, weight_ref), (pick_hbm, pick_ref), (source_hbm, source_ref), (target_hbm, target_ref),
     )
     needed = [pltpu.make_async_copy(a, b, sems.at[i]) for i, (a, b) in enumerate(pairs)]
-    side = []
+    side, side_out = [], []
     for k in range(comps):
         for p in range(2):
             rows = pl.ds((k * 2 + p) * height, height)
+            side_out.append(pltpu.make_async_copy(head.at[rows], head_out.at[rows], side_sems.at[2, k, p]))
+            side_out.append(pltpu.make_async_copy(tail.at[rows], tail_out.at[rows], side_sems.at[3, k, p]))
             side.append(pltpu.make_async_copy(mesh_ref.at[k, p], head.at[rows], side_sems.at[0, k, p]))
             side.append(
                 pltpu.make_async_copy(mesh_ref.at[k, width - 2 + p], tail.at[rows], side_sems.at[1, k, p])
@@ -116,14 +118,17 @@
                 at, j = start + row // tiles, row % tiles * LANES
                 head[at : at + 1, j : j + LANES] = value
                 tail[at : at + 1, j : j + LANES] = value
-            for copy in side:
-                copy.wait()
+            rest = pl.ds(start, head.shape[0] - start)
             leave = [
-                pltpu.make_async_copy(head, head_out, sems.at[8]),
-                pltpu.make_async_copy(tail, tail_out, sems.at[9]),
+                pltpu.make_async_copy(head.at[rest], head_out.at[rest], sems.at[8]),
+                pltpu.make_async_copy(tail.at[rest], tail_out.at[rest], sems.at[9]),
             ]
             for copy in leave:
                 copy.start()
+            for before, after in zip(side, side_out):
+                before.wait()
+                after.start()
+            leave = leave + side_out
     for copy in needed[3:] + leave:
         copy.wait()
 
@@ -522,7 +527,7 @@
 
 def finish_body(
     base_ref, returned_ref, vertex_ref, left_ref, right_ref, out_ref,
-    wall, left, right, split, high_sc, low_sc, rows_sc, ones_sc, sems, *, per,
+    wall, left, right, split, high_sc, low_sc, sems, *, per,
 ):
     comps, width, _, depth = wall.shape
     tiles = depth // LANES
@@ -561,21 +566,25 @@
         one = jnp.ones((lows, LANES), bf16)
         nothing = jnp.zeros((lows, LANES), bf16)
         empty = jnp.zeros((size, LANES), bf16)
-        for row in range(rows):
-            match = line == spread(low_sc[row : row + 1, :], lows)
-            ones_sc[row, :lows] = jnp.where(match, one, nothing)
-            here = home == spread(high_sc[row : row + 1, :], size)
-            for term in range(2):
-                for k in range(comps):
-                    value = spread(slot_row(split.at[term], k, row, per, group), size)
-                    at = (term * comps + k) * size
-                    rows_sc[row, at : at + size] = jnp.where(here, value, empty)
-        total = lax.dot_general(
-            jnp.concatenate([rows_sc[row, : 2 * comps * size] for row in range(rows)], axis=1),
-            jnp.concatenate([ones_sc[row, :lows] for row in range(rows)], axis=1),
-            (((1,), (1,)), ((), ())),
-            preferred_element_type=f32,
-        )
+        total = None
+        for first in range(0, rows, 4):
+            wide, tall = [], []
+            for row in range(first, min(rows, first + 4)):
+                wide.append(jnp.where(line == spread(low_sc[row : row + 1, :], lows), one, nothing))
+                here = home == spread(high_sc[row : row + 1, :], size)
+                parts = []
+                for term in range(2):
+                    for k in range(comps):
+                        value = spread(slot_row(split.at[term], k, row, per, group), size)
+                        parts.append(jnp.where(here, value, empty))
+                tall.append(jnp.concatenate(parts, axis=0))
+            part = lax.dot_general(
+                jnp.concatenate(tall, axis=1),
+                jnp.concatenate(wide, axis=1),
+                (((1,), (1,)), ((), ())),
+                preferred_element_type=f32,
+            )
+            total = part if total is None else total + part
         total = total[: comps * size] + total[comps * size :]
         return [total[k * size : (k + 1) * size] for k in range(comps)]
 
@@ -689,7 +698,7 @@
             pltpu.VMEM(side, f32),
             pltpu.VMEM(side, f32),
             pltpu.SemaphoreType.DMA((10,)),
-            pltpu.SemaphoreType.DMA((2, comps, 2)),
+            pltpu.SemaphoreType.DMA((4, comps, 2)),
         ],
         compiler_params=params(6),
         name="pick_nodes",
@@ -766,7 +775,6 @@
     )(in_hbm(base), edges, field, in_hbm(kept), halo_left, halo_right)
 
     slot_rows = receive_vertex.shape[0] // LANES
-    size = width * (depth // WIDE)
     return pl.pallas_call(
         lambda *refs: finish_body(*refs, per=result_per),
         out_shape=jax.ShapeDtypeStruct(mesh_before.shape, f32),
@@ -779,8 +787,6 @@
             pltpu.VMEM((2,) + returned.shape, f32),
             pltpu.VMEM((slot_rows, LANES), f32),
             pltpu.VMEM((slot_rows, LANES), f32),
-            pltpu.VMEM((slot_rows, 2 * comps * max(size, TALL), LANES), bf16),
-            pltpu.VMEM((slot_rows, WIDE, LANES), bf16),
             pltpu.SemaphoreType.DMA((2 * comps + 2,)),
         ],
         input_output_aliases={0: 0},

time: 78.4 us -> 76.6 us (0.977)
  Pallas kernels: 37.9 us -> 36.2 us
    pallas_call x1, Pallas kernels: 5.6 us -> 3.76 us  [local(): pl.pallas_call(lambda *refs: finish_body(*refs, per=result_per), out_shap...]
  transfers between devices with their start and end apart: 3 -> 3, of which waited for: 0 -> 0; matrix products, arithmetic and copies ran while one was open for 0% -> 0% of each run, Pallas kernels for 36% -> 37%
where the time goes in v6:
time: 76.6 us; the launch traced here: 76.4 us
  Pallas kernels  36.2 us (47%)
  blocking collectives  31 us (40%)
  starting transfers between devices  8.9 us (12%)
    all_to_all x1, blocking collectives, exchange(): lax.all_to_all(packed, 'dev', split_axis=0, concat_axis=0, tiled=True)  31 us
    pallas_call x1, Pallas kernels, local(): pl.pallas_call(with_sums(mesh_body), out_shape=(jax.ShapeDtypeStruct(mesh...  12.1 us
    pallas_call x1, Pallas kernels, local(): pl.pallas_call(lambda *refs: result_body(*refs, per_in=send_per, per_out=...  10.1 us
    pallas_call x1, Pallas kernels, local(): pl.pallas_call(with_sums(edges_body), out_shape=jax.ShapeDtypeStruct(mesh...  6.33 us
    all_to_all x1, starting transfers between devices, exchange(): lax.all_to_all(packed, 'dev', split_axis=0, concat_axis=0, tiled=True)  5.14 us
    pallas_call x1, Pallas kernels, local(): pl.pallas_call(lambda *refs: pick_body(*refs, per=send_per), out_shape=(p...  3.9 us
    pallas_call x1, Pallas kernels, local(): pl.pallas_call(lambda *refs: finish_body(*refs, per=result_per), out_shap...  3.76 us
    ppermute x1, starting transfers between devices, local(): halo_left = lax.ppermute(tail, 'dev', up)  2.47 us
  transfers between devices with their start and end apart: 3, of which 0 were waited for; matrix products, arithmetic and copies ran while one was open for 0% of the time, Pallas kernels for 37%

profile of v6, /device:TPU:0, one launch (start us, length us, event | category | flops | bytes accessed | tf_op | source)
XLA Modules:
  0.0 76.4 jit_solution(2592870864885567275)
XLA Ops:
  0.0 3.9 %pick_nodes.1 = (f32[32,6,128]{2,1,0:T(8,128)S(1)}, f32[592,512]{1,0:T(8,128)}, f32[592,512]{1,0:T(8,128)}, s32[64,128]{1,0:T(8,128)S(1)}, s32[4,1024]{1,0:T(4,1...) custom-call(f32[3,4096]{1,0:T(4,128)} %refs_0_.1, ...), custom_call_target="tpu_custom_call" | custom-call | tf_op jit(solution)/shard_map/pick_nodes/pallas_call | solution.py:689
  3.9 2.5 %collective-permute-start = (f32[592,512]{1,0:T(8,128)}, f32[592,512]{1,0:T(8,128)S(1)}, u32[]{:S(2)}, u32[]{:S(2)}) collective-permute-start(f32[592,512]{1,0:T(8,128)} %get-tuple-element.24), channel_id=1, source_target_pairs={{0,1},{1,2},{2,3},{3,4},{4,5},{5,6},{6,7},{7,8},{8,9},{9,10},{10,1... | collective-permute-start | bytes 3637256 | tf_op jit(solution)/shard_map/ppermute | solution.py:707
  6.4 1.3 %collective-permute-start.1 = (f32[592,512]{1,0:T(8,128)}, f32[592,512]{1,0:T(8,128)S(1)}, u32[]{:S(2)}, u32[]{:S(2)}) collective-permute-start(f32[592,512]{1,0:T(8,128)} %get-tuple-element.25), channel_id=1, source_target_pairs={{1,0},{2,1},{3,2},{4,3},{5,4},{6,5},{7,6},{8,7},{9,8},{10,9},{11,1... | collective-permute-start | bytes 3637256 | tf_op jit(solution)/shard_map/ppermute | solution.py:708
  7.7 31.0 %all_to_all.10.refs_0_ = f32[32,6,128]{2,1,0:T(8,128)S(1)} all-to-all(f32[32,6,128]{2,1,0:T(8,128)S(1)} %get-tuple-element.16), channel_id=1, replica_groups=mesh['dev'=32] {'dev'}, dimensions={0} | all-to-all | bytes 196608 | tf_op jit(solution)/shard_map/all_to_all | solution.py:635
  38.7 10.1 %cluster_results.1.refs_0_ = f32[32,18,128]{2,1,0:T(8,128)} custom-call(f32[32,6,128]{2,1,0:T(8,128)S(1)} %all_to_all.10.refs_0_, s32[4,1024]{1,0:T(4,128)S(1)} %get-tuple-element.17.refs_1_, f32[3,4,1024]{2,1,0:T(4,128)S(1)} %get-tuple-element.18.refs_2_, f32[3,4,1024]{2,1,0:T(4,128)S(1)} %get-tuple-element.19.refs_3_, bf16[4,1024,1024]{2,1,0:T(8,128)(2,1)} %refs_4_.3, ...), custom_call_target="tpu_custom_call" | custom-call | tf_op jit(solution)/shard_map/cluster_results/pallas_call | solution.py:721
  48.8 5.1 %all-to-all-start.1 = ((f32[32,18,128]{2,1,0:T(8,128)}), f32[32,18,128]{2,1,0:T(8,128)S(1)}, u32[]{:S(2)}, u32[]{:S(2)}) async-start(f32[32,18,128]{2,1,0:T(8,128)} %cluster_results.1.refs_0_), calls=%async_computation.1 | async-start | bytes 786432 | tf_op jit(solution)/shard_map/all_to_all | solution.py:635
  53.9 0.1 pad_add_fusion.refs_1_
  54.0 12.1 %sweeps.1 = (f32[3,16,96,512]{3,2,1,0:T(8,128)}, f32[3,4,4,96,128]{4,3,2,1,0:T(8,128)}) custom-call(f32[32,18,128]{2,1,0:T(8,128)} %cluster_results.1.refs_0_, f32[3,16,96,512]{3,2,1,0:T(8,128)} %refs_2_.3), custom_call_target="tpu_custom_call" | custom-call | tf_op jit(solution)/shard_map/sweeps/pallas_call | solution.py:737
  66.1 0.0 collective-permute-done.refs_4_.refs_3_
  66.1 0.0 collective-permute-done.1.refs_5_.refs_4_
  66.1 6.3 %edges.1.refs_0_ = f32[3,16,96,512]{3,2,1,0:T(8,128)} custom-call(f32[3,16,96,512]{3,2,1,0:T(8,128)} %get-tuple-element.22.refs_0_, s32[2]{0:T(128)S(1)} %pad_add_fusion.refs_1_, f32[3,16,96,512]{3,2,1,0:T(8,128)} %refs_2_.3, f32[3,4,4,96,128]{4,3,2,1,0:T(8,128)} %get-tuple-element.23.refs_3_, ...), custom_call_target="tpu_custom_call", output_to_operand_aliasing={{}: (0, {})} | custom-call | tf_op jit(solution)/shard_map/edges/pallas_call | solution.py:758
  72.4 0.0 all-to-all-done.1.refs_1_
  72.5 3.8 %finish.1 = f32[3,16,96,512]{3,2,1,0:T(8,128)} custom-call(f32[3,16,96,512]{3,2,1,0:T(8,128)} %edges.1.refs_0_, f32[32,18,128]{2,1,0:T(8,128)S(1)} %all-to-all-done.1.refs_1_, s32[64,128]{1,0:T(8,128)S(1)} %get-tuple-element.26.refs_2_, f32[592,512]{1,0:T(8,128)S(1)} %collective-permute-done.refs_4_.refs_3_, ...), custom_call_target="tpu_custom_call", output_to_operand_aliasing={{}: (0, {})} | custom-call | tf_op jit(solution)/shard_map/finish/pallas_call | solution.py:778
Async XLA Ops:
  3.9 62.2 %collective-permute-start = (f32[592,512]{1,0:T(8,128)}, f32[592,512]{1,0:T(8,128)S(1)}, u32[]{:S(2)}, u32[]{:S(2)}) collective-permute-start(f32[592,512]{1,0:T(8,128)} %get-tuple-element.24), channel_id=1, source_target_pairs={{0,1},{1,2},{2,3},{3,4},{4,5},{5,6},{6,7},{7,8},{8,9},{9,10},{10,1... | collective-permute-start | bytes 3637256 | tf_op jit(solution)/shard_map/ppermute | solution.py:707
  6.4 59.7 %collective-permute-start.1 = (f32[592,512]{1,0:T(8,128)}, f32[592,512]{1,0:T(8,128)S(1)}, u32[]{:S(2)}, u32[]{:S(2)}) collective-permute-start(f32[592,512]{1,0:T(8,128)} %get-tuple-element.25), channel_id=1, source_target_pairs={{1,0},{2,1},{3,2},{4,3},{5,4},{6,5},{7,6},{8,7},{9,8},{10,9},{11,1... | collective-permute-start | bytes 3637256 | tf_op jit(solution)/shard_map/ppermute | solution.py:708
  48.8 23.7 %all-to-all-start.1 = ((f32[32,18,128]{2,1,0:T(8,128)}), f32[32,18,128]{2,1,0:T(8,128)S(1)}, u32[]{:S(2)}, u32[]{:S(2)}) async-start(f32[32,18,128]{2,1,0:T(8,128)} %cluster_results.1.refs_0_), calls=%async_computation.1 | async-start | bytes 786432 | tf_op jit(solution)/shard_map/all_to_all | solution.py:635

commit v7 on v6

--- a/solution.py
+++ b/solution.py
@@ -100,7 +100,7 @@
         copy.wait()
     groups = index_ref.shape[0] // SUB
     blocks = table_ref.shape[1] // LANES
-    half = max(1, groups // 2)
+    half = max(1, groups // 4)
     for first in range(0, groups, half):
         got = gather_rows(
             lambda k, b: table_ref[k : k + 1, b * LANES : (b + 1) * LANES],
@@ -265,7 +265,7 @@
     return ends
 
 
-def sweep_planes(jobs, height, depth, sums):
+def sweep_planes(jobs, height, depth, sums, turn):
     tiles, strips = depth // LANES, height // TALL
     wides, part = depth // WIDE, WIDE // LANES
     units = len(sums)
@@ -310,15 +310,11 @@
                 value = jnp.where(row == 0, 0.0, value)
             put(j, y, value)
 
-    group = 3
-    for y in range(0, strips + group, group):
-        base = y // group % 2 * 2 * group
-        if y < strips:
-            multiply([(job[0], y + n, base + n * 2 + i) for n in range(group) for i, job in enumerate(jobs)])
-        if y >= group:
-            for n in range(group):
-                for i, (center, before, after, put) in enumerate(jobs):
-                    complete(center, before, after, y - group + n, 2 * group - base + n * 2 + i, put)
+    spot = turn % 2 * 2 * strips
+    multiply([(job[0], y, spot + y * 2 + i) for y in range(strips) for i, job in enumerate(jobs)])
+    for y in range(strips):
+        for i, (center, before, after, put) in enumerate(jobs):
+            complete(center, before, after, y, spot + y * 2 + i, put)
 
 
 def mesh_body(_, mesh_ref, out_ref, kept_out, field, ring, stage, kept, in_sems, out_sems, kept_sems, sums):
@@ -374,7 +370,7 @@
         jobs = [(field.at[k, x], field.at[k, x - 1], field.at[k, x + 1], put_first)]
         if slot is not None:
             jobs.append((ring[(phase - 2) % turns], ring[(phase - 3) % turns], ring[(phase - 1) % turns], put_second))
-        sweep_planes(jobs, height, depth, sums)
+        sweep_planes(jobs, height, depth, sums, phase)
 
     def component(k, _):
         for b in range(2):
@@ -422,11 +418,11 @@
     comps, width, height, depth = mesh_ref.shape
     tiles = depth // LANES
 
-    def outer(k):
+    def outer(k, beside=True, own_planes=True):
         found = []
         for side, ref in enumerate((left_ref, right_ref)):
             own, other = (2, 0) if side == 0 else (0, 2)
-            for j in range(tiles):
+            for j in range(tiles if own_planes else 0):
                 found.append(
                     pltpu.make_async_copy(
                         mesh_ref.at[k, pl.ds(side * (width - 2), 2), :, columns(j)],
@@ -434,6 +430,15 @@
                         in_sems.at[k, j, side, 0],
                     )
                 )
+            for p in range(2 if own_planes else 0):
+                found.append(
+                    pltpu.make_async_copy(
+                        kept_ref.at[k, side * 2 + p],
+                        fetched.at[k, side, p, :, pl.ds(SUB, height), :],
+                        kept_sems.at[k, side, p],
+                    )
+                )
+            for j in range(tiles if beside else 0):
                 for p in range(2):
                     found.append(
                         pltpu.make_async_copy(
@@ -442,19 +447,12 @@
                             in_sems.at[k, j, side, 1 + p],
                         )
                     )
-            for p in range(2):
-                found.append(
-                    pltpu.make_async_copy(
-                        kept_ref.at[k, side * 2 + p],
-                        fetched.at[k, side, p, :, pl.ds(SUB, height), :],
-                        kept_sems.at[k, side, p],
-                    )
-                )
         return found
 
-    for k in range(comps):
-        for copy in outer(k):
-            copy.start()
+    for beside in (False, True):
+        for k in range(comps):
+            for copy in outer(k, beside, not beside):
+                copy.start()
 
     blank = jnp.zeros((SUB, LANES), f32)
     for j in range(tiles):
@@ -503,7 +501,7 @@
                     computed[side * 2 + p][j, pl.ds(SUB + y * TALL, TALL), :] = value
 
                 jobs.append((field.at[k, side, p + 1], field.at[k, side, p], field.at[k, side, p + 2], put))
-            sweep_planes(jobs, height, depth, sums)
+            sweep_planes(jobs, height, depth, sums, p)
         for p in range(2):
             jobs = []
             for side in range(2):
@@ -514,7 +512,7 @@
                     stage[k, side * 2 + p, y * TALL : (y + 1) * TALL, span] = value
 
                 jobs.append((swept[side][p + 1], swept[side][p], swept[side][p + 2], put))
-            sweep_planes(jobs, height, depth, sums)
+            sweep_planes(jobs, height, depth, sums, p)
         for copy in save(k):
             copy.start()
         return 0
@@ -713,7 +711,7 @@
         raise ValueError("mesh shape")
 
     def with_sums(body):
-        places = 12 * (depth // WIDE // 2)
+        places = 4 * (height // TALL) * (depth // WIDE // 2)
         sums = tuple(tuple(pltpu.ACC(unit)((TALL, WIDE), f32) for _ in range(places)) for unit in range(2))
         return lambda *refs: pl.run_scoped(lambda *sums: body(*refs, sums), *sums)
 

time: 76.6 us -> 75.1 us (0.980)
  Pallas kernels: 36.2 us -> 34.6 us
    pallas_call x1, Pallas kernels: 12.1 us -> 11.2 us  [local(): pl.pallas_call(with_sums(mesh_body), out_shape=(jax.ShapeDtypeStruct(mesh...]
where the time goes in v7:
time: 75.1 us; the launch traced here: 74.8 us
  Pallas kernels  34.6 us (46%)
  blocking collectives  31 us (41%)
  starting transfers between devices  8.9 us (12%)
    all_to_all x1, blocking collectives, exchange(): lax.all_to_all(packed, 'dev', split_axis=0, concat_axis=0, tiled=True)  31 us
    pallas_call x1, Pallas kernels, local(): pl.pallas_call(with_sums(mesh_body), out_shape=(jax.ShapeDtypeStruct(mesh...  11.2 us
    pallas_call x1, Pallas kernels, local(): pl.pallas_call(lambda *refs: result_body(*refs, per_in=send_per, per_out=...  10.1 us
    pallas_call x1, Pallas kernels, local(): pl.pallas_call(with_sums(edges_body), out_shape=jax.ShapeDtypeStruct(mesh...  6.06 us
    all_to_all x1, starting transfers between devices, exchange(): lax.all_to_all(packed, 'dev', split_axis=0, concat_axis=0, tiled=True)  5.14 us
    pallas_call x1, Pallas kernels, local(): pl.pallas_call(lambda *refs: finish_body(*refs, per=result_per), out_shap...  3.76 us
    pallas_call x1, Pallas kernels, local(): pl.pallas_call(lambda *refs: pick_body(*refs, per=send_per), out_shape=(p...  3.49 us
    ppermute x1, starting transfers between devices, local(): halo_left = lax.ppermute(tail, 'dev', up)  2.47 us
  transfers between devices with their start and end apart: 3, of which 0 were waited for; matrix products, arithmetic and copies ran while one was open for 0% of the time, Pallas kernels for 37%

profile of v7, /device:TPU:0, one launch (start us, length us, event | category | flops | bytes accessed | tf_op | source)
XLA Modules:
  0.0 74.8 jit_solution(1947651954567805990)
XLA Ops:
  0.0 3.5 %pick_nodes.1 = (f32[32,6,128]{2,1,0:T(8,128)S(1)}, f32[592,512]{1,0:T(8,128)}, f32[592,512]{1,0:T(8,128)}, s32[64,128]{1,0:T(8,128)S(1)}, s32[4,1024]{1,0:T(4,1...) custom-call(f32[3,4096]{1,0:T(4,128)} %refs_0_.1, ...), custom_call_target="tpu_custom_call" | custom-call | tf_op jit(solution)/shard_map/pick_nodes/pallas_call | solution.py:687
  3.5 2.5 %collective-permute-start = (f32[592,512]{1,0:T(8,128)}, f32[592,512]{1,0:T(8,128)S(1)}, u32[]{:S(2)}, u32[]{:S(2)}) collective-permute-start(f32[592,512]{1,0:T(8,128)} %get-tuple-element.24), channel_id=1, source_target_pairs={{0,1},{1,2},{2,3},{3,4},{4,5},{5,6},{6,7},{7,8},{8,9},{9,10},{10,1... | collective-permute-start | bytes 3637256 | tf_op jit(solution)/shard_map/ppermute | solution.py:705
  6.0 1.3 %collective-permute-start.1 = (f32[592,512]{1,0:T(8,128)}, f32[592,512]{1,0:T(8,128)S(1)}, u32[]{:S(2)}, u32[]{:S(2)}) collective-permute-start(f32[592,512]{1,0:T(8,128)} %get-tuple-element.25), channel_id=1, source_target_pairs={{1,0},{2,1},{3,2},{4,3},{5,4},{6,5},{7,6},{8,7},{9,8},{10,9},{11,1... | collective-permute-start | bytes 3637256 | tf_op jit(solution)/shard_map/ppermute | solution.py:706
  7.3 31.0 %all_to_all.10.refs_0_ = f32[32,6,128]{2,1,0:T(8,128)S(1)} all-to-all(f32[32,6,128]{2,1,0:T(8,128)S(1)} %get-tuple-element.16), channel_id=1, replica_groups=mesh['dev'=32] {'dev'}, dimensions={0} | all-to-all | bytes 196608 | tf_op jit(solution)/shard_map/all_to_all | solution.py:633
  38.3 10.1 %cluster_results.1.refs_0_ = f32[32,18,128]{2,1,0:T(8,128)} custom-call(f32[32,6,128]{2,1,0:T(8,128)S(1)} %all_to_all.10.refs_0_, s32[4,1024]{1,0:T(4,128)S(1)} %get-tuple-element.17.refs_1_, f32[3,4,1024]{2,1,0:T(4,128)S(1)} %get-tuple-element.18.refs_2_, f32[3,4,1024]{2,1,0:T(4,128)S(1)} %get-tuple-element.19.refs_3_, bf16[4,1024,1024]{2,1,0:T(8,128)(2,1)} %refs_4_.3, ...), custom_call_target="tpu_custom_call" | custom-call | tf_op jit(solution)/shard_map/cluster_results/pallas_call | solution.py:719
  48.3 5.1 %all-to-all-start.1 = ((f32[32,18,128]{2,1,0:T(8,128)}), f32[32,18,128]{2,1,0:T(8,128)S(1)}, u32[]{:S(2)}, u32[]{:S(2)}) async-start(f32[32,18,128]{2,1,0:T(8,128)} %cluster_results.1.refs_0_), calls=%async_computation.1 | async-start | bytes 786432 | tf_op jit(solution)/shard_map/all_to_all | solution.py:633
  53.5 0.1 pad_add_fusion.refs_1_
  53.6 11.2 %sweeps.1 = (f32[3,16,96,512]{3,2,1,0:T(8,128)}, f32[3,4,4,96,128]{4,3,2,1,0:T(8,128)}) custom-call(f32[32,18,128]{2,1,0:T(8,128)} %cluster_results.1.refs_0_, f32[3,16,96,512]{3,2,1,0:T(8,128)} %refs_2_.3), custom_call_target="tpu_custom_call" | custom-call | tf_op jit(solution)/shard_map/sweeps/pallas_call | solution.py:735
  64.8 0.0 collective-permute-done.refs_4_.refs_3_
  64.8 0.0 collective-permute-done.1.refs_5_.refs_4_
  64.8 6.1 %edges.1.refs_0_ = f32[3,16,96,512]{3,2,1,0:T(8,128)} custom-call(f32[3,16,96,512]{3,2,1,0:T(8,128)} %get-tuple-element.22.refs_0_, s32[2]{0:T(128)S(1)} %pad_add_fusion.refs_1_, f32[3,16,96,512]{3,2,1,0:T(8,128)} %refs_2_.3, f32[3,4,4,96,128]{4,3,2,1,0:T(8,128)} %get-tuple-element.23.refs_3_, ...), custom_call_target="tpu_custom_call", output_to_operand_aliasing={{}: (0, {})} | custom-call | tf_op jit(solution)/shard_map/edges/pallas_call | solution.py:756
  70.9 0.0 all-to-all-done.1.refs_1_
  70.9 3.8 %finish.1 = f32[3,16,96,512]{3,2,1,0:T(8,128)} custom-call(f32[3,16,96,512]{3,2,1,0:T(8,128)} %edges.1.refs_0_, f32[32,18,128]{2,1,0:T(8,128)S(1)} %all-to-all-done.1.refs_1_, s32[64,128]{1,0:T(8,128)S(1)} %get-tuple-element.26.refs_2_, f32[592,512]{1,0:T(8,128)S(1)} %collective-permute-done.refs_4_.refs_3_, ...), custom_call_target="tpu_custom_call", output_to_operand_aliasing={{}: (0, {})} | custom-call | tf_op jit(solution)/shard_map/finish/pallas_call | solution.py:776
Async XLA Ops:
  3.5 61.3 %collective-permute-start = (f32[592,512]{1,0:T(8,128)}, f32[592,512]{1,0:T(8,128)S(1)}, u32[]{:S(2)}, u32[]{:S(2)}) collective-permute-start(f32[592,512]{1,0:T(8,128)} %get-tuple-element.24), channel_id=1, source_target_pairs={{0,1},{1,2},{2,3},{3,4},{4,5},{5,6},{6,7},{7,8},{8,9},{9,10},{10,1... | collective-permute-start | bytes 3637256 | tf_op jit(solution)/shard_map/ppermute | solution.py:705
  6.0 58.8 %collective-permute-start.1 = (f32[592,512]{1,0:T(8,128)}, f32[592,512]{1,0:T(8,128)S(1)}, u32[]{:S(2)}, u32[]{:S(2)}) collective-permute-start(f32[592,512]{1,0:T(8,128)} %get-tuple-element.25), channel_id=1, source_target_pairs={{1,0},{2,1},{3,2},{4,3},{5,4},{6,5},{7,6},{8,7},{9,8},{10,9},{11,1... | collective-permute-start | bytes 3637256 | tf_op jit(solution)/shard_map/ppermute | solution.py:706
  48.3 22.5 %all-to-all-start.1 = ((f32[32,18,128]{2,1,0:T(8,128)}), f32[32,18,128]{2,1,0:T(8,128)S(1)}, u32[]{:S(2)}, u32[]{:S(2)}) async-start(f32[32,18,128]{2,1,0:T(8,128)} %cluster_results.1.refs_0_), calls=%async_computation.1 | async-start | bytes 786432 | tf_op jit(solution)/shard_map/all_to_all | solution.py:633
